TPU v7x, 32 devices: a whole 2x2x4 slice. The times are simulated.
32 devices in a mesh: dp: 8 (over z, x), seq: 4 (over y, core).
Axes of the slice: x: 2, y: 2, z: 4, core: 2. Of those that a mesh axis runs over, the one named last changes fastest.
Arguments:
- hidden_states: bfloat16 [8, 2, 1024, 1024], P('dp', None, 'seq'), may hold values from -8.5 to 8.5
- lengths: int32 [8, 2], P('dp'), may hold values from 256 to 1024, as said below
- w_query: bfloat16 [1024, 1024], replicated, may hold values from -0.1875 to 0.1875
- w_key: bfloat16 [1024, 1024], replicated, may hold values from -0.1875 to 0.1875
- w_value: bfloat16 [1024, 1024], replicated, may hold values from -0.1875 to 0.1875
- w_out: bfloat16 [1024, 1024], replicated, may hold values from -0.1875 to 0.1875
- running_cov: float32 [1024, 1024], P('seq'), as said below
Outputs:
- whitened: float32 [8, 2, 1024], P('dp')
- cov_new: float32 [1024, 1024], P('seq')
- loss: float32 [], replicated
Inputs may be any that keep to these rules, and one draw needn't show every extreme that they name: `lengths`: at least a quarter of a module is valid; some module has all 1024 tokens valid. `running_cov`: Symmetric, with a diagonal larger than the sum of the magnitudes of its row's other entries.
All inputs are finite; a program needn't handle non-finite values.
Results may differ from a plain program's by a relative error of at most 0.0037.
The roundings to bfloat16 on the way count: a program that leaves them out, or rounds other values in their place, can miss the bound.
Values sent between devices are 32-bit elements; how exact they have to be, the bound alone decides.
No kernel may reach another device: no remote copies, remote signals or barrier semaphores. Data moves between devices by JAX's collectives and lax.ppermute only.
A program may use at most 128 MiB of HBM per device.

v0:
```python
import jax
import jax.numpy as jnp
from jax import lax
from jax.sharding import PartitionSpec as P

HEADS = 16
HEAD_DIM = 64


def passed_along(array, axis, by):
    size = lax.axis_size(axis)
    pairs = [(i, i + by) for i in range(size) if 0 <= i + by < size]
    return lax.ppermute(array, axis, pairs)


def feature(u):
    return jnp.where(u > 0.0, u + 1.0, jnp.exp(jnp.minimum(u, 0.0)))


def whiten_rows(full_cov, sum_embed, second, total, rows_in):
    mean = sum_embed / total
    batch_cov = (second - total * mean[:, None] * mean[None, :]) / (total - 1)
    cov_full = 0.5 * full_cov + 0.5 * batch_cov
    chol = jnp.linalg.cholesky(cov_full)
    result = lax.linalg.triangular_solve(chol, (rows_in - mean).T, left_side=True, lower=True).T
    return (cov_full, result)


def pair_terms(whitened_rows):
    normed = whitened_rows / jnp.sqrt(
        jnp.sum(whitened_rows * whitened_rows, axis=1, keepdims=True) + 1e-06
    )
    normed = normed.reshape(-1, 2, normed.shape[1])
    gap = normed[:, 0] - normed[:, 1]
    return jnp.sum(gap * gap)


def body(hidden_states, lengths, w_query, w_key, w_value, w_out, running_cov):
    pairs, two, span, width = hidden_states.shape
    count = pairs * two
    heads = HEADS
    head_dim = HEAD_DIM
    rows = hidden_states.reshape(count * span, width)

    def project(weight):
        return jnp.dot(rows, weight, preferred_element_type=jnp.float32)

    f_query = feature(project(w_query)).astype(jnp.bfloat16).reshape(count, span, heads, head_dim)
    f_key = feature(project(w_key)).astype(jnp.bfloat16).reshape(count, span, heads, head_dim)
    values = project(w_value).astype(jnp.bfloat16).reshape(count, span, heads, head_dim)
    local_state = jnp.einsum("slhe,slhf->shef", f_key, values, preferred_element_type=jnp.float32)
    local_norm = jnp.sum(f_key.astype(jnp.float32), axis=1)
    empty_state = jnp.zeros_like(local_state)
    empty_norm = jnp.zeros_like(local_norm)

    def relay(step, carried):
        return passed_along((carried[0] + local_state, carried[1] + local_norm), "seq", 1)

    prior_state, prior_norm = lax.fori_loop(
        0, lax.axis_size("seq") - 1, relay, (empty_state, empty_norm)
    )
    scores = jnp.einsum("slhe,smhe->shlm", f_query, f_key, preferred_element_type=jnp.float32)
    causal = jnp.arange(span)[:, None] >= jnp.arange(span)[None, :]
    scores = jnp.where(causal, scores, 0.0)
    weights = scores.astype(jnp.bfloat16)
    numer = jnp.einsum("shlm,smhf->slhf", weights, values, preferred_element_type=jnp.float32)
    numer = numer + jnp.einsum(
        "slhe,shef->slhf",
        f_query,
        prior_state.astype(jnp.bfloat16),
        preferred_element_type=jnp.float32,
    )
    denom = jnp.transpose(jnp.sum(scores, axis=-1), (0, 2, 1))
    denom = denom + jnp.einsum("slhe,she->slh", f_query.astype(jnp.float32), prior_norm)
    attended = (numer / denom[..., None]).astype(jnp.bfloat16).reshape(count * span, width)
    layer_out = rows.astype(jnp.float32) + jnp.dot(
        attended, w_out, preferred_element_type=jnp.float32
    )
    position = lax.axis_index("seq") * span + jnp.arange(span)
    flat_len = lengths.reshape(count)
    valid = (position[None, :] < flat_len[:, None]).astype(jnp.float32)
    pooled = jnp.sum(layer_out.reshape(count, span, width) * valid[:, :, None], axis=1)
    pooled = lax.psum(pooled, "seq")
    embed = pooled / flat_len[:, None].astype(jnp.float32)
    full_cov = lax.all_gather(running_cov, "seq", axis=0, tiled=True)
    total = lax.axis_size("dp") * count
    own_outer = jnp.dot(
        embed.T, embed, precision=lax.Precision.HIGHEST, preferred_element_type=jnp.float32
    )
    sum_embed, second = lax.psum((jnp.sum(embed, axis=0), own_outer), "dp")
    cov_full, whitened = whiten_rows(full_cov, sum_embed, second, total, embed)
    loss = lax.psum(pair_terms(whitened), "dp") / (pairs * lax.axis_size("dp"))
    share = running_cov.shape[0]
    cov_rows = lax.dynamic_slice_in_dim(cov_full, lax.axis_index("seq") * share, share, 0)
    return (whitened.reshape(pairs, two, width), cov_rows, loss)


def solution(mesh):
    placed = (P("dp", None, "seq", None), P("dp", None), P(), P(), P(), P(), P("seq", None))
    return jax.shard_map(
        body,
        mesh=mesh,
        in_specs=placed,
        out_specs=(P("dp", None, None), P("seq", None), P()),
        check_vma=False,
    )
```

profile of v0, /device:TPU:0, one launch (start us, length us, event | category | flops | bytes accessed | tf_op | source)
XLA Modules:
  0.0 632.6 jit_solution(18064278824719180027)
XLA Ops:
  9.6 2.7 select_convert_fusion.2
  14.5 3.0 select_convert_fusion.3
  17.6 2.4 reshape.210
  19.9 3.5 copy.35
  23.5 2.8 convolution_convert_fusion
  26.3 2.4 reshape.209
  28.7 2.8 copy.37
  32.5 40.9 %while.13 = (s32[]{:T(128)}, f32[2,16,64,64]{3,2,1,0:T(8,128)S(1)}, f32[2,16,64]{2,1,0:T(8,128)S(1)}, f32[2,16,64,64]{3,2,1,0:T(8,128)S(1)}, f32[2,16,64]{2,1,0:T(8,128)S(1)}, /*index=5*/s32[]{:T(128)}) while((s32[]{:T(128)}, f32[2,16,64,64]{3,2,1,0:T(8,128)S(1)}, f32[2,16,64]{2,1,0:T(8,128)S(1)}, f32[2,16,64,64]{3,2,1,0:T(8,128)S(1)}, ...), condition=%wide.region_2.3_spmd, body=%wide.region_1.2_spmd.sunk | while | flops 133122 | bytes 3727509 | solution.py:59
  32.6 2.4 collective-permute-start
  35.1 4.5 collective-permute-start.1
  40.5 11.1 %collective-permute-start = (f32[2,16,64,64]{3,2,1,0:T(8,128)S(1)}, f32[2,16,64,64]{3,2,1,0:T(8,128)S(1)}, u32[]{:S(2)}, u32[]{:S(2)}) collective-permute-start(f32[2,16,64,64]{3,2,1,0:T(8,128)S(1)} %add.171), channel_id=1, source_target_pairs={{0,1},{1,2},{2,3},{4,5},{5,6},{6,7},{8,9},{9,10},{10,11},{12,13},{... | collective-permute-start | bytes 1572872 | tf_op jit(solution)/shard_map/while/body/eval_jaxpr/ppermute | solution.py:13
  51.7 4.3 collective-permute-start.1
  57.0 11.1 %collective-permute-start = (f32[2,16,64,64]{3,2,1,0:T(8,128)S(1)}, f32[2,16,64,64]{3,2,1,0:T(8,128)S(1)}, u32[]{:S(2)}, u32[]{:S(2)}) collective-permute-start(f32[2,16,64,64]{3,2,1,0:T(8,128)S(1)} %add.171), channel_id=1, source_target_pairs={{0,1},{1,2},{2,3},{4,5},{5,6},{6,7},{8,9},{9,10},{10,11},{12,13},{... | collective-permute-start | bytes 1572872 | tf_op jit(solution)/shard_map/while/body/eval_jaxpr/ppermute | solution.py:13
  68.1 4.3 collective-permute-start.1
  82.3 15.1 %psum.28 = f32[2,1024]{1,0:T(2,128)S(1)} all-reduce(f32[2,1024]{1,0:T(2,128)S(1)} %multiply_reduce_fusion), channel_id=1, replica_groups=mesh['dp'=8,'seq'=4] {'seq'}, use_global_device_ids=true, to_apply=%region_5.6 | all-reduce | flops 2048 | bytes 16384 | tf_op jit(solution)/shard_map/psum | solution.py:83
  97.5 5.1 fusion.80
  103.2 22.2 %psum.30 = f32[1024]{0:T(1024)S(1)} all-reduce(f32[1024]{0:T(1024)S(1)} %get-tuple-element.64), channel_id=1, replica_groups=mesh['dp'=8,'seq'=4] {'dp'}, use_global_device_ids=true, to_apply=%region_8.9 | all-reduce | flops 1024 | bytes 8192 | tf_op jit(solution)/shard_map/psum | solution.py:90
  125.4 135.8 %all-reduce.3.cloned.1.call-done = f32[1024,1024]{1,0:T(8,128)} async-done(((f32[1024,1024]{1,0:T(8,128)}), f32[1024,1024]{1,0:T(8,128)}) %all-reduce.3.cloned.1.call-update) | async-done | bytes 4194320 | tf_op jit(solution)/shard_map/psum | solution.py:90
  261.2 6.2 multiply_add_fusion
  267.4 5.5 copy.45
  272.9 4.4 fusion.1
  279.3 11.7 %cholesky.223 = f32[128,128]{1,0:T(8,128)S(1)} custom-call(f32[128,128]{1,0:T(8,128)S(1)} %cholesky.580), custom_call_target="Cholesky" | custom-call | tf_op jit(solution)/shard_map/jit(cholesky)/cholesky | solution.py:24
  291.1 2.5 cholesky.255
  293.6 9.8 %custom-call.62 = f32[1,128,128]{1,2,0:T(8,128)S(1)} custom-call(f32[1,128,128]{2,1,0:T(8,128)S(1)} %get-tuple-element.89), custom_call_target="InvertDiagBlocksLowerTriangular" | custom-call | tf_op jit(solution)/shard_map/jit(cholesky)/cholesky | solution.py:24
  303.4 2.3 constant_dynamic-update-slice_fusion.31
  307.3 12.1 %cholesky.244 = f32[128,128]{1,0:T(8,128)S(1)} custom-call(f32[128,128]{1,0:T(8,128)S(1)} %cholesky.584), custom_call_target="Cholesky" | custom-call | tf_op jit(solution)/shard_map/jit(cholesky)/cholesky | solution.py:24
  320.1 9.8 %custom-call.63 = f32[1,128,128]{1,2,0:T(8,128)S(1)} custom-call(f32[1,128,128]{2,1,0:T(8,128)S(1)} %get-tuple-element.86), custom_call_target="InvertDiagBlocksLowerTriangular" | custom-call | tf_op jit(solution)/shard_map/jit(cholesky)/cholesky | solution.py:24
  333.2 11.7 %cholesky.468 = f32[128,128]{1,0:T(8,128)S(1)} custom-call(f32[128,128]{1,0:T(8,128)S(1)} %cholesky.589), custom_call_target="Cholesky" | custom-call | tf_op jit(solution)/shard_map/jit(cholesky)/cholesky | solution.py:24
  346.3 9.8 %custom-call.64 = f32[1,128,128]{1,2,0:T(8,128)S(1)} custom-call(f32[1,128,128]{2,1,0:T(8,128)S(1)} %get-tuple-element.83), custom_call_target="InvertDiagBlocksLowerTriangular" | custom-call | tf_op jit(solution)/shard_map/jit(cholesky)/cholesky | solution.py:24
  357.2 2.3 convolution_subtract_fusion.2
  359.6 11.8 %cholesky.487 = f32[128,128]{1,0:T(8,128)S(1)} custom-call(f32[128,128]{1,0:T(8,128)S(1)} %cholesky.594), custom_call_target="Cholesky" | custom-call | tf_op jit(solution)/shard_map/jit(cholesky)/cholesky | solution.py:24
  372.8 9.8 %custom-call.65 = f32[1,128,128]{1,2,0:T(8,128)S(1)} custom-call(f32[1,128,128]{2,1,0:T(8,128)S(1)} %get-tuple-element.80), custom_call_target="InvertDiagBlocksLowerTriangular" | custom-call | tf_op jit(solution)/shard_map/jit(cholesky)/cholesky | solution.py:24
  383.7 2.4 convolution_subtract_fusion.3
  386.1 11.7 %cholesky.506 = f32[128,128]{1,0:T(8,128)S(1)} custom-call(f32[128,128]{1,0:T(8,128)S(1)} %cholesky.599), custom_call_target="Cholesky" | custom-call | tf_op jit(solution)/shard_map/jit(cholesky)/cholesky | solution.py:24
  399.2 10.0 %custom-call.66 = f32[1,128,128]{1,2,0:T(8,128)S(1)} custom-call(f32[1,128,128]{2,1,0:T(8,128)S(1)} %get-tuple-element.77), custom_call_target="InvertDiagBlocksLowerTriangular" | custom-call | tf_op jit(solution)/shard_map/jit(cholesky)/cholesky | solution.py:24
  412.5 11.7 %cholesky.526 = f32[128,128]{1,0:T(8,128)S(1)} custom-call(f32[128,128]{1,0:T(8,128)S(1)} %cholesky.604), custom_call_target="Cholesky" | custom-call | tf_op jit(solution)/shard_map/jit(cholesky)/cholesky | solution.py:24
  425.5 9.8 %custom-call.67 = f32[1,128,128]{1,2,0:T(8,128)S(1)} custom-call(f32[1,128,128]{2,1,0:T(8,128)S(1)} %get-tuple-element.74), custom_call_target="InvertDiagBlocksLowerTriangular" | custom-call | tf_op jit(solution)/shard_map/jit(cholesky)/cholesky | solution.py:24
  438.3 12.1 %cholesky.546 = f32[128,128]{1,0:T(8,128)S(1)} custom-call(f32[128,128]{1,0:T(8,128)S(1)} %cholesky.609), custom_call_target="Cholesky" | custom-call | tf_op jit(solution)/shard_map/jit(cholesky)/cholesky | solution.py:24
  451.7 9.8 %custom-call.68 = f32[1,128,128]{1,2,0:T(8,128)S(1)} custom-call(f32[1,128,128]{2,1,0:T(8,128)S(1)} %get-tuple-element.71), custom_call_target="InvertDiagBlocksLowerTriangular" | custom-call | tf_op jit(solution)/shard_map/jit(cholesky)/cholesky | solution.py:24
  464.2 11.7 %cholesky.564 = f32[128,128]{1,0:T(8,128)S(1)} custom-call(f32[128,128]{1,0:T(8,128)S(1)} %convolution_subtract_fusion.6), custom_call_target="Cholesky" | custom-call | tf_op jit(solution)/shard_map/jit(cholesky)/cholesky | solution.py:24
  483.0 5.0 select_select_fusion
  488.0 23.2 %while.14 = (s32[]{:T(128)}, f32[1024,1024]{1,0:T(8,128)}, s32[8,2]{0,1:T(2,128)S(1)}, f32[8,128,128]{2,1,0:T(8,128)S(1)}, s32[]{:T(128)}) while((s32[]{:T(128)}, f32[1024,1024]{1,0:T(8,128)}, s32[8,2]{0,1:T(2,128)S(1)}, f32[8,128,128]{2,1,0:T(8,128)S(1)}, s32[]{:T(128)}) %tuple.81), condition=%wide.while_cond, body=%wide.while_body.sunk | while | flops 2 | bytes 131189 | solution.py:25
  491.5 2.3 bitcast_dynamic-update-slice_fusion.2
  494.4 2.3 bitcast_dynamic-update-slice_fusion.2
  497.3 2.3 bitcast_dynamic-update-slice_fusion.2
  511.2 78.6 %custom-call.69 = f32[8,128,128]{1,2,0:T(8,128)S(1)} custom-call(f32[8,128,128]{2,1,0:T(8,128)S(1)} %get-tuple-element.40), custom_call_target="InvertDiagBlocksLowerTriangular" | custom-call | tf_op jit(solution)/shard_map/triangular_solve | solution.py:25
  601.1 2.3 constant_dynamic-slice_fusion.1
  603.4 19.7 %psum.31 = f32[]{:T(128)} all-reduce(f32[]{:T(128)} %fusion.63), channel_id=1, replica_groups=mesh['dp'=8,'seq'=4] {'dp'}, use_global_device_ids=true, to_apply=%region_27.28 | all-reduce | flops 1 | bytes 8 | tf_op jit(solution)/shard_map/psum | solution.py:92
  (141 shorter events, 72.0 us)
Async XLA Ops:
  8.0 1.6 copy-start
  8.0 253.2 %all-reduce.3.cloned.1.call-start = ((), (), s32[]{:S(2)}) async-start(), calls=%async_computation.1 | async-start | bytes 8388608 | tf_op jit(solution)/shard_map/psum | solution.py:90
  12.8 1.7 copy-start.9
  13.1 18.4 %copy-start.3 = (bf16[2,256,16,64]{1,0,3,2:T(2,128)(2,1)}, bf16[2,256,16,64]{1,0,3,2:T(2,128)(2,1)S(1)}, u32[]{:S(2)}) copy-start(bf16[2,256,16,64]{1,0,3,2:T(2,128)(2,1)S(1)} %reshape.179) | copy-start | bytes 3145732
  31.5 1.0 copy-start.6
  32.6 7.7 %collective-permute-start = (f32[2,16,64,64]{3,2,1,0:T(8,128)S(1)}, f32[2,16,64,64]{3,2,1,0:T(8,128)S(1)}, u32[]{:S(2)}, u32[]{:S(2)}) collective-permute-start(f32[2,16,64,64]{3,2,1,0:T(8,128)S(1)} %add.171), channel_id=1, source_target_pairs={{0,1},{1,2},{2,3},{4,5},{5,6},{6,7},{8,9},{9,10},{10,11},{12,13},{... | collective-permute-start | bytes 1572872 | tf_op jit(solution)/shard_map/while/body/eval_jaxpr/ppermute | solution.py:13
  35.1 5.3 collective-permute-start.1
  40.5 16.3 %collective-permute-start = (f32[2,16,64,64]{3,2,1,0:T(8,128)S(1)}, f32[2,16,64,64]{3,2,1,0:T(8,128)S(1)}, u32[]{:S(2)}, u32[]{:S(2)}) collective-permute-start(f32[2,16,64,64]{3,2,1,0:T(8,128)S(1)} %add.171), channel_id=1, source_target_pairs={{0,1},{1,2},{2,3},{4,5},{5,6},{6,7},{8,9},{9,10},{10,11},{12,13},{... | collective-permute-start | bytes 1572872 | tf_op jit(solution)/shard_map/while/body/eval_jaxpr/ppermute | solution.py:13
  51.7 5.2 collective-permute-start.1
  57.0 16.3 %collective-permute-start = (f32[2,16,64,64]{3,2,1,0:T(8,128)S(1)}, f32[2,16,64,64]{3,2,1,0:T(8,128)S(1)}, u32[]{:S(2)}, u32[]{:S(2)}) collective-permute-start(f32[2,16,64,64]{3,2,1,0:T(8,128)S(1)} %add.171), channel_id=1, source_target_pairs={{0,1},{1,2},{2,3},{4,5},{5,6},{6,7},{8,9},{9,10},{10,11},{12,13},{... | collective-permute-start | bytes 1572872 | tf_op jit(solution)/shard_map/while/body/eval_jaxpr/ppermute | solution.py:13
  68.1 5.2 collective-permute-start.1
  73.4 3.4 copy-start.4
  73.4 3.4 copy-start.5
  76.8 1.4 copy-start.7
  79.1 1.4 copy-start.12
  79.1 1.6 copy-start.8
  79.1 1.9 copy-start.10
  102.6 158.6 %all-gather.2.cloned.1.call-start = ((), (), s32[]{:S(2)}) async-start(), calls=%async_computation | async-start | bytes 5242880 | tf_op jit(solution)/shard_map/all_gather | solution.py:85
  277.4 2.0 copy-start.2
  483.0 140.8 %copy-start.1 = (bf16[1024,1024]{1,0:T(8,128)(2,1)S(1)}, bf16[1024,1024]{1,0:T(8,128)(2,1)}, u32[]{:S(2)}) copy-start(bf16[1024,1024]{1,0:T(8,128)(2,1)} %param.12) | copy-start | bytes 6291460
  600.3 23.5 %copy-start.11 = (f32[1024,2]{0,1:T(2,128)}, f32[1024,2]{0,1:T(2,128)S(1)}, u32[]{:S(2)}) copy-start(f32[1024,2]{0,1:T(2,128)S(1)} %convolution_dynamic-update-slice_fusion.6) | copy-start | bytes 24580
Sparse Core Ops, SparseCore 0:
  102.7 158.4 all-reduce.2
Sparse Core Ops, SparseCore 1:
  104.7 36.3 all-gather.1
where the time goes:
time: 641 us; the launch traced here: 633 us
  other arithmetic  270 us (42%)
  waiting for transfers between devices  139 us (22%)
  blocking collectives  57 us (9%)
  matrix products  54.5 us (9%)
  local copies, waits for them, and re-layouts  50.6 us (8%)
  starting transfers between devices  37.9 us (6%)
  between operations  23.1 us (4%)
    another operation x30, other arithmetic, whiten_rows(): chol = jnp.linalg.cholesky(cov_full)  173 us
    psum x1, waiting for transfers between devices, body(): sum_embed, second = lax.psum((jnp.sum(embed, axis=0), own_outer), 'dp')  136 us
    another operation x3, other arithmetic, whiten_rows(): lax.linalg.triangular_solve(chol, (rows_in - mean).T, left_side=True, low...  83.6 us
    ppermute x6, starting transfers between devices, passed_along(): return lax.ppermute(array, axis, pairs)  37.8 us
    another operation x14, matrix products, whiten_rows(): chol = jnp.linalg.cholesky(cov_full)  23.1 us
    another operation x24, local copies, waits for them, and re-layouts  23 us
    psum x1, blocking collectives, body(): sum_embed, second = lax.psum((jnp.sum(embed, axis=0), own_outer), 'dp')  22.2 us
    psum x1, blocking collectives, body(): loss = lax.psum(pair_terms(whitened), 'dp') / (pairs * lax.axis_size('dp'))  19.7 us
  transfers between devices with their start and end apart: 8, of which 4 were waited for; matrix products, arithmetic and copies ran while one was open for 0% of the time, Pallas kernels for 0%

commit v1 on v0

v1 whole, which is shorter than its diff:
```python
import functools

import jax
import jax.numpy as jnp
from jax import lax
from jax.experimental import pallas as pl
from jax.experimental.pallas import tpu as pltpu
from jax.sharding import PartitionSpec as P

HEADS = 16
HEAD_DIM = 64
LANES = 128
COLS = 256
F32 = jnp.float32
BF16 = jnp.bfloat16
HIGHEST = lax.Precision.HIGHEST
VMEM = pltpu.VMEM
SMEM = pltpu.SMEM


def params(mib):
    return pltpu.CompilerParams(vmem_limit_bytes=mib << 20)


def feature(u):
    return jnp.where(u > 0.0, u + 1.0, jnp.exp(jnp.minimum(u, 0.0)))


def split(x, parts):
    out = []
    for _ in range(parts):
        piece = x.astype(BF16)
        out.append(piece)
        x = x - piece.astype(F32)
    return out


def dot(a, b, ca=1, cb=0):
    return lax.dot_general(a, b, (((ca,), (cb,)), ((), ())), preferred_element_type=F32)


def dot_f32(a, b, ca=1, cb=0):
    return lax.dot_general(
        a, b, (((ca,), (cb,)), ((), ())), precision=HIGHEST, preferred_element_type=F32
    )


def iota(shape, dim):
    return lax.broadcasted_iota(jnp.int32, shape, dim)


def encode_kernel(h_ref, wq_ref, wk_ref, wv_ref, fq_ref, num_ref, den_ref, state_ref):
    count, span = h_ref.shape[0], h_ref.shape[1]
    rows = h_ref[...].reshape(count * span, h_ref.shape[2])
    fq = feature(dot(rows, wq_ref[...])).astype(BF16)
    fk = feature(dot(rows, wk_ref[...])).astype(BF16)
    values = dot(rows, wv_ref[...]).astype(BF16)
    fq_ref[...] = fq.reshape(fq_ref.shape)
    causal = iota((span, span), 0) >= iota((span, span), 1)
    ones_below = causal.astype(BF16)
    low = iota((span, LANES), 1) < HEAD_DIM
    same_head = (iota((LANES, LANES), 0) < HEAD_DIM) == (iota((LANES, LANES), 1) < HEAD_DIM)
    summing = jnp.concatenate([same_head.astype(BF16)] * 2, axis=0)
    for module in range(count):
        at = slice(module * span, (module + 1) * span)
        running = dot(ones_below, fk[at])
        for pair in range(COLS // LANES):
            cols = slice(pair * LANES, (pair + 1) * LANES)
            q, k, v = fq[at, cols], fk[at, cols], values[at, cols]
            state = dot(k, v, 0, 0)
            merged = jnp.where(low[:HEAD_DIM], state[:HEAD_DIM], state[HEAD_DIM:])
            state_ref[pair, module] = jnp.concatenate(
                [merged, jnp.broadcast_to(running[span - 1 :, cols], (8, LANES))], axis=0
            )
            hi, lo = split(q.astype(F32) * running[:, cols], 2)
            den_ref[module, :, cols] = dot(jnp.concatenate([hi, lo], axis=1), summing)
            parts = []
            for half in range(2):
                own = low if half == 0 else jnp.logical_not(low)
                scores = dot(jnp.where(own, q, jnp.zeros_like(q)), k, 1, 1)
                weights = jnp.where(causal, scores, 0.0).astype(BF16)
                parts.append(dot(weights, v))
            num_ref[module, :, cols] = jnp.where(low, parts[0], parts[1])


def encode(hidden, w_query, w_key, w_value):
    count, span, width = hidden.shape
    steps = width // COLS
    weight = pl.BlockSpec((width, COLS), lambda j: (0, j))
    block = pl.BlockSpec((count, span, COLS), lambda j: (0, 0, j))
    pairs = COLS // LANES
    shape = (count, span, width)
    state_shape = (width // LANES, count, HEAD_DIM + 8, LANES)
    return pl.pallas_call(
        encode_kernel,
        grid=(steps,),
        in_specs=[pl.BlockSpec(hidden.shape, lambda j: (0, 0, 0)), weight, weight, weight],
        out_specs=[
            block,
            block,
            block,
            pl.BlockSpec((pairs,) + state_shape[1:], lambda j: (j, 0, 0, 0)),
        ],
        out_shape=[
            jax.ShapeDtypeStruct(shape, BF16),
            jax.ShapeDtypeStruct(shape, F32),
            jax.ShapeDtypeStruct(shape, F32),
            jax.ShapeDtypeStruct(state_shape, F32),
        ],
        compiler_params=params(48),
        name="encode",
    )(hidden, w_query, w_key, w_value)


def pool_kernel(len_ref, start_ref, h_ref, fq_ref, num_ref, den_ref, prior_ref, wo_ref, out_ref):
    count, span = fq_ref.shape[0], fq_ref.shape[1]
    step = pl.program_id(0)
    low = iota((HEAD_DIM, LANES), 1) < HEAD_DIM
    same_head = (iota((LANES, LANES), 0) < HEAD_DIM) == (iota((LANES, LANES), 1) < HEAD_DIM)
    summing = jnp.concatenate([same_head.astype(BF16)] * 2, axis=0)
    sums = []
    hsums = []
    for module in range(count):
        valid = iota((span, LANES), 0) + start_ref[0] < len_ref[module]
        heads = []
        plain = []
        for pair in range(COLS // LANES):
            cols = slice(pair * LANES, (pair + 1) * LANES)
            q = fq_ref[module, :, cols]
            prior = prior_ref[pair, module]
            state = prior[:HEAD_DIM].astype(BF16)
            empty = jnp.zeros_like(state)
            state = jnp.concatenate(
                [jnp.where(low, state, empty), jnp.where(low, empty, state)], axis=0
            )
            hi, lo = split(q.astype(F32) * prior[HEAD_DIM : HEAD_DIM + 1], 2)
            numer = num_ref[module, :, cols] + dot(q, state)
            denom = den_ref[module, :, cols] + dot(jnp.concatenate([hi, lo], axis=1), summing)
            attended = (numer / denom).astype(BF16).astype(F32)
            heads.append(jnp.sum(jnp.where(valid, attended, 0.0), axis=0, keepdims=True))
            plain.append(
                jnp.sum(
                    jnp.where(valid, h_ref[module, :, cols].astype(F32), 0.0), axis=0, keepdims=True
                )
            )
        sums.append(jnp.concatenate(heads, axis=1))
        hsums.append(jnp.concatenate(plain, axis=1))
    sums = jnp.concatenate(sums, axis=0)
    pieces = split(sums, 3)
    part = dot(jnp.concatenate(pieces, axis=0), wo_ref[...])
    part = part[:count] + part[count : 2 * count] + part[2 * count :]

    @pl.when(step == 0)
    def _():
        out_ref[...] = part

    @pl.when(step > 0)
    def _():
        out_ref[...] += part

    here = pl.ds(pl.multiple_of(step * COLS, COLS), COLS)
    out_ref[:, here] += jnp.concatenate(hsums, axis=0)

    @pl.when(step == pl.num_programs(0) - 1)
    def _():
        for module in range(count):
            out_ref[module : module + 1, :] /= len_ref[module].astype(F32)


def pooled_rows(flat_len, start, hidden, fq, num, den, prior, w_out):
    count, span, width = hidden.shape
    block = pl.BlockSpec((count, span, COLS), lambda j: (0, 0, j))
    pairs = COLS // LANES
    return pl.pallas_call(
        pool_kernel,
        grid=(width // COLS,),
        in_specs=[
            pl.BlockSpec(memory_space=SMEM),
            pl.BlockSpec(memory_space=SMEM),
            block,
            block,
            block,
            block,
            pl.BlockSpec((pairs,) + prior.shape[1:], lambda j: (j, 0, 0, 0)),
            pl.BlockSpec((COLS, width), lambda j: (j, 0)),
        ],
        out_specs=pl.BlockSpec((count, width), lambda j: (0, 0)),
        out_shape=jax.ShapeDtypeStruct((count, width), F32),
        compiler_params=params(40),
        name="pool",
    )(flat_len, start, hidden, fq, num, den, prior, w_out)


def leaf_factor(mat):
    groups = LANES // 8
    sub, lane = iota((8, LANES), 0), iota((8, LANES), 1)
    rows = [mat[8 * g : 8 * g + 8, :] for g in range(groups)]

    def row_of(x, i):
        return jnp.broadcast_to(x[i : i + 1, :], (8, LANES))

    def col_of(x, c):
        return jnp.broadcast_to(x[:, c : c + 1], (8, LANES))

    for g in range(groups):
        base = 8 * g
        own = (lane >= base) & (lane < base + 8)
        here = [col_of(rows[g], base + c) for c in range(8)]
        now = jnp.where(own, (lane - base == sub).astype(F32), rows[g])
        following = g + 1 < groups
        if following:
            after = [col_of(rows[g + 1], base + c) for c in range(8)]
            then = jnp.where(own, 0.0, rows[g + 1])
        done = []
        for i in range(8):
            r = lax.rsqrt(row_of(here[i], i))
            u = row_of(now, i) * r
            done.append(u)
            m = here[i] * r
            if i < 7:
                now = now - m * u
            if following:
                mh = after[i] * r
                then = then - mh * u
            for c in range(i + 1, 8):
                s = row_of(here[c], i) * r
                here[c] = here[c] - m * s
                if following:
                    after[c] = after[c] - mh * s
        final = done[0]
        for i in range(1, 8):
            final = jnp.where(sub == i, done[i], final)
        rows[g] = final
        if following:
            rows[g + 1] = then
        if g + 2 < groups:
            turned = final.T
            for h in range(g + 2, groups):
                coef = turned[8 * h : 8 * h + 8, :]
                x = jnp.where(own, 0.0, rows[h])
                for i in range(8):
                    x = x - col_of(coef, i) * done[i]
                rows[h] = x
    return jnp.concatenate(rows, axis=0)


def factor_kernel(offsets, mine_ref, *refs):
    *piece_refs, out_ref, sems = refs
    n = out_ref.shape[0]
    panels = n // LANES
    share = piece_refs[0].shape[1]
    copies = []
    slot = 0
    for ref in piece_refs:
        for b in range(ref.shape[0]):
            block = jnp.bitwise_xor(mine_ref[0], offsets[slot])
            to = pl.ds(pl.multiple_of(block * share, share), share)
            copies.append(pltpu.make_async_copy(ref.at[b], out_ref.at[to, :], sems.at[slot]))
            slot += 1
    for copy in copies:
        copy.start()
    for copy in copies:
        copy.wait()
    row, col = iota((LANES, LANES), 0), iota((LANES, LANES), 1)
    out_ref[...] = out_ref[...] * 0.5

    def run(k, carried):
        ks = pl.ds(pl.multiple_of(k * LANES, LANES), LANES)
        inverse = jnp.where(col <= row, leaf_factor(out_ref[ks, ks]), 0.0)
        out_ref[ks, :] = dot_f32(inverse, out_ref[ks, :])
        out_ref[ks, ks] = inverse

        def trail(h, carried):
            hs = pl.ds(pl.multiple_of(h * LANES, LANES), LANES)
            out_ref[hs, ks] = jnp.zeros((LANES, LANES), F32)
            out_ref[hs, :] = out_ref[hs, :] - dot_f32(out_ref[ks, hs], out_ref[ks, :], 0, 0)
            return carried

        return lax.fori_loop(k + 1, panels, trail, carried)

    lax.fori_loop(0, panels, run, 0)


def inverse_factor(mine, pieces, offsets):
    n = pieces[0].shape[2]
    return pl.pallas_call(
        functools.partial(factor_kernel, offsets),
        in_specs=[pl.BlockSpec(memory_space=SMEM)]
        + [pl.BlockSpec(memory_space=pl.ANY)] * len(pieces),
        out_specs=pl.BlockSpec(memory_space=VMEM),
        out_shape=jax.ShapeDtypeStruct((n, n), F32),
        scratch_shapes=[pltpu.SemaphoreType.DMA((len(offsets),))],
        compiler_params=params(40),
        name="factor",
        cost_estimate=pl.CostEstimate(flops=60_000_000_000, transcendentals=0, bytes_accessed=8 << 20),
    )(mine, *pieces)


def whiten_kernel(
    at_ref, embed_ref, inv_ref, cov_ref, white_ref, cov_out_ref, loss_ref, rows_ref, centred_ref
):
    total, n = embed_ref.shape
    chunks = n // LANES
    share = cov_ref.shape[0]
    embed = embed_ref[...]
    centred = embed - jnp.sum(embed, axis=0, keepdims=True) / total
    weight = 0.5 / (total - 1)
    for k in range(chunks):
        upto = (k + 1) * LANES
        rows_ref[:, k, :] = dot_f32(centred[:, :upto], inv_ref[k * LANES : upto, :upto], 1, 1)
    w = [rows_ref[a] for a in range(total)]
    pairs = [(a, b) for a in range(total) for b in range(a, total)]
    products = jnp.concatenate([w[a] * w[b] for a, b in pairs], axis=0)
    before = iota((LANES, 2 * LANES), 0) < iota((LANES, 2 * LANES), 1)
    earlier = before.astype(BF16)
    sums = [dot(piece, earlier) for piece in split(products, 3)]
    sums = sums[0] + sums[1] + sums[2]
    chunk = iota((8, LANES), 0)
    entry = {}
    for i, (a, b) in enumerate(pairs):
        inside = sums[8 * i : 8 * i + 8, :LANES]
        whole = sums[8 * i : 8 * i + 8, LANES:]
        carry = jnp.where(chunk >= 1, pltpu.roll(whole, 1, 0), 0.0)
        for by in (1, 2, 4):
            carry = carry + jnp.where(chunk >= by, pltpu.roll(carry, by, 0), 0.0)
        entry[a, b] = weight * (inside + carry) + (1.0 if a == b else 0.0)
    right = list(w)
    inverse = []
    spread = jnp.ones((8, LANES), F32)
    for p in range(total):
        inv = 1.0 / entry[p, p]
        inverse.append(inv)
        spread = spread + weight * right[p] * right[p] * inv
        for a in range(p + 1, total):
            f = entry[p, a] * inv
            for b in range(a, total):
                entry[a, b] = entry[a, b] - f * entry[p, b]
            right[a] = right[a] - f * right[p]
    scale = lax.rsqrt(spread)
    solved = [None] * total
    for p in reversed(range(total)):
        x = right[p]
        for b in range(p + 1, total):
            x = x - entry[p, b] * solved[b]
        solved[p] = x * inverse[p]
    solved = [x * scale for x in solved]
    gap = jnp.zeros((8, LANES), F32)
    normed = []
    for a in range(total):
        norm = jnp.sum(jnp.sum(solved[a] * solved[a], axis=1, keepdims=True), axis=0, keepdims=True)
        normed.append(solved[a] / jnp.sqrt(norm + 1e-06))
    for pair in range(total // 2):
        diff = normed[2 * pair] - normed[2 * pair + 1]
        gap = gap + diff * diff
    gap = jnp.sum(jnp.sum(gap, axis=1, keepdims=True), axis=0, keepdims=True)
    loss_ref[...] = gap / (total // 2)
    for a in range(total):
        rows_ref[a] = solved[a]
    count = white_ref.shape[0]
    for m in range(count):
        own = rows_ref[at_ref[0] * count + m]
        for k in range(chunks):
            white_ref[m : m + 1, k * LANES : (k + 1) * LANES] = own[k : k + 1, :]
    start = pl.multiple_of(at_ref[1] * share, share)
    centred_ref[...] = centred
    left = centred_ref[:, pl.ds(start, share)]
    cov_out_ref[...] = 0.5 * cov_ref[...] + weight * dot_f32(left, centred, 0, 0)


def whiten(at, embed, inverse, running_cov, count):
    total, n = embed.shape
    vmem = pl.BlockSpec(memory_space=VMEM)
    return pl.pallas_call(
        whiten_kernel,
        in_specs=[pl.BlockSpec(memory_space=SMEM), vmem, vmem, vmem],
        out_specs=[vmem, vmem, vmem],
        out_shape=[
            jax.ShapeDtypeStruct((count, n), F32),
            jax.ShapeDtypeStruct(running_cov.shape, F32),
            jax.ShapeDtypeStruct((1, 1), F32),
        ],
        scratch_shapes=[
            pltpu.VMEM((total, n // LANES, LANES), F32),
            pltpu.VMEM((total, n), F32),
        ],
        compiler_params=params(48),
        name="whiten",
    )(at, embed, inverse, running_cov)


def bits(size):
    return [1 << b for b in range(size.bit_length() - 1)]


def swap(x, axis, by):
    size = lax.axis_size(axis)
    return lax.ppermute(x, axis, [(i, i ^ by) for i in range(size)])


def earlier_sum(x, axis):
    size = lax.axis_size(axis)
    me = lax.axis_index(axis)
    prior = jnp.zeros_like(x)
    whole = x
    for by in bits(size):
        upper = (me & by) != 0
        if by == size // 2:
            got = lax.ppermute(whole, axis, [(i, i + by) for i in range(by)])
            prior = prior + got
        else:
            got = swap(whole, axis, by)
            prior = prior + jnp.where(upper, got, 0.0)
            whole = whole + got
    return prior


def body(hidden_states, lengths, w_query, w_key, w_value, w_out, running_cov):
    pairs, two, span, width = hidden_states.shape
    count = pairs * two
    seq, dp = lax.axis_size("seq"), lax.axis_size("dp")
    me, group = lax.axis_index("seq"), lax.axis_index("dp")
    hidden = hidden_states.reshape(count, span, width)
    flat_len = lengths.reshape(count)

    pieces, offsets = [running_cov[None]], [0]
    for by in reversed(bits(seq)):
        held = jnp.concatenate(pieces, axis=0) if len(pieces) > 1 else pieces[0]
        pieces.append(swap(held, "seq", by))
        offsets = offsets + [o ^ by for o in offsets]
    fq, num, den, states = encode(hidden, w_query, w_key, w_value)
    prior = earlier_sum(states, "seq")
    start = (me * span).astype(jnp.int32).reshape(1)
    partial = pooled_rows(flat_len, start, hidden, fq, num, den, prior, w_out)
    gathered = lax.all_gather(partial, ("dp", "seq"))
    embed = gathered.reshape(dp, seq, count, width).sum(axis=1).reshape(dp * count, width)
    if dp * count <= 16:
        inverse = inverse_factor(me.astype(jnp.int32).reshape(1), pieces, offsets)
        at = jnp.stack([group, me]).astype(jnp.int32)
        white, cov, loss = whiten(at, embed, inverse, running_cov, count)
        loss = loss.reshape(())
    else:
        white, cov, loss = whiten_many(embed, running_cov, count)
    return white.reshape(pairs, two, width), cov, loss


def whiten_many(embed, running_cov, count):
    total = embed.shape[0]
    share = running_cov.shape[0]
    centred = embed - jnp.sum(embed, axis=0) / total
    full = lax.all_gather(running_cov, "seq", axis=0, tiled=True)
    full = 0.5 * full + (0.5 / (total - 1)) * jnp.dot(centred.T, centred, precision=HIGHEST)
    chol = jnp.linalg.cholesky(full)
    rows = lax.linalg.triangular_solve(chol, centred.T, left_side=True, lower=True).T
    normed = rows / jnp.sqrt(jnp.sum(rows * rows, axis=1, keepdims=True) + 1e-06)
    normed = normed.reshape(total // 2, 2, -1)
    gap = normed[:, 0] - normed[:, 1]
    loss = jnp.sum(gap * gap) / (total // 2)
    white = lax.dynamic_slice_in_dim(rows, lax.axis_index("dp") * count, count, 0)
    cov = lax.dynamic_slice_in_dim(full, lax.axis_index("seq") * share, share, 0)
    return white, cov, loss


def solution(mesh):
    placed = (P("dp", None, "seq", None), P("dp", None), P(), P(), P(), P(), P("seq", None))
    return jax.shard_map(
        body,
        mesh=mesh,
        in_specs=placed,
        out_specs=(P("dp", None, None), P("seq", None), P()),
        check_vma=False,
    )
```

time: 641 us -> 184 us (0.29); the launches traced: 633 us -> 184 us
  other arithmetic: 270 us -> 5.17 us
  waiting for transfers between devices: 139 us -> 37.5 us
  Pallas kernels: 0 us -> 81.5 us
  matrix products: 54.5 us -> 0 us
  local copies, waits for them, and re-layouts: 50.6 us -> 7.46 us
  starting transfers between devices: 37.9 us -> 8.03 us
  between operations: 23.1 us -> 0.72 us
  blocking collectives: 57 us -> 43.4 us
    another operation x33 -> x1, other arithmetic: 256 us -> 0.07 us  [body(): at = jnp.stack([group, me]).astype(jnp.int32)]
    psum x1 -> x0, waiting for transfers between devices: 136 us -> none  [body(): sum_embed, second = lax.psum((jnp.sum(embed, axis=0), own_outer), 'dp')]
    pallas_call x0 -> x4, Pallas kernels: none -> 81.5 us  [the longest x1 59.4 us: inverse_factor(): pl.pallas_call(functools.partial(factor_kernel, offsets), in_specs=[pl.Bl...]
    psum x3 -> x0, blocking collectives: 57 us -> none  [the longest x1 22.2 us: body(): sum_embed, second = lax.psum((jnp.sum(embed, axis=0), own_outer), 'dp')]
    all_gather x0 -> x1, blocking collectives: none -> 43.4 us  [body(): gathered = lax.all_gather(partial, ('dp', 'seq'))]
    ppermute x6 -> x4, waiting for transfers between devices: 2.46 us -> 37.5 us  [the longest x3 25 us: swap(): return lax.ppermute(x, axis, [(i, i ^ by) for i in range(size)])]
    another operation x29 -> x0, matrix products: 33.6 us -> none  [the longest x14 23.1 us: whiten_rows(): chol = jnp.linalg.cholesky(cov_full)]
    ppermute x6 -> x4, starting transfers between devices: 37.8 us -> 8.03 us  [the longest x1 4.49 us: earlier_sum(): got = lax.ppermute(whole, axis, [(i, i + by) for i in range(by)])]
  transfers between devices with their start and end apart: 8 -> 4, of which waited for: 4 -> 3; matrix products, arithmetic and copies ran while one was open for 0% -> 1% of each run, Pallas kernels for 0% -> 9%
where the time goes in v1:
time: 184 us
  Pallas kernels  81.5 us (44%)
  blocking collectives  43.4 us (24%)
  waiting for transfers between devices  37.5 us (20%)
  starting transfers between devices  8.03 us (4%)
  local copies, waits for them, and re-layouts  7.46 us (4%)
  other arithmetic  5.17 us (3%)
    pallas_call x1, Pallas kernels, inverse_factor(): pl.pallas_call(functools.partial(factor_kernel, offsets), in_specs=[pl.Bl...  59.4 us
    all_gather x1, blocking collectives, body(): gathered = lax.all_gather(partial, ('dp', 'seq'))  43.4 us
    ppermute x3, waiting for transfers between devices, swap(): return lax.ppermute(x, axis, [(i, i ^ by) for i in range(size)])  25 us
    ppermute x1, waiting for transfers between devices, earlier_sum(): got = lax.ppermute(whole, axis, [(i, i + by) for i in range(by)])  12.5 us
    pallas_call x1, Pallas kernels, encode(): pl.pallas_call(encode_kernel, grid=(steps,), in_specs=[pl.BlockSpec(hidde...  12.5 us
    unnamed x20, local copies, waits for them, and re-layouts  7.41 us
    pallas_call x1, Pallas kernels, whiten(): pl.pallas_call(whiten_kernel, in_specs=[pl.BlockSpec(memory_space=SMEM),...  6.04 us
    ppermute x1, starting transfers between devices, earlier_sum(): got = lax.ppermute(whole, axis, [(i, i + by) for i in range(by)])  4.49 us
  transfers between devices with their start and end apart: 4, of which 3 were waited for; matrix products, arithmetic and copies ran while one was open for 1% of the time, Pallas kernels for 9%

profile of v1, /device:TPU:0, one launch (start us, length us, event | category | flops | bytes accessed | tf_op | source)
XLA Modules:
  0.0 183.8 jit_solution(10875938670283556767)
XLA Ops:
  0.6 0.0 copy-start
  0.6 3.0 %collective-permute-start.2 = (f32[1,256,1024]{2,1,0:T(8,128)}, f32[1,256,1024]{2,1,0:T(8,128)S(1)}, u32[]{:S(2)}, u32[]{:S(2)}) collective-permute-start(f32[1,256,1024]{2,1,0:T(8,128)} %bitcast.13), channel_id=1, source_target_pairs={{0,2},{1,3},{2,0},{3,1},{4,6},{5,7},{6,4},{7,5},{8,10},{9,11},{10,... | collective-permute-start | bytes 3145736 | tf_op jit(solution)/shard_map/ppermute | solution.py:397
  3.7 23.4 %collective-permute-done.2.refs_1_ = f32[1,256,1024]{2,1,0:T(8,128)S(1)} collective-permute-done((f32[1,256,1024]{2,1,0:T(8,128)}, f32[1,256,1024]{2,1,0:T(8,128)S(1)}, u32[]{:S(2)}, u32[]{:S(2)}) %collective-permute-start.2) | collective-permute-done | bytes 1048608 | tf_op jit(solution)/shard_map/ppermute | solution.py:397
  27.0 2.9 %pad_maximum_fusion = f32[2,256,1024]{2,1,0:T(8,128)} fusion(f32[1,256,1024]{2,1,0:T(8,128)S(1)} %collective-permute-done.2.refs_1_, f32[1,256,1024]{2,1,0:T(8,128)} %bitcast.14), kind=kLoop, calls=%fused_computation | loop fusion | flops 524288 | bytes 4194304 | tf_op jit(solution)/shard_map/concatenate | solution.py:427
  30.0 0.0 collective-permute-start.3
  30.0 0.0 copy-done
  30.0 12.5 %encode.1 = (bf16[2,256,1024]{2,1,0:T(8,128)(2,1)S(1)}, f32[2,256,1024]{2,1,0:T(8,128)S(1)}, f32[2,256,1024]{2,1,0:T(8,128)}, f32[8,2,72,128]{3,2,1,0:T(8,128)S(1)}) custom-call(bf16[2,256,1024]{2,1,0:T(8,128)(2,1)S(1)} %bitcast.11, bf16[1024,1024]{1,0:T(8,128)(2,1)} %wq_ref.1, bf16[1024,1024]{1,0:T(8,128)(2,1)} %wk_ref.1, bf16[1024,1024]{1,0:T(8,128)(2,1)} %wv_ref.1), custom_call_target="tpu_custom_call" | custom-call | tf_op jit(solution)/shard_map/encode/pallas_call | solution.py:94
  42.4 0.0 copy-start.3
  42.4 1.3 copy-done.3
  43.8 0.0 copy-start.6
  43.8 0.0 copy-start.8
  43.8 0.5 collective-permute-start
  44.3 1.6 collective-permute-done
  45.9 0.0 copy-start.9
  45.9 1.0 add.6
  46.9 0.1 copy-done.9
  46.9 4.5 %collective-permute-start.1 = (f32[8,2,72,128]{3,2,1,0:T(8,128)}, f32[8,2,72,128]{3,2,1,0:T(8,128)}, u32[]{:S(2)}, u32[]{:S(2)}) collective-permute-start(f32[8,2,72,128]{3,2,1,0:T(8,128)} %add.6), channel_id=1, source_target_pairs={{0,2},{1,3},{4,6},{5,7},{8,10},{9,11},{12,14},{13,15},{16,18},{17,... | collective-permute-start | bytes 1769480 | tf_op jit(solution)/shard_map/ppermute | solution.py:408
  51.4 0.1 pad_add_fusion.at_ref
  51.5 12.5 %collective-permute-done.1 = f32[8,2,72,128]{3,2,1,0:T(8,128)} collective-permute-done((f32[8,2,72,128]{3,2,1,0:T(8,128)}, f32[8,2,72,128]{3,2,1,0:T(8,128)}, u32[]{:S(2)}, u32[]{:S(2)}) %collective-permute-start.1) | collective-permute-done | bytes 589856 | tf_op jit(solution)/shard_map/ppermute | solution.py:408
  64.0 1.1 select_add_fusion.prior_ref
  65.1 0.0 copy-done.6
  65.1 0.0 copy-done.8
  65.2 0.0 copy-start.2
  65.2 1.6 copy-done.2
  66.7 0.0 copy-start.4
  66.7 1.6 copy-done.4
  68.3 0.0 copy-start.5
  68.3 1.6 copy-done.5
  69.9 0.0 copy-start.7
  69.9 1.2 copy-done.7
  71.2 0.0 copy-start.1
  71.2 3.6 %pool.1 = f32[2,1024]{1,0:T(2,128)S(1)} custom-call(s32[2]{0:T(128)S(1)} %bitcast.17, s32[1]{0:T(128)} %bitcast.3.start_ref, bf16[2,256,1024]{2,1,0:T(8,128)(2,1)S(1)} %bitcast.12, bf16[2,256,1024]{2,1,0:T(8,128)(2,1)S(1)} %copy-done.7, f32[2,256,1024]{2,1,0:T(8,128)S(1)} %copy-done.4, f32[2,256,1024]{2,1,0:T(8,128)S(1)} %copy-done.5, ...), custom_call_target="tpu_custom_call" | custom-call | tf_op jit(solution)/shard_map/pool/pallas_call | solution.py:174
  74.8 43.4 %all-gather.1 = f32[32,2,1024]{2,1,0:T(2,128)S(1)} all-gather(f32[1,2,1024]{2,1,0:T(2,128)S(1)} %bitcast.16), channel_id=2, replica_groups=mesh['dp'=8,'seq'=4] {'dp','seq'}, dimensions={0}, use_global_device_ids=true | all-gather | bytes 270336 | tf_op jit(solution)/shard_map/all_gather | solution.py:434
  118.2 0.1 bitcast_reduce_fusion
  118.3 0.0 collective-permute-done.3.refs_2_
  118.3 0.0 copy-done.1
  118.4 59.4 %factor.1.inv_ref = f32[1024,1024]{1,0:T(8,128)S(1)} custom-call(s32[1]{0:T(128)} %bitcast.1.mine_ref, f32[1,256,1024]{2,1,0:T(8,128)S(1)} %bitcast.15, f32[1,256,1024]{2,1,0:T(8,128)S(1)} %collective-permute-done.2.refs_1_, f32[2,256,1024]{2,1,0:T(8,128)} %collective-permute-done.3.refs_2_), custom_call_target="tpu_custom_call" | custom-call | flops 60000002048 | bytes 8388608 | tf_op jit(solution)/shard_map/factor/pallas_call | solution.py:286
  177.8 6.0 %whiten.1 = (f32[2,1024]{1,0:T(2,128)}, f32[256,1024]{1,0:T(8,128)}, f32[1,1]{1,0:T(1,128)}) custom-call(s32[2]{0:T(128)S(1)} %pad_add_fusion.at_ref, f32[16,1024]{1,0:T(8,128)S(1)} %reshape.32.embed_ref, f32[1024,1024]{1,0:T(8,128)S(1)} %factor.1.inv_ref, f32[256,1024]{1,0:T(8,128)S(1)} %copy-done.1), custom_call_target="tpu_custom_call" | custom-call | tf_op jit(solution)/shard_map/whiten/pallas_call | solution.py:373
  (1 shorter events, 0.0 us)
Async XLA Ops:
  0.6 29.3 %copy-start = (bf16[1,2,256,1024]{3,2,1,0:T(8,128)(2,1)S(1)}, bf16[1,2,256,1024]{3,2,1,0:T(8,128)(2,1)}, u32[]{:S(2)}) copy-start(bf16[1,2,256,1024]{3,2,1,0:T(8,128)(2,1)} %param.7) | copy-start | bytes 3145732
  0.6 26.4 %collective-permute-start.2 = (f32[1,256,1024]{2,1,0:T(8,128)}, f32[1,256,1024]{2,1,0:T(8,128)S(1)}, u32[]{:S(2)}, u32[]{:S(2)}) collective-permute-start(f32[1,256,1024]{2,1,0:T(8,128)} %bitcast.13), channel_id=1, source_target_pairs={{0,2},{1,3},{2,0},{3,1},{4,6},{5,7},{6,4},{7,5},{8,10},{9,11},{10,... | collective-permute-start | bytes 3145736 | tf_op jit(solution)/shard_map/ppermute | solution.py:397
  30.0 88.4 %collective-permute-start.3 = (f32[2,256,1024]{2,1,0:T(8,128)}, f32[2,256,1024]{2,1,0:T(8,128)}, u32[]{:S(2)}, u32[]{:S(2)}) collective-permute-start(f32[2,256,1024]{2,1,0:T(8,128)} %pad_maximum_fusion), channel_id=1, source_target_pairs={{0,1},{1,0},{2,3},{3,2},{4,5},{5,4},{6,7},{7,6},{8,9},{9,8},{10,11... | collective-permute-start | bytes 6291464 | tf_op jit(solution)/shard_map/ppermute | solution.py:397
  42.4 1.3 copy-start.3
  43.8 21.4 %copy-start.6 = (bf16[2,256,1024]{2,1,0:T(8,128)(2,1)}, bf16[2,256,1024]{2,1,0:T(8,128)(2,1)S(1)}, u32[]{:S(2)}) copy-start(bf16[2,256,1024]{2,1,0:T(8,128)(2,1)S(1)} %get-tuple-element.10.fq_ref) | copy-start | bytes 3145732
  43.8 21.4 %copy-start.8 = (s32[1,2]{1,0:T(1,128)S(1)}, s32[1,2]{1,0:T(1,128)}, u32[]{:S(2)}) copy-start(s32[1,2]{1,0:T(1,128)} %param.8) | copy-start | bytes 28
  43.8 2.1 %collective-permute-start = (f32[8,2,72,128]{3,2,1,0:T(8,128)S(1)}, f32[8,2,72,128]{3,2,1,0:T(8,128)S(1)}, u32[]{:S(2)}, u32[]{:S(2)}) collective-permute-start(f32[8,2,72,128]{3,2,1,0:T(8,128)S(1)} %get-tuple-element.13), channel_id=1, source_target_pairs={{0,1},{1,0},{2,3},{3,2},{4,5},{5,4},{6,7},{7,6},{8,9},{9,8},{10,11... | collective-permute-start | bytes 1769480 | tf_op jit(solution)/shard_map/ppermute | solution.py:397
  45.9 1.0 copy-start.9
  46.9 17.1 %collective-permute-start.1 = (f32[8,2,72,128]{3,2,1,0:T(8,128)}, f32[8,2,72,128]{3,2,1,0:T(8,128)}, u32[]{:S(2)}, u32[]{:S(2)}) collective-permute-start(f32[8,2,72,128]{3,2,1,0:T(8,128)} %add.6), channel_id=1, source_target_pairs={{0,2},{1,3},{4,6},{5,7},{8,10},{9,11},{12,14},{13,15},{16,18},{17,... | collective-permute-start | bytes 1769480 | tf_op jit(solution)/shard_map/ppermute | solution.py:408
  65.2 1.6 copy-start.2
  66.7 1.6 copy-start.4
  68.3 1.6 copy-start.5
  69.9 1.2 copy-start.7
  71.2 47.2 %copy-start.1 = (f32[256,1024]{1,0:T(8,128)S(1)}, f32[256,1024]{1,0:T(8,128)}, u32[]{:S(2)}) copy-start(f32[256,1024]{1,0:T(8,128)} %cov_ref.1) | copy-start | bytes 3145732

commit v2 on v1

--- a/solution.py
+++ b/solution.py
@@ -191,10 +191,23 @@
     )(flat_len, start, hidden, fq, num, den, prior, w_out)
 
 
+def split_six(x, axis):
+    one, two, three = split(x, 3)
+    left = jnp.concatenate([one, one, two, two, one, three], axis=axis)
+    right = jnp.concatenate([one, two, one, two, three, one], axis=axis)
+    return left, right
+
+
+GROUP = 16
+
+
 def leaf_factor(mat):
-    groups = LANES // 8
+    groups, tiles = LANES // GROUP, GROUP // 8
     sub, lane = iota((8, LANES), 0), iota((8, LANES), 1)
-    rows = [mat[8 * g : 8 * g + 8, :] for g in range(groups)]
+    rows = [
+        [mat[GROUP * g + 8 * v : GROUP * g + 8 * v + 8, :] for v in range(tiles)]
+        for g in range(groups)
+    ]
 
     def row_of(x, i):
         return jnp.broadcast_to(x[i : i + 1, :], (8, LANES))
@@ -203,111 +216,187 @@
         return jnp.broadcast_to(x[:, c : c + 1], (8, LANES))
 
     for g in range(groups):
-        base = 8 * g
-        own = (lane >= base) & (lane < base + 8)
-        here = [col_of(rows[g], base + c) for c in range(8)]
-        now = jnp.where(own, (lane - base == sub).astype(F32), rows[g])
+        base = GROUP * g
+        own = (lane >= base) & (lane < base + GROUP)
+        here = [[col_of(rows[g][v], base + c) for v in range(tiles)] for c in range(GROUP)]
+        now = [
+            jnp.where(own, (lane - base == sub + 8 * v).astype(F32), rows[g][v])
+            for v in range(tiles)
+        ]
         following = g + 1 < groups
         if following:
-            after = [col_of(rows[g + 1], base + c) for c in range(8)]
-            then = jnp.where(own, 0.0, rows[g + 1])
+            after = [[col_of(rows[g + 1][v], base + c) for v in range(tiles)] for c in range(GROUP)]
+            then = [jnp.where(own, 0.0, rows[g + 1][v]) for v in range(tiles)]
         done = []
-        for i in range(8):
-            r = lax.rsqrt(row_of(here[i], i))
-            u = row_of(now, i) * r
+        for i in range(GROUP):
+            tile, at = divmod(i, 8)
+            r = lax.rsqrt(row_of(here[i][tile], at))
+            u = row_of(now[tile], at) * r
             done.append(u)
-            m = here[i] * r
-            if i < 7:
-                now = now - m * u
+            below = [v for v in range(tile, tiles) if not (v == tile and at == 7)]
+            m = {v: here[i][v] * r for v in below}
+            for v in below:
+                now[v] = now[v] - m[v] * u
             if following:
-                mh = after[i] * r
-                then = then - mh * u
-            for c in range(i + 1, 8):
-                s = row_of(here[c], i) * r
-                here[c] = here[c] - m * s
+                mh = [after[i][v] * r for v in range(tiles)]
+                then = [then[v] - mh[v] * u for v in range(tiles)]
+            for c in range(i + 1, GROUP):
+                s = row_of(here[c][tile], at) * r
+                for v in below:
+                    here[c][v] = here[c][v] - m[v] * s
                 if following:
-                    after[c] = after[c] - mh * s
-        final = done[0]
-        for i in range(1, 8):
-            final = jnp.where(sub == i, done[i], final)
+                    after[c] = [after[c][v] - mh[v] * s for v in range(tiles)]
+        final = []
+        for v in range(tiles):
+            x = done[8 * v]
+            for i in range(1, 8):
+                x = jnp.where(sub == i, done[8 * v + i], x)
+            final.append(x)
         rows[g] = final
         if following:
             rows[g + 1] = then
         if g + 2 < groups:
-            turned = final.T
+            left, right = split_six(jnp.concatenate(final, axis=0), 0)
+            product = dot(left, right, 0, 0)
             for h in range(g + 2, groups):
-                coef = turned[8 * h : 8 * h + 8, :]
-                x = jnp.where(own, 0.0, rows[h])
-                for i in range(8):
-                    x = x - col_of(coef, i) * done[i]
-                rows[h] = x
-    return jnp.concatenate(rows, axis=0)
-
-
-def factor_kernel(offsets, mine_ref, *refs):
-    *piece_refs, out_ref, sems = refs
+                rows[h] = [
+                    jnp.where(own, 0.0, rows[h][v])
+                    - product[GROUP * h + 8 * v : GROUP * h + 8 * v + 8, :]
+                    for v in range(tiles)
+                ]
+    return jnp.concatenate([x for pair in rows for x in pair], axis=0)
+
+
+def eliminate(ref, k):
+    n = ref.shape[0]
+    panels = n // LANES
+    low, high = k * LANES, (k + 1) * LANES
+    row, col = iota((LANES, LANES), 0), iota((LANES, LANES), 1)
+    inverse = jnp.where(col <= row, leaf_factor(ref[low:high, low:high]), 0.0)
+    one, two, three = split(inverse, 3)
+    left = jnp.concatenate([one, one, two, two, one, three], axis=1)
+    parts = []
+    if k + 1 < panels:
+        parts.append(ref[low:high, high:])
+    if k > 0:
+        parts.append(ref[low:high, :low])
+    if parts:
+        one, two, three = split(jnp.concatenate(parts, axis=1), 3)
+        scaled = dot(left, jnp.concatenate([one, two, one, two, three, one], axis=0))
+    ref[low:high, low:high] = inverse
+    if k > 0:
+        ref[low:high, :low] = scaled[:, n - high :]
+    if k + 1 == panels:
+        return
+    rest = n - high
+    coefs, beyond = split_six(scaled[:, :rest], 0)
+    near = slice(high, high + LANES)
+    ref[near, near] -= dot(coefs[:, :LANES], beyond[:, :LANES], 0, 0)
+    for h in range(k + 1, panels):
+        at = slice(h * LANES, (h + 1) * LANES)
+        first = h + 1 if h == k + 1 else h
+        if first < panels:
+            mine = slice((h - k - 1) * LANES, (h - k) * LANES)
+            ref[at, first * LANES :] -= dot(
+                coefs[:, mine], beyond[:, first * LANES - high :], 0, 0
+            )
+    one, two, three = split(inverse, 3)
+    own = jnp.concatenate([one, two, one, two, three, one], axis=0)
+    ref[high:, low:high] = -dot(coefs, own, 0, 0)
+    if k > 0:
+        one, two, three = split(scaled[:, rest:], 3)
+        before = jnp.concatenate([one, two, one, two, three, one], axis=0)
+        ref[high:, :low] -= dot(coefs, before, 0, 0)
+
+
+def load_kernel(panels, me_ref, own_ref, core_ref, far_ref, far_core_ref, out_ref, sems):
     n = out_ref.shape[0]
-    panels = n // LANES
-    share = piece_refs[0].shape[1]
+    share, half = own_ref.shape[0], n // 2
+    me = me_ref[0]
+    side = jnp.where(me >= 2, 0, half)
     copies = []
-    slot = 0
-    for ref in piece_refs:
-        for b in range(ref.shape[0]):
-            block = jnp.bitwise_xor(mine_ref[0], offsets[slot])
-            to = pl.ds(pl.multiple_of(block * share, share), share)
-            copies.append(pltpu.make_async_copy(ref.at[b], out_ref.at[to, :], sems.at[slot]))
-            slot += 1
+    for slot, ref in enumerate((own_ref, core_ref, far_ref, far_core_ref)):
+        block = jnp.bitwise_xor(me, slot)
+        to = pl.ds(pl.multiple_of(block * share, share), share)
+        if slot < 2:
+            target = out_ref.at[to, :]
+        else:
+            target = out_ref.at[to, pl.ds(pl.multiple_of(side, half), half)]
+        copies.append(pltpu.make_async_copy(ref, target, sems.at[slot]))
     for copy in copies:
         copy.start()
     for copy in copies:
         copy.wait()
-    row, col = iota((LANES, LANES), 0), iota((LANES, LANES), 1)
-    out_ref[...] = out_ref[...] * 0.5
-
-    def run(k, carried):
-        ks = pl.ds(pl.multiple_of(k * LANES, LANES), LANES)
-        inverse = jnp.where(col <= row, leaf_factor(out_ref[ks, ks]), 0.0)
-        out_ref[ks, :] = dot_f32(inverse, out_ref[ks, :])
-        out_ref[ks, ks] = inverse
-
-        def trail(h, carried):
-            hs = pl.ds(pl.multiple_of(h * LANES, LANES), LANES)
-            out_ref[hs, ks] = jnp.zeros((LANES, LANES), F32)
-            out_ref[hs, :] = out_ref[hs, :] - dot_f32(out_ref[ks, hs], out_ref[ks, :], 0, 0)
-            return carried
-
-        return lax.fori_loop(k + 1, panels, trail, carried)
-
-    lax.fori_loop(0, panels, run, 0)
-
-
-def inverse_factor(mine, pieces, offsets):
-    n = pieces[0].shape[2]
+
+    @pl.when(me >= 2)
+    def _():
+        for a in range(0, half, LANES):
+            for b in range(0, half, LANES):
+                out_ref[a : a + LANES, half + b : half + b + LANES] = out_ref[
+                    half + b : half + b + LANES, a : a + LANES
+                ].T
+
+    for k in panels:
+        eliminate(out_ref, k)
+
+
+def panels_kernel(panels, in_ref, out_ref):
+    out_ref[...] = in_ref[...]
+    for k in panels:
+        eliminate(out_ref, k)
+
+
+def factor_first(panels, me, own, core, far, far_core):
+    n = own.shape[1]
+    anywhere = pl.BlockSpec(memory_space=pl.ANY)
     return pl.pallas_call(
-        functools.partial(factor_kernel, offsets),
-        in_specs=[pl.BlockSpec(memory_space=SMEM)]
-        + [pl.BlockSpec(memory_space=pl.ANY)] * len(pieces),
+        functools.partial(load_kernel, panels),
+        in_specs=[pl.BlockSpec(memory_space=SMEM)] + [anywhere] * 4,
         out_specs=pl.BlockSpec(memory_space=VMEM),
         out_shape=jax.ShapeDtypeStruct((n, n), F32),
-        scratch_shapes=[pltpu.SemaphoreType.DMA((len(offsets),))],
-        compiler_params=params(40),
-        name="factor",
-        cost_estimate=pl.CostEstimate(flops=60_000_000_000, transcendentals=0, bytes_accessed=8 << 20),
-    )(mine, *pieces)
+        scratch_shapes=[pltpu.SemaphoreType.DMA((4,))],
+        compiler_params=params(24),
+        name="factor_first",
+        cost_estimate=pl.CostEstimate(flops=8_000_000_000, transcendentals=0, bytes_accessed=4 << 20),
+    )(me, own, core, far, far_core)
+
+
+def factor_next(panels, matrix):
+    n = matrix.shape[1]
+    return pl.pallas_call(
+        functools.partial(panels_kernel, panels),
+        in_specs=[pl.BlockSpec(memory_space=VMEM)],
+        out_specs=pl.BlockSpec(memory_space=VMEM),
+        out_shape=jax.ShapeDtypeStruct((n, n), F32),
+        input_output_aliases={0: 0},
+        compiler_params=params(24),
+        name="factor_next",
+        cost_estimate=pl.CostEstimate(flops=8_000_000_000, transcendentals=0, bytes_accessed=4 << 20),
+    )(matrix)
 
 
 def whiten_kernel(
-    at_ref, embed_ref, inv_ref, cov_ref, white_ref, cov_out_ref, loss_ref, rows_ref, centred_ref
+    at_ref, *refs
 ):
-    total, n = embed_ref.shape
+    *piece_refs, inv_ref, cov_ref, white_ref, cov_out_ref, loss_ref, rows_ref, centred_ref, held_ref = refs
+    count, n = white_ref.shape
+    total = centred_ref.shape[0]
     chunks = n // LANES
     share = cov_ref.shape[0]
-    embed = embed_ref[...]
+    slot = 0
+    for ref in piece_refs:
+        for b in range(ref.shape[0]):
+            held_ref[slot] = ref[b]
+            slot += 1
+    embed = jnp.concatenate(
+        [held_ref[jnp.bitwise_xor(at_ref[0], d)] for d in range(total // count)], axis=0
+    )
     centred = embed - jnp.sum(embed, axis=0, keepdims=True) / total
     weight = 0.5 / (total - 1)
+    root = 2.0**0.5
     for k in range(chunks):
         upto = (k + 1) * LANES
-        rows_ref[:, k, :] = dot_f32(centred[:, :upto], inv_ref[k * LANES : upto, :upto], 1, 1)
+        rows_ref[:, k, :] = dot_f32(root * centred[:, :upto], inv_ref[k * LANES : upto, :upto], 1, 1)
     w = [rows_ref[a] for a in range(total)]
     pairs = [(a, b) for a in range(total) for b in range(a, total)]
     products = jnp.concatenate([w[a] * w[b] for a, b in pairs], axis=0)
@@ -356,7 +445,6 @@
     loss_ref[...] = gap / (total // 2)
     for a in range(total):
         rows_ref[a] = solved[a]
-    count = white_ref.shape[0]
     for m in range(count):
         own = rows_ref[at_ref[0] * count + m]
         for k in range(chunks):
@@ -367,12 +455,14 @@
     cov_out_ref[...] = 0.5 * cov_ref[...] + weight * dot_f32(left, centred, 0, 0)
 
 
-def whiten(at, embed, inverse, running_cov, count):
-    total, n = embed.shape
+def whiten(at, pieces, inverse, running_cov):
+    groups = sum(piece.shape[0] for piece in pieces)
+    count, n = pieces[0].shape[1:]
+    total = groups * count
     vmem = pl.BlockSpec(memory_space=VMEM)
     return pl.pallas_call(
         whiten_kernel,
-        in_specs=[pl.BlockSpec(memory_space=SMEM), vmem, vmem, vmem],
+        in_specs=[pl.BlockSpec(memory_space=SMEM)] + [vmem] * (len(pieces) + 2),
         out_specs=[vmem, vmem, vmem],
         out_shape=[
             jax.ShapeDtypeStruct((count, n), F32),
@@ -382,10 +472,11 @@
         scratch_shapes=[
             pltpu.VMEM((total, n // LANES, LANES), F32),
             pltpu.VMEM((total, n), F32),
+            pltpu.VMEM((groups, count, n), F32),
         ],
-        compiler_params=params(48),
+        compiler_params=params(40),
         name="whiten",
-    )(at, embed, inverse, running_cov)
+    )(at, *pieces, inverse, running_cov)
 
 
 def bits(size):
@@ -422,25 +513,59 @@
     hidden = hidden_states.reshape(count, span, width)
     flat_len = lengths.reshape(count)
 
-    pieces, offsets = [running_cov[None]], [0]
-    for by in reversed(bits(seq)):
-        held = jnp.concatenate(pieces, axis=0) if len(pieces) > 1 else pieces[0]
-        pieces.append(swap(held, "seq", by))
-        offsets = offsets + [o ^ by for o in offsets]
-    fq, num, den, states = encode(hidden, w_query, w_key, w_value)
-    prior = earlier_sum(states, "seq")
     start = (me * span).astype(jnp.int32).reshape(1)
-    partial = pooled_rows(flat_len, start, hidden, fq, num, den, prior, w_out)
-    gathered = lax.all_gather(partial, ("dp", "seq"))
-    embed = gathered.reshape(dp, seq, count, width).sum(axis=1).reshape(dp * count, width)
-    if dp * count <= 16:
-        inverse = inverse_factor(me.astype(jnp.int32).reshape(1), pieces, offsets)
-        at = jnp.stack([group, me]).astype(jnp.int32)
-        white, cov, loss = whiten(at, embed, inverse, running_cov, count)
-        loss = loss.reshape(())
+    if seq == 4 and dp == 8 and count == 2:
+        white, cov, loss = body_fixed(hidden, flat_len, start, w_query, w_key, w_value, w_out, running_cov)
     else:
+        fq, num, den, states = encode(hidden, w_query, w_key, w_value)
+        prior = earlier_sum(states, "seq")
+        partial = pooled_rows(flat_len, start, hidden, fq, num, den, prior, w_out)
+        gathered = lax.all_gather(partial, ("dp", "seq"))
+        embed = gathered.reshape(dp, seq, count, width).sum(axis=1).reshape(dp * count, width)
         white, cov, loss = whiten_many(embed, running_cov, count)
     return white.reshape(pairs, two, width), cov, loss
+
+
+def body_fixed(hidden, flat_len, start, w_query, w_key, w_value, w_out, running_cov):
+    me, group = lax.axis_index("seq"), lax.axis_index("dp")
+    width = hidden.shape[2]
+    half = width // 2
+    core, far_side = me & 1, me >= 2
+    at = jnp.stack([group, me]).astype(jnp.int32)
+    chip_columns = lax.dynamic_slice_in_dim(running_cov, (me >> 1) * half, half, 1)
+    far_cov = swap(chip_columns, "seq", 2)
+    core_cov = swap(running_cov, "seq", 1)
+    fq, num, den, states = encode(hidden, w_query, w_key, w_value)
+    far_cov, core_cov, states = lax.optimization_barrier((far_cov, core_cov, states))
+    core_states = swap(states, "seq", 1)
+    far_core_cov = swap(far_cov, "seq", 1)
+    quarter = states.shape[0] // 2
+    mine = lax.dynamic_slice_in_dim(states, core * quarter, quarter, 0)
+    mine = mine + lax.dynamic_slice_in_dim(core_states, core * quarter, quarter, 0)
+    far_half = lax.ppermute(mine, "seq", [(0, 2), (1, 3)])
+    matrix = factor_first((0, 1), at[1:], running_cov, core_cov, far_cov, far_core_cov)
+    far_half, matrix = lax.optimization_barrier((far_half, matrix))
+    other_half = swap(far_half, "seq", 1)
+    prior = jnp.where(
+        core == 0,
+        jnp.concatenate([far_half, other_half], axis=0),
+        jnp.concatenate([other_half, far_half], axis=0),
+    )
+    prior = prior + jnp.where(core == 1, core_states, 0.0)
+    partial = pooled_rows(flat_len, start, hidden, fq, num, den, prior, w_out)
+    partial, matrix = lax.optimization_barrier((partial, matrix))
+    got = [swap(partial, "seq", by) for by in (1, 2, 3)]
+    matrix = factor_next((2, 3), matrix)
+    partial, got, matrix = lax.optimization_barrier((partial, got, matrix))
+    embed = ((partial + got[0]) + (got[1] + got[2]))[None]
+    beside = swap(embed, "dp", 1)
+    matrix = factor_next((4, 5), matrix)
+    embed, beside, matrix = lax.optimization_barrier((embed, beside, matrix))
+    embed = jnp.concatenate([embed, beside], axis=0)
+    pieces = [embed] + [swap(embed, "dp", by) for by in (2, 4, 6)]
+    matrix = factor_next((6, 7), matrix)
+    white, cov, loss = whiten(at, pieces, matrix, running_cov)
+    return white, cov, loss.reshape(())
 
 
 def whiten_many(embed, running_cov, count):

time: 184 us -> 86.6 us (0.47)
  blocking collectives: 43.4 us -> 0 us
  waiting for transfers between devices: 37.5 us -> 3.22 us
  Pallas kernels: 81.5 us -> 55.4 us
  starting transfers between devices: 8.03 us -> 14.1 us
  local copies, waits for them, and re-layouts: 7.46 us -> 10.4 us
  other arithmetic: 5.17 us -> 2.23 us
    all_gather x1 -> x0, blocking collectives: 43.4 us -> none  [body(): gathered = lax.all_gather(partial, ('dp', 'seq'))]
    pallas_call x2 -> x5, Pallas kernels: 65.5 us -> 39.1 us  [the longest x3 23 us: factor_next(): pl.pallas_call(functools.partial(panels_kernel, panels), in_specs=[pl.Blo...]
    ppermute x3 -> x12, waiting for transfers between devices: 25 us -> 3.21 us  [swap(): return lax.ppermute(x, axis, [(i, i ^ by) for i in range(size)])]
    ppermute x1, waiting for transfers between devices: 12.5 us -> 0.01 us  [body_fixed(): far_half = lax.ppermute(mine, 'seq', [(0, 2), (1, 3)])]
    ppermute x3 -> x12, starting transfers between devices: 3.54 us -> 11.9 us  [swap(): return lax.ppermute(x, axis, [(i, i ^ by) for i in range(size)])]
    concatenate x1 -> x0, other arithmetic: 2.93 us -> none  [body(): held = jnp.concatenate(pieces, axis=0) if len(pieces) > 1 else pieces[0]]
    ppermute x1, starting transfers between devices: 4.49 us -> 2.16 us  [body_fixed(): far_half = lax.ppermute(mine, 'seq', [(0, 2), (1, 3)])]
    unnamed x20 -> x21, local copies, waits for them, and re-layouts: 7.41 us -> 9.32 us
  transfers between devices with their start and end apart: 4 -> 13, of which waited for: 3 -> 2; matrix products, arithmetic and copies ran while one was open for 1% -> 2% of each run, Pallas kernels for 9% -> 53%
where the time goes in v2:
time: 86.6 us; the launch traced here: 86.2 us
  Pallas kernels  55.4 us (64%)
  starting transfers between devices  14.1 us (16%)
  local copies, waits for them, and re-layouts  10.4 us (12%)
  waiting for transfers between devices  3.22 us (4%)
  other arithmetic  2.23 us (3%)
    pallas_call x3, Pallas kernels, factor_next(): pl.pallas_call(functools.partial(panels_kernel, panels), in_specs=[pl.Blo...  23 us
    pallas_call x1, Pallas kernels, encode(): pl.pallas_call(encode_kernel, grid=(steps,), in_specs=[pl.BlockSpec(hidde...  12.6 us
    ppermute x12, starting transfers between devices, swap(): return lax.ppermute(x, axis, [(i, i ^ by) for i in range(size)])  11.9 us
    pallas_call x1, Pallas kernels, factor_first(): pl.pallas_call(functools.partial(load_kernel, panels), in_specs=[pl.Block...  10 us
    unnamed x21, local copies, waits for them, and re-layouts  9.32 us
    pallas_call x1, Pallas kernels, whiten(): pl.pallas_call(whiten_kernel, in_specs=[pl.BlockSpec(memory_space=SMEM)]...  6.04 us
    pallas_call x1, Pallas kernels, pooled_rows(): pl.pallas_call(pool_kernel, grid=(width // COLS,), in_specs=[pl.BlockSpec...  3.77 us
    ppermute x12, waiting for transfers between devices, swap(): return lax.ppermute(x, axis, [(i, i ^ by) for i in range(size)])  3.21 us
  transfers between devices with their start and end apart: 13, of which 2 were waited for; matrix products, arithmetic and copies ran while one was open for 2% of the time, Pallas kernels for 53%

profile of v2, /device:TPU:0, one launch (start us, length us, event | category | flops | bytes accessed | tf_op | source)
XLA Modules:
  0.0 86.2 jit_solution(14727025938299868638)
XLA Ops:
  0.6 0.5 collective-permute-start.1
  1.1 1.1 %constant_dynamic-slice_fusion = f32[256,512]{1,0:T(8,128)S(1)} fusion(f32[256,1024]{1,0:T(8,128)} %refs_5_.1, s32[]{:T(128)S(6)} %select_n.24), kind=kLoop, calls=%fused_computation.6 | loop fusion | bytes 1048580 | tf_op jit(solution)/shard_map/dynamic_slice | solution.py:535
  2.2 2.6 %collective-permute-start = (f32[256,512]{1,0:T(8,128)S(1)}, f32[256,512]{1,0:T(8,128)}, u32[]{:S(2)}, u32[]{:S(2)}) collective-permute-start(f32[256,512]{1,0:T(8,128)S(1)} %constant_dynamic-slice_fusion), channel_id=1, source_target_pairs={{0,2},{1,3},{2,0},{3,1},{4,6},{5,7},{6,4},{7,5},{8,10},{9,11},{10,... | collective-permute-start | bytes 1572872 | tf_op jit(solution)/shard_map/ppermute | solution.py:488
  4.8 1.2 %copy-done.2 = bf16[1,2,256,1024]{3,2,1,0:T(8,128)(2,1)S(1)} copy-done((bf16[1,2,256,1024]{3,2,1,0:T(8,128)(2,1)S(1)}, bf16[1,2,256,1024]{3,2,1,0:T(8,128)(2,1)}, u32[]{:S(2)}) %copy-start.2) | copy-done | bytes 1048600
  6.1 12.6 %encode.1 = (bf16[2,256,1024]{2,1,0:T(8,128)(2,1)S(1)}, f32[2,256,1024]{2,1,0:T(8,128)S(1)}, f32[2,256,1024]{2,1,0:T(8,128)}, f32[8,2,72,128]{3,2,1,0:T(8,128)S(1)}) custom-call(bf16[2,256,1024]{2,1,0:T(8,128)(2,1)S(1)} %bitcast.9, bf16[1024,1024]{1,0:T(8,128)(2,1)} %wq_ref.1, bf16[1024,1024]{1,0:T(8,128)(2,1)} %wk_ref.1, bf16[1024,1024]{1,0:T(8,128)(2,1)} %wv_ref.1), custom_call_target="tpu_custom_call" | custom-call | tf_op jit(solution)/shard_map/encode/pallas_call | solution.py:94
  18.6 1.4 %copy-done.6 = f32[2,256,1024]{2,1,0:T(8,128)} copy-done((f32[2,256,1024]{2,1,0:T(8,128)}, f32[2,256,1024]{2,1,0:T(8,128)S(1)}, u32[]{:S(2)}) %copy-start.6) | copy-done | bytes 2097176
  20.0 0.0 collective-permute-done.far_ref
  20.0 0.0 collective-permute-done.1.core_ref
  20.0 0.2 collective-permute-start.2
  20.2 0.3 collective-permute-start.4
  20.5 1.6 %collective-permute-done.2 = f32[8,2,72,128]{3,2,1,0:T(8,128)} collective-permute-done((f32[8,2,72,128]{3,2,1,0:T(8,128)S(1)}, f32[8,2,72,128]{3,2,1,0:T(8,128)}, u32[]{:S(2)}, u32[]{:S(2)}) %collective-permute-start.2) | collective-permute-done | bytes 589856 | tf_op jit(solution)/shard_map/ppermute | solution.py:488
  22.1 1.0 %dynamic-slice_add_fusion = f32[4,2,72,128]{3,2,1,0:T(8,128)S(1)} fusion(f32[8,2,72,128]{3,2,1,0:T(8,128)} %collective-permute-done.2, s32[]{:T(128)S(6)} %select_n.25, f32[8,2,72,128]{3,2,1,0:T(8,128)S(1)} %get-tuple-element.29), kind=kLoop, calls=%fused_computation.2 | loop fusion | flops 73728 | bytes 884740 | tf_op jit(solution)/shard_map/add | solution.py:544
  23.1 2.2 %collective-permute-start.3 = (f32[4,2,72,128]{3,2,1,0:T(8,128)S(1)}, f32[4,2,72,128]{3,2,1,0:T(8,128)S(1)}, u32[]{:S(2)}, u32[]{:S(2)}) collective-permute-start(f32[4,2,72,128]{3,2,1,0:T(8,128)S(1)} %dynamic-slice_add_fusion), channel_id=1, source_target_pairs={{0,2},{1,3},{4,6},{5,7},{8,10},{9,11},{12,14},{13,15},{16,18},{17,... | collective-permute-start | bytes 884744 | tf_op jit(solution)/shard_map/ppermute | solution.py:545
  25.3 0.0 collective-permute-done.4.far_core_ref
  25.3 0.0 copy-done.4
  25.3 0.0 copy-start.9
  25.4 10.0 %factor_first.1.in_ref = f32[1024,1024]{1,0:T(8,128)S(1)} custom-call(s32[1]{0:T(128)} %bitcast.1.me_ref, f32[256,1024]{1,0:T(8,128)S(1)} %copy-done.4, f32[256,1024]{1,0:T(8,128)} %collective-permute-done.1.core_ref, f32[256,512]{1,0:T(8,128)} %collective-permute-done.far_ref, f32[256,512]{1,0:T(8,128)} %collective-permute-done.4.far_core_ref), custom_call_target="tpu_custom_call" | custom-call | flops 8000000000 | bytes 4194304 | tf_op jit(solution)/shard_map/factor_first/pallas_call | solution.py:352
  35.4 0.0 copy-start
  35.4 1.9 %copy-done = f32[1024,1024]{1,0:T(8,128)} copy-done((f32[1024,1024]{1,0:T(8,128)}, f32[1024,1024]{1,0:T(8,128)S(1)}, u32[]{:S(2)}) %copy-start) | copy-done | bytes 4194328
  37.3 0.0 collective-permute-done.3
  37.3 0.1 collective-permute-start.5
  37.4 0.1 pad_add_fusion.at_ref
  37.5 1.6 %collective-permute-done.5 = f32[4,2,72,128]{3,2,1,0:T(8,128)} collective-permute-done((f32[4,2,72,128]{3,2,1,0:T(8,128)S(1)}, f32[4,2,72,128]{3,2,1,0:T(8,128)}, u32[]{:S(2)}, u32[]{:S(2)}) %collective-permute-start.5) | collective-permute-done | bytes 294944 | tf_op jit(solution)/shard_map/ppermute | solution.py:488
  39.1 1.1 %fusion.prior_ref = f32[8,2,72,128]{3,2,1,0:T(8,128)S(1)} fusion(f32[4,2,72,128]{3,2,1,0:T(8,128)} %collective-permute-done.5, f32[4,2,72,128]{3,2,1,0:T(8,128)S(1)} %collective-permute-done.3, f32[8,2,72,128]{3,2,1,0:T(8,128)} %collective-permute-done.2, pred[]{:T(512)S(6)} %eq.7, pred[]{:T(512)S(6)} %eq.6), kind=kLoop, calls=%fused_computation.1 | loop fusion | flops 737280 | bytes 1769474 | tf_op jit(solution)/shard_map/add | solution.py:554
  40.2 0.0 copy-done.9
  40.2 0.0 copy-start.5
  40.2 1.6 %copy-done.5 = bf16[1024,1024]{1,0:T(8,128)(2,1)S(1)} copy-done((bf16[1024,1024]{1,0:T(8,128)(2,1)S(1)}, bf16[1024,1024]{1,0:T(8,128)(2,1)}, u32[]{:S(2)}) %copy-start.5) | copy-done | bytes 2097176
  41.8 1.6 %copy-done.7 = f32[2,256,1024]{2,1,0:T(8,128)S(1)} copy-done((f32[2,256,1024]{2,1,0:T(8,128)S(1)}, f32[2,256,1024]{2,1,0:T(8,128)}, u32[]{:S(2)}) %copy-start.7) | copy-done | bytes 2097176
  43.4 1.6 %copy-done.8 = f32[2,256,1024]{2,1,0:T(8,128)S(1)} copy-done((f32[2,256,1024]{2,1,0:T(8,128)S(1)}, f32[2,256,1024]{2,1,0:T(8,128)}, u32[]{:S(2)}) %copy-start.8) | copy-done | bytes 2097176
  45.0 3.8 %pool.1 = f32[2,1024]{1,0:T(2,128)S(1)} custom-call(s32[2]{0:T(128)S(1)} %bitcast.11, s32[1]{0:T(128)} %bitcast.3.start_ref, bf16[2,256,1024]{2,1,0:T(8,128)(2,1)S(1)} %bitcast.10, bf16[2,256,1024]{2,1,0:T(8,128)(2,1)S(1)} %get-tuple-element.25.fq_ref, f32[2,256,1024]{2,1,0:T(8,128)S(1)} %copy-done.7, f32[2,256,1024]{2,1,0:T(8,128)S(1)} %copy-done.8, ...), custom_call_target="tpu_custom_call" | custom-call | tf_op jit(solution)/shard_map/pool/pallas_call | solution.py:174
  48.8 0.4 collective-permute-start.6
  49.2 0.0 collective-permute-start.7
  49.2 1.5 %collective-permute-start.8 = (f32[2,1024]{1,0:T(2,128)S(1)}, f32[2,1024]{1,0:T(2,128)S(1)}, u32[]{:S(2)}, u32[]{:S(2)}) collective-permute-start(f32[2,1024]{1,0:T(2,128)S(1)} %pool.1), channel_id=1, source_target_pairs={{0,3},{1,2},{2,1},{3,0},{4,7},{5,6},{6,5},{7,4},{8,11},{9,10},{10,... | collective-permute-start | bytes 24584 | tf_op jit(solution)/shard_map/ppermute | solution.py:488
  50.7 8.4 %factor_next.3.in_ref = f32[1024,1024]{1,0:T(8,128)S(1)} custom-call(f32[1024,1024]{1,0:T(8,128)S(1)} %copy-done.1), custom_call_target="tpu_custom_call", output_to_operand_aliasing={{}: (0, {})} | custom-call | flops 8000000000 | bytes 4194304 | tf_op jit(solution)/shard_map/factor_next/pallas_call | solution.py:366
  59.1 0.0 collective-permute-done.6
  59.1 0.0 collective-permute-done.7
  59.2 0.0 collective-permute-done.8
  59.2 1.8 %collective-permute-start.9 = (f32[1,2,1024]{2,1,0:T(2,128)S(1)}, f32[1,2,1024]{2,1,0:T(2,128)S(1)}, u32[]{:S(2)}, u32[]{:S(2)}) collective-permute-start(f32[1,2,1024]{2,1,0:T(2,128)S(1)} %add_bitcast_fusion), channel_id=1, source_target_pairs={{0,4},{4,0},{8,12},{12,8},{16,20},{20,16},{24,28},{28,24},{1,5},{5... | collective-permute-start | bytes 24584 | tf_op jit(solution)/shard_map/ppermute | solution.py:488
  61.0 7.7 %factor_next.4.in_ref = f32[1024,1024]{1,0:T(8,128)S(1)} custom-call(f32[1024,1024]{1,0:T(8,128)S(1)} %factor_next.3.in_ref), custom_call_target="tpu_custom_call", output_to_operand_aliasing={{}: (0, {})} | custom-call | flops 8000000000 | bytes 4194304 | tf_op jit(solution)/shard_map/factor_next/pallas_call | solution.py:366
  68.7 0.0 collective-permute-done.9
  68.8 1.6 %collective-permute-start.10 = (f32[2,2,1024]{2,1,0:T(2,128)S(1)}, f32[2,2,1024]{2,1,0:T(2,128)S(1)}, u32[]{:S(2)}, u32[]{:S(2)}) collective-permute-start(f32[2,2,1024]{2,1,0:T(2,128)S(1)} %constant_dynamic-update-slice_fusion.refs_0_), channel_id=1, source_target_pairs={{0,8},{4,12},{8,0},{12,4},{16,24},{20,28},{24,16},{28,20},{1,9},{5... | collective-permute-start | bytes 49160 | tf_op jit(solution)/shard_map/ppermute | solution.py:488
  70.4 2.6 %collective-permute-start.11 = (f32[2,2,1024]{2,1,0:T(2,128)S(1)}, f32[2,2,1024]{2,1,0:T(2,128)S(1)}, u32[]{:S(2)}, u32[]{:S(2)}) collective-permute-start(f32[2,2,1024]{2,1,0:T(2,128)S(1)} %constant_dynamic-update-slice_fusion.refs_0_), channel_id=1, source_target_pairs={{0,16},{4,20},{8,24},{12,28},{16,0},{20,4},{24,8},{28,12},{1,17},{... | collective-permute-start | bytes 49160 | tf_op jit(solution)/shard_map/ppermute | solution.py:488
  73.0 0.2 collective-permute-start.12
  73.2 6.9 %factor_next.5.refs_4_ = f32[1024,1024]{1,0:T(8,128)S(1)} custom-call(f32[1024,1024]{1,0:T(8,128)S(1)} %factor_next.4.in_ref), custom_call_target="tpu_custom_call", output_to_operand_aliasing={{}: (0, {})} | custom-call | flops 8000000000 | bytes 4194304 | tf_op jit(solution)/shard_map/factor_next/pallas_call | solution.py:366
  80.1 0.0 collective-permute-done.10.refs_1_
  80.1 0.0 collective-permute-done.11.refs_2_
  80.1 0.0 collective-permute-done.12.refs_3_
  80.1 6.0 %whiten.1 = (f32[2,1024]{1,0:T(2,128)}, f32[256,1024]{1,0:T(8,128)}, f32[1,1]{1,0:T(1,128)}) custom-call(s32[2]{0:T(128)S(1)} %pad_add_fusion.at_ref, f32[2,2,1024]{2,1,0:T(2,128)S(1)} %constant_dynamic-update-slice_fusion.refs_0_, f32[2,2,1024]{2,1,0:T(2,128)S(1)} %collective-permute-done.10.refs_1_, f32[2,2,1024]{2,1,0:T(2,128)S(1)} %collective-permute-done.11.refs_2_, ...), custom_call_target="tpu_custom_call" | custom-call | tf_op jit(solution)/shard_map/whiten/pallas_call | solution.py:463
  (12 shorter events, 0.0 us)
Async XLA Ops:
  0.6 19.4 %collective-permute-start.1 = (f32[256,1024]{1,0:T(8,128)}, f32[256,1024]{1,0:T(8,128)}, u32[]{:S(2)}, u32[]{:S(2)}) collective-permute-start(f32[256,1024]{1,0:T(8,128)} %refs_5_.1), channel_id=1, source_target_pairs={{0,1},{1,0},{2,3},{3,2},{4,5},{5,4},{6,7},{7,6},{8,9},{9,8},{10,11... | collective-permute-start | bytes 3145736 | tf_op jit(solution)/shard_map/ppermute | solution.py:488
  2.2 17.8 %collective-permute-start = (f32[256,512]{1,0:T(8,128)S(1)}, f32[256,512]{1,0:T(8,128)}, u32[]{:S(2)}, u32[]{:S(2)}) collective-permute-start(f32[256,512]{1,0:T(8,128)S(1)} %constant_dynamic-slice_fusion), channel_id=1, source_target_pairs={{0,2},{1,3},{2,0},{3,1},{4,6},{5,7},{6,4},{7,5},{8,10},{9,11},{10,... | collective-permute-start | bytes 1572872 | tf_op jit(solution)/shard_map/ppermute | solution.py:488
  4.8 1.2 %copy-start.2 = (bf16[1,2,256,1024]{3,2,1,0:T(8,128)(2,1)S(1)}, bf16[1,2,256,1024]{3,2,1,0:T(8,128)(2,1)}, u32[]{:S(2)}) copy-start(bf16[1,2,256,1024]{3,2,1,0:T(8,128)(2,1)} %param.7) | copy-start | bytes 3145732
  6.1 19.3 %copy-start.4 = (f32[256,1024]{1,0:T(8,128)S(1)}, f32[256,1024]{1,0:T(8,128)}, u32[]{:S(2)}) copy-start(f32[256,1024]{1,0:T(8,128)} %refs_5_.1) | copy-start | bytes 3145732
  18.6 1.4 %copy-start.6 = (f32[2,256,1024]{2,1,0:T(8,128)}, f32[2,256,1024]{2,1,0:T(8,128)S(1)}, u32[]{:S(2)}) copy-start(f32[2,256,1024]{2,1,0:T(8,128)S(1)} %get-tuple-element.26.num_ref) | copy-start | bytes 6291460
  20.0 2.1 %collective-permute-start.2 = (f32[8,2,72,128]{3,2,1,0:T(8,128)S(1)}, f32[8,2,72,128]{3,2,1,0:T(8,128)}, u32[]{:S(2)}, u32[]{:S(2)}) collective-permute-start(f32[8,2,72,128]{3,2,1,0:T(8,128)S(1)} %get-tuple-element.29), channel_id=1, source_target_pairs={{0,1},{1,0},{2,3},{3,2},{4,5},{5,4},{6,7},{7,6},{8,9},{9,8},{10,11... | collective-permute-start | bytes 1769480 | tf_op jit(solution)/shard_map/ppermute | solution.py:488
  20.2 5.1 %collective-permute-start.4 = (f32[256,512]{1,0:T(8,128)}, f32[256,512]{1,0:T(8,128)}, u32[]{:S(2)}, u32[]{:S(2)}) collective-permute-start(f32[256,512]{1,0:T(8,128)} %collective-permute-done.far_ref), channel_id=1, source_target_pairs={{0,1},{1,0},{2,3},{3,2},{4,5},{5,4},{6,7},{7,6},{8,9},{9,8},{10,11... | collective-permute-start | bytes 1572872 | tf_op jit(solution)/shard_map/ppermute | solution.py:488
  23.1 14.2 %collective-permute-start.3 = (f32[4,2,72,128]{3,2,1,0:T(8,128)S(1)}, f32[4,2,72,128]{3,2,1,0:T(8,128)S(1)}, u32[]{:S(2)}, u32[]{:S(2)}) collective-permute-start(f32[4,2,72,128]{3,2,1,0:T(8,128)S(1)} %dynamic-slice_add_fusion), channel_id=1, source_target_pairs={{0,2},{1,3},{4,6},{5,7},{8,10},{9,11},{12,14},{13,15},{16,18},{17,... | collective-permute-start | bytes 884744 | tf_op jit(solution)/shard_map/ppermute | solution.py:545
  25.3 14.9 %copy-start.9 = (s32[1,2]{1,0:T(1,128)S(1)}, s32[1,2]{1,0:T(1,128)}, u32[]{:S(2)}) copy-start(s32[1,2]{1,0:T(1,128)} %param.8) | copy-start | bytes 28
  35.4 1.9 %copy-start = (f32[1024,1024]{1,0:T(8,128)}, f32[1024,1024]{1,0:T(8,128)S(1)}, u32[]{:S(2)}) copy-start(f32[1024,1024]{1,0:T(8,128)S(1)} %factor_first.1.in_ref) | copy-start | bytes 12582916
  37.3 2.9 %copy-start.3 = (bf16[1,2,256,1024]{3,2,1,0:T(8,128)(2,1)S(1)}, bf16[1,2,256,1024]{3,2,1,0:T(8,128)(2,1)}, u32[]{:S(2)}) copy-start(bf16[1,2,256,1024]{3,2,1,0:T(8,128)(2,1)} %param.7) | copy-start | bytes 3145732
  37.3 1.7 %collective-permute-start.5 = (f32[4,2,72,128]{3,2,1,0:T(8,128)S(1)}, f32[4,2,72,128]{3,2,1,0:T(8,128)}, u32[]{:S(2)}, u32[]{:S(2)}) collective-permute-start(f32[4,2,72,128]{3,2,1,0:T(8,128)S(1)} %collective-permute-done.3), channel_id=1, source_target_pairs={{0,1},{1,0},{2,3},{3,2},{4,5},{5,4},{6,7},{7,6},{8,9},{9,8},{10,11... | collective-permute-start | bytes 884744 | tf_op jit(solution)/shard_map/ppermute | solution.py:488
  40.2 1.6 %copy-start.5 = (bf16[1024,1024]{1,0:T(8,128)(2,1)S(1)}, bf16[1024,1024]{1,0:T(8,128)(2,1)}, u32[]{:S(2)}) copy-start(bf16[1024,1024]{1,0:T(8,128)(2,1)} %wo_ref.1) | copy-start | bytes 6291460
  41.8 1.6 %copy-start.7 = (f32[2,256,1024]{2,1,0:T(8,128)S(1)}, f32[2,256,1024]{2,1,0:T(8,128)}, u32[]{:S(2)}) copy-start(f32[2,256,1024]{2,1,0:T(8,128)} %copy-done.6) | copy-start | bytes 6291460
  43.4 1.6 %copy-start.8 = (f32[2,256,1024]{2,1,0:T(8,128)S(1)}, f32[2,256,1024]{2,1,0:T(8,128)}, u32[]{:S(2)}) copy-start(f32[2,256,1024]{2,1,0:T(8,128)} %get-tuple-element.27.den_ref) | copy-start | bytes 6291460
  45.0 5.7 %copy-start.1 = (f32[1024,1024]{1,0:T(8,128)S(1)}, f32[1024,1024]{1,0:T(8,128)}, u32[]{:S(2)}) copy-start(f32[1024,1024]{1,0:T(8,128)} %copy-done) | copy-start | bytes 12582916
  48.8 10.4 %collective-permute-start.6 = (f32[2,1024]{1,0:T(2,128)S(1)}, f32[2,1024]{1,0:T(2,128)S(1)}, u32[]{:S(2)}, u32[]{:S(2)}) collective-permute-start(f32[2,1024]{1,0:T(2,128)S(1)} %pool.1), channel_id=1, source_target_pairs={{0,1},{1,0},{2,3},{3,2},{4,5},{5,4},{6,7},{7,6},{8,9},{9,8},{10,11... | collective-permute-start | bytes 24584 | tf_op jit(solution)/shard_map/ppermute | solution.py:488
  49.2 10.0 %collective-permute-start.7 = (f32[2,1024]{1,0:T(2,128)S(1)}, f32[2,1024]{1,0:T(2,128)S(1)}, u32[]{:S(2)}, u32[]{:S(2)}) collective-permute-start(f32[2,1024]{1,0:T(2,128)S(1)} %pool.1), channel_id=1, source_target_pairs={{0,2},{1,3},{2,0},{3,1},{4,6},{5,7},{6,4},{7,5},{8,10},{9,11},{10,... | collective-permute-start | bytes 24584 | tf_op jit(solution)/shard_map/ppermute | solution.py:488
  49.2 10.0 %collective-permute-start.8 = (f32[2,1024]{1,0:T(2,128)S(1)}, f32[2,1024]{1,0:T(2,128)S(1)}, u32[]{:S(2)}, u32[]{:S(2)}) collective-permute-start(f32[2,1024]{1,0:T(2,128)S(1)} %pool.1), channel_id=1, source_target_pairs={{0,3},{1,2},{2,1},{3,0},{4,7},{5,6},{6,5},{7,4},{8,11},{9,10},{10,... | collective-permute-start | bytes 24584 | tf_op jit(solution)/shard_map/ppermute | solution.py:488
  59.2 9.5 %collective-permute-start.9 = (f32[1,2,1024]{2,1,0:T(2,128)S(1)}, f32[1,2,1024]{2,1,0:T(2,128)S(1)}, u32[]{:S(2)}, u32[]{:S(2)}) collective-permute-start(f32[1,2,1024]{2,1,0:T(2,128)S(1)} %add_bitcast_fusion), channel_id=1, source_target_pairs={{0,4},{4,0},{8,12},{12,8},{16,20},{20,16},{24,28},{28,24},{1,5},{5... | collective-permute-start | bytes 24584 | tf_op jit(solution)/shard_map/ppermute | solution.py:488
  68.8 11.3 %collective-permute-start.10 = (f32[2,2,1024]{2,1,0:T(2,128)S(1)}, f32[2,2,1024]{2,1,0:T(2,128)S(1)}, u32[]{:S(2)}, u32[]{:S(2)}) collective-permute-start(f32[2,2,1024]{2,1,0:T(2,128)S(1)} %constant_dynamic-update-slice_fusion.refs_0_), channel_id=1, source_target_pairs={{0,8},{4,12},{8,0},{12,4},{16,24},{20,28},{24,16},{28,20},{1,9},{5... | collective-permute-start | bytes 49160 | tf_op jit(solution)/shard_map/ppermute | solution.py:488
  70.4 9.7 %collective-permute-start.11 = (f32[2,2,1024]{2,1,0:T(2,128)S(1)}, f32[2,2,1024]{2,1,0:T(2,128)S(1)}, u32[]{:S(2)}, u32[]{:S(2)}) collective-permute-start(f32[2,2,1024]{2,1,0:T(2,128)S(1)} %constant_dynamic-update-slice_fusion.refs_0_), channel_id=1, source_target_pairs={{0,16},{4,20},{8,24},{12,28},{16,0},{20,4},{24,8},{28,12},{1,17},{... | collective-permute-start | bytes 49160 | tf_op jit(solution)/shard_map/ppermute | solution.py:488
  73.0 7.1 %collective-permute-start.12 = (f32[2,2,1024]{2,1,0:T(2,128)S(1)}, f32[2,2,1024]{2,1,0:T(2,128)S(1)}, u32[]{:S(2)}, u32[]{:S(2)}) collective-permute-start(f32[2,2,1024]{2,1,0:T(2,128)S(1)} %constant_dynamic-update-slice_fusion.refs_0_), channel_id=1, source_target_pairs={{0,24},{4,28},{8,16},{12,20},{16,8},{20,12},{24,0},{28,4},{1,25},{... | collective-permute-start | bytes 49160 | tf_op jit(solution)/shard_map/ppermute | solution.py:488

commit v3 on v2

--- a/solution.py
+++ b/solution.py
@@ -16,6 +16,10 @@
 HIGHEST = lax.Precision.HIGHEST
 VMEM = pltpu.VMEM
 SMEM = pltpu.SMEM
+
+
+def hbm(x):
+    return pltpu.with_memory_space_constraint(x, pltpu.HBM)
 
 
 def params(mib):
@@ -102,14 +106,14 @@
             pl.BlockSpec((pairs,) + state_shape[1:], lambda j: (j, 0, 0, 0)),
         ],
         out_shape=[
-            jax.ShapeDtypeStruct(shape, BF16),
-            jax.ShapeDtypeStruct(shape, F32),
-            jax.ShapeDtypeStruct(shape, F32),
-            jax.ShapeDtypeStruct(state_shape, F32),
+            pltpu.HBM(shape, BF16),
+            pltpu.HBM(shape, F32),
+            pltpu.HBM(shape, F32),
+            pltpu.HBM(state_shape, F32),
         ],
-        compiler_params=params(48),
+        compiler_params=params(14),
         name="encode",
-    )(hidden, w_query, w_key, w_value)
+    )(hbm(hidden), hbm(w_query), hbm(w_key), hbm(w_value))
 
 
 def pool_kernel(len_ref, start_ref, h_ref, fq_ref, num_ref, den_ref, prior_ref, wo_ref, out_ref):
@@ -186,9 +190,9 @@
         ],
         out_specs=pl.BlockSpec((count, width), lambda j: (0, 0)),
         out_shape=jax.ShapeDtypeStruct((count, width), F32),
-        compiler_params=params(40),
+        compiler_params=params(10),
         name="pool",
-    )(flat_len, start, hidden, fq, num, den, prior, w_out)
+    )(flat_len, start, hbm(hidden), hbm(fq), hbm(num), hbm(den), prior, hbm(w_out))
 
 
 def split_six(x, axis):
@@ -355,7 +359,7 @@
         out_specs=pl.BlockSpec(memory_space=VMEM),
         out_shape=jax.ShapeDtypeStruct((n, n), F32),
         scratch_shapes=[pltpu.SemaphoreType.DMA((4,))],
-        compiler_params=params(24),
+        compiler_params=params(14),
         name="factor_first",
         cost_estimate=pl.CostEstimate(flops=8_000_000_000, transcendentals=0, bytes_accessed=4 << 20),
     )(me, own, core, far, far_core)
@@ -369,7 +373,7 @@
         out_specs=pl.BlockSpec(memory_space=VMEM),
         out_shape=jax.ShapeDtypeStruct((n, n), F32),
         input_output_aliases={0: 0},
-        compiler_params=params(24),
+        compiler_params=params(14),
         name="factor_next",
         cost_estimate=pl.CostEstimate(flops=8_000_000_000, transcendentals=0, bytes_accessed=4 << 20),
     )(matrix)
@@ -474,7 +478,7 @@
             pltpu.VMEM((total, n), F32),
             pltpu.VMEM((groups, count, n), F32),
         ],
-        compiler_params=params(40),
+        compiler_params=params(12),
         name="whiten",
     )(at, *pieces, inverse, running_cov)
 

time: 86.6 us -> 81.4 us (0.940)
  local copies, waits for them, and re-layouts: 10.4 us -> 3.05 us
  starting transfers between devices: 14.1 us -> 16 us
  Pallas kernels: 55.4 us -> 56.7 us
  other arithmetic: 2.23 us -> 1.25 us
    unnamed x21 -> x9, local copies, waits for them, and re-layouts: 9.32 us -> 1.97 us
    pallas_call x1, Pallas kernels: 3.77 us -> 5.69 us  [pooled_rows(): pl.pallas_call(pool_kernel, grid=(width // COLS,), in_specs=[pl.BlockSpec...]
    ppermute x1, starting transfers between devices: 2.16 us -> 3.64 us  [body_fixed(): far_half = lax.ppermute(mine, 'seq', [(0, 2), (1, 3)])]
    pallas_call x1, Pallas kernels: 10 us -> 8.64 us  [factor_first(): pl.pallas_call(functools.partial(load_kernel, panels), in_specs=[pl.Block...]
    add x1, other arithmetic: 1.15 us -> 0.08 us  [body_fixed(): prior = prior + jnp.where(core == 1, core_states, 0.0)]
  transfers between devices with their start and end apart: 13 -> 13, of which waited for: 2 -> 2; matrix products, arithmetic and copies ran while one was open for 2% -> 3% of each run, Pallas kernels for 53% -> 55%
where the time goes in v3:
time: 81.4 us; the launch traced here: 81.2 us
  Pallas kernels  56.7 us (70%)
  starting transfers between devices  16 us (20%)
  waiting for transfers between devices  3.37 us (4%)
  local copies, waits for them, and re-layouts  3.05 us (4%)
  other arithmetic  1.25 us (2%)
  between operations  0.82 us (1%)
    pallas_call x3, Pallas kernels, factor_next(): pl.pallas_call(functools.partial(panels_kernel, panels), in_specs=[pl.Blo...  23.1 us
    pallas_call x1, Pallas kernels, encode(): pl.pallas_call(encode_kernel, grid=(steps,), in_specs=[pl.BlockSpec(hidde...  13.3 us
    ppermute x12, starting transfers between devices, swap(): return lax.ppermute(x, axis, [(i, i ^ by) for i in range(size)])  12.4 us
    pallas_call x1, Pallas kernels, factor_first(): pl.pallas_call(functools.partial(load_kernel, panels), in_specs=[pl.Block...  8.64 us
    pallas_call x1, Pallas kernels, whiten(): pl.pallas_call(whiten_kernel, in_specs=[pl.BlockSpec(memory_space=SMEM)]...  6.04 us
    pallas_call x1, Pallas kernels, pooled_rows(): pl.pallas_call(pool_kernel, grid=(width // COLS,), in_specs=[pl.BlockSpec...  5.69 us
    ppermute x1, starting transfers between devices, body_fixed(): far_half = lax.ppermute(mine, 'seq', [(0, 2), (1, 3)])  3.64 us
    ppermute x12, waiting for transfers between devices, swap(): return lax.ppermute(x, axis, [(i, i ^ by) for i in range(size)])  3.37 us
  transfers between devices with their start and end apart: 13, of which 2 were waited for; matrix products, arithmetic and copies ran while one was open for 3% of the time, Pallas kernels for 55%

profile of v3, /device:TPU:0, one launch (start us, length us, event | category | flops | bytes accessed | tf_op | source)
XLA Modules:
  0.0 81.2 jit_solution(16923150047133257198)
XLA Ops:
  0.6 0.5 collective-permute-start.1
  1.1 1.1 %constant_dynamic-slice_fusion = f32[256,512]{1,0:T(8,128)S(1)} fusion(f32[256,1024]{1,0:T(8,128)} %refs_5_.1, s32[]{:T(128)S(6)} %select_n.24), kind=kLoop, calls=%fused_computation.6 | loop fusion | bytes 1048580 | tf_op jit(solution)/shard_map/dynamic_slice | solution.py:539
  2.2 2.6 %collective-permute-start = (f32[256,512]{1,0:T(8,128)S(1)}, f32[256,512]{1,0:T(8,128)S(1)}, u32[]{:S(2)}, u32[]{:S(2)}) collective-permute-start(f32[256,512]{1,0:T(8,128)S(1)} %constant_dynamic-slice_fusion), channel_id=1, source_target_pairs={{0,2},{1,3},{2,0},{3,1},{4,6},{5,7},{6,4},{7,5},{8,10},{9,11},{10,... | collective-permute-start | bytes 1572872 | tf_op jit(solution)/shard_map/ppermute | solution.py:492
  4.8 0.0 copy-start.2
  4.8 13.3 %encode.1 = (bf16[2,256,1024]{2,1,0:T(8,128)(2,1)}, f32[2,256,1024]{2,1,0:T(8,128)}, f32[2,256,1024]{2,1,0:T(8,128)}, f32[8,2,72,128]{3,2,1,0:T(8,128)}) custom-call(bf16[2,256,1024]{2,1,0:T(8,128)(2,1)} %bitcast.10, bf16[1024,1024]{1,0:T(8,128)(2,1)} %wq_ref.1, bf16[1024,1024]{1,0:T(8,128)(2,1)} %wk_ref.1, bf16[1024,1024]{1,0:T(8,128)(2,1)} %wv_ref.1), custom_call_target="tpu_custom_call" | custom-call | tf_op jit(solution)/shard_map/encode/pallas_call | solution.py:98
  18.1 0.0 collective-permute-done.far_ref
  18.1 0.0 collective-permute-done.1.core_ref
  18.1 0.3 collective-permute-start.2
  18.4 0.3 collective-permute-start.4
  18.7 1.8 %collective-permute-done.2 = f32[8,2,72,128]{3,2,1,0:T(8,128)} collective-permute-done((f32[8,2,72,128]{3,2,1,0:T(8,128)}, f32[8,2,72,128]{3,2,1,0:T(8,128)}, u32[]{:S(2)}, u32[]{:S(2)}) %collective-permute-start.2) | collective-permute-done | bytes 589856 | tf_op jit(solution)/shard_map/ppermute | solution.py:492
  20.5 1.1 %dynamic-slice_add_fusion = f32[4,2,72,128]{3,2,1,0:T(8,128)S(1)} fusion(f32[8,2,72,128]{3,2,1,0:T(8,128)} %collective-permute-done.2, s32[]{:T(128)S(6)} %select_n.25, f32[8,2,72,128]{3,2,1,0:T(8,128)} %get-tuple-element.29), kind=kLoop, calls=%fused_computation.2 | loop fusion | flops 73728 | bytes 884740 | tf_op jit(solution)/shard_map/add | solution.py:548
  21.6 3.6 %collective-permute-start.3 = (f32[4,2,72,128]{3,2,1,0:T(8,128)S(1)}, f32[4,2,72,128]{3,2,1,0:T(8,128)S(1)}, u32[]{:S(2)}, u32[]{:S(2)}) collective-permute-start(f32[4,2,72,128]{3,2,1,0:T(8,128)S(1)} %dynamic-slice_add_fusion), channel_id=1, source_target_pairs={{0,2},{1,3},{4,6},{5,7},{8,10},{9,11},{12,14},{13,15},{16,18},{17,... | collective-permute-start | bytes 884744 | tf_op jit(solution)/shard_map/ppermute | solution.py:549
  25.3 0.0 collective-permute-done.4.far_core_ref
  25.3 0.0 copy-done.2
  25.3 0.0 copy-start.3
  25.3 8.6 %factor_first.1.in_ref = f32[1024,1024]{1,0:T(8,128)S(1)} custom-call(s32[1]{0:T(128)} %bitcast.1.me_ref, f32[256,1024]{1,0:T(8,128)S(1)} %copy-done.2, f32[256,1024]{1,0:T(8,128)S(1)} %collective-permute-done.1.core_ref, f32[256,512]{1,0:T(8,128)S(1)} %collective-permute-done.far_ref, f32[256,512]{1,0:T(8,128)S(1)} %collective-permute-done.4.far_core_ref), custom_call_target="tpu_custom_call" | custom-call | flops 8000000000 | bytes 4194304 | tf_op jit(solution)/shard_map/factor_first/pallas_call | solution.py:356
  33.9 0.0 copy-start
  34.0 1.9 %copy-done = f32[1024,1024]{1,0:T(8,128)} copy-done((f32[1024,1024]{1,0:T(8,128)}, f32[1024,1024]{1,0:T(8,128)S(1)}, u32[]{:S(2)}) %copy-start) | copy-done | bytes 4194328
  35.9 0.0 collective-permute-done.3
  35.9 0.0 collective-permute-start.5
  35.9 0.1 pad_add_fusion.at_ref
  36.0 1.5 %collective-permute-done.5 = f32[4,2,72,128]{3,2,1,0:T(8,128)S(1)} collective-permute-done((f32[4,2,72,128]{3,2,1,0:T(8,128)S(1)}, f32[4,2,72,128]{3,2,1,0:T(8,128)S(1)}, u32[]{:S(2)}, u32[]{:S(2)}) %collective-permute-start.5) | collective-permute-done | bytes 294944 | tf_op jit(solution)/shard_map/ppermute | solution.py:492
  37.5 0.1 fusion.prior_ref
  37.6 0.0 copy-done.3
  37.6 0.0 copy-start.1
  37.6 5.7 %pool.1 = f32[2,1024]{1,0:T(2,128)S(1)} custom-call(s32[2]{0:T(128)S(1)} %bitcast.9, s32[1]{0:T(128)} %bitcast.3.start_ref, bf16[2,256,1024]{2,1,0:T(8,128)(2,1)} %bitcast.11, bf16[2,256,1024]{2,1,0:T(8,128)(2,1)} %get-tuple-element.25.fq_ref, f32[2,256,1024]{2,1,0:T(8,128)} %get-tuple-element.26.num_ref, f32[2,256,1024]{2,1,0:T(8,128)} %get-tuple-element.27.den_ref, ...), custom_call_target="tpu_custom_call" | custom-call | tf_op jit(solution)/shard_map/pool/pallas_call | solution.py:178
  43.3 1.3 %collective-permute-start.6 = (f32[2,1024]{1,0:T(2,128)S(1)}, f32[2,1024]{1,0:T(2,128)S(1)}, u32[]{:S(2)}, u32[]{:S(2)}) collective-permute-start(f32[2,1024]{1,0:T(2,128)S(1)} %pool.1), channel_id=1, source_target_pairs={{0,1},{1,0},{2,3},{3,2},{4,5},{5,4},{6,7},{7,6},{8,9},{9,8},{10,11... | collective-permute-start | bytes 24584 | tf_op jit(solution)/shard_map/ppermute | solution.py:492
  44.6 0.0 collective-permute-start.7
  44.6 1.4 %collective-permute-start.8 = (f32[2,1024]{1,0:T(2,128)S(1)}, f32[2,1024]{1,0:T(2,128)S(1)}, u32[]{:S(2)}, u32[]{:S(2)}) collective-permute-start(f32[2,1024]{1,0:T(2,128)S(1)} %pool.1), channel_id=1, source_target_pairs={{0,3},{1,2},{2,1},{3,0},{4,7},{5,6},{6,5},{7,4},{8,11},{9,10},{10,... | collective-permute-start | bytes 24584 | tf_op jit(solution)/shard_map/ppermute | solution.py:492
  46.0 0.0 copy-done.1
  46.0 8.4 %factor_next.3.in_ref = f32[1024,1024]{1,0:T(8,128)S(1)} custom-call(f32[1024,1024]{1,0:T(8,128)S(1)} %copy-done.1), custom_call_target="tpu_custom_call", output_to_operand_aliasing={{}: (0, {})} | custom-call | flops 8000000000 | bytes 4194304 | tf_op jit(solution)/shard_map/factor_next/pallas_call | solution.py:370
  54.4 0.0 collective-permute-done.6
  54.4 0.0 collective-permute-done.7
  54.4 0.0 collective-permute-done.8
  54.5 1.6 %collective-permute-start.9 = (f32[1,2,1024]{2,1,0:T(2,128)S(1)}, f32[1,2,1024]{2,1,0:T(2,128)S(1)}, u32[]{:S(2)}, u32[]{:S(2)}) collective-permute-start(f32[1,2,1024]{2,1,0:T(2,128)S(1)} %add_bitcast_fusion), channel_id=1, source_target_pairs={{0,4},{4,0},{8,12},{12,8},{16,20},{20,16},{24,28},{28,24},{1,5},{5... | collective-permute-start | bytes 24584 | tf_op jit(solution)/shard_map/ppermute | solution.py:492
  56.0 7.7 %factor_next.4.in_ref = f32[1024,1024]{1,0:T(8,128)S(1)} custom-call(f32[1024,1024]{1,0:T(8,128)S(1)} %factor_next.3.in_ref), custom_call_target="tpu_custom_call", output_to_operand_aliasing={{}: (0, {})} | custom-call | flops 8000000000 | bytes 4194304 | tf_op jit(solution)/shard_map/factor_next/pallas_call | solution.py:370
  63.8 0.0 collective-permute-done.9
  63.8 1.6 %collective-permute-start.10 = (f32[2,2,1024]{2,1,0:T(2,128)S(1)}, f32[2,2,1024]{2,1,0:T(2,128)S(1)}, u32[]{:S(2)}, u32[]{:S(2)}) collective-permute-start(f32[2,2,1024]{2,1,0:T(2,128)S(1)} %constant_dynamic-update-slice_fusion.refs_0_), channel_id=1, source_target_pairs={{0,8},{4,12},{8,0},{12,4},{16,24},{20,28},{24,16},{28,20},{1,9},{5... | collective-permute-start | bytes 49160 | tf_op jit(solution)/shard_map/ppermute | solution.py:492
  65.5 2.6 %collective-permute-start.11 = (f32[2,2,1024]{2,1,0:T(2,128)S(1)}, f32[2,2,1024]{2,1,0:T(2,128)S(1)}, u32[]{:S(2)}, u32[]{:S(2)}) collective-permute-start(f32[2,2,1024]{2,1,0:T(2,128)S(1)} %constant_dynamic-update-slice_fusion.refs_0_), channel_id=1, source_target_pairs={{0,16},{4,20},{8,24},{12,28},{16,0},{20,4},{24,8},{28,12},{1,17},{... | collective-permute-start | bytes 49160 | tf_op jit(solution)/shard_map/ppermute | solution.py:492
  68.1 0.2 collective-permute-start.12
  68.3 6.9 %factor_next.5.refs_4_ = f32[1024,1024]{1,0:T(8,128)S(1)} custom-call(f32[1024,1024]{1,0:T(8,128)S(1)} %factor_next.4.in_ref), custom_call_target="tpu_custom_call", output_to_operand_aliasing={{}: (0, {})} | custom-call | flops 8000000000 | bytes 4194304 | tf_op jit(solution)/shard_map/factor_next/pallas_call | solution.py:370
  75.1 0.0 collective-permute-done.10.refs_1_
  75.2 0.0 collective-permute-done.11.refs_2_
  75.2 0.0 collective-permute-done.12.refs_3_
  75.2 6.0 %whiten.1 = (f32[2,1024]{1,0:T(2,128)}, f32[256,1024]{1,0:T(8,128)}, f32[1,1]{1,0:T(1,128)}) custom-call(s32[2]{0:T(128)S(1)} %pad_add_fusion.at_ref, f32[2,2,1024]{2,1,0:T(2,128)S(1)} %constant_dynamic-update-slice_fusion.refs_0_, f32[2,2,1024]{2,1,0:T(2,128)S(1)} %collective-permute-done.10.refs_1_, f32[2,2,1024]{2,1,0:T(2,128)S(1)} %collective-permute-done.11.refs_2_, ...), custom_call_target="tpu_custom_call" | custom-call | tf_op jit(solution)/shard_map/whiten/pallas_call | solution.py:467
  (3 shorter events, 0.0 us)
Async XLA Ops:
  0.6 17.5 %collective-permute-start.1 = (f32[256,1024]{1,0:T(8,128)}, f32[256,1024]{1,0:T(8,128)S(1)}, u32[]{:S(2)}, u32[]{:S(2)}) collective-permute-start(f32[256,1024]{1,0:T(8,128)} %refs_5_.1), channel_id=1, source_target_pairs={{0,1},{1,0},{2,3},{3,2},{4,5},{5,4},{6,7},{7,6},{8,9},{9,8},{10,11... | collective-permute-start | bytes 3145736 | tf_op jit(solution)/shard_map/ppermute | solution.py:492
  2.2 15.9 %collective-permute-start = (f32[256,512]{1,0:T(8,128)S(1)}, f32[256,512]{1,0:T(8,128)S(1)}, u32[]{:S(2)}, u32[]{:S(2)}) collective-permute-start(f32[256,512]{1,0:T(8,128)S(1)} %constant_dynamic-slice_fusion), channel_id=1, source_target_pairs={{0,2},{1,3},{2,0},{3,1},{4,6},{5,7},{6,4},{7,5},{8,10},{9,11},{10,... | collective-permute-start | bytes 1572872 | tf_op jit(solution)/shard_map/ppermute | solution.py:492
  4.8 20.4 %copy-start.2 = (f32[256,1024]{1,0:T(8,128)S(1)}, f32[256,1024]{1,0:T(8,128)}, u32[]{:S(2)}) copy-start(f32[256,1024]{1,0:T(8,128)} %refs_5_.1) | copy-start | bytes 3145732
  18.1 2.4 %collective-permute-start.2 = (f32[8,2,72,128]{3,2,1,0:T(8,128)}, f32[8,2,72,128]{3,2,1,0:T(8,128)}, u32[]{:S(2)}, u32[]{:S(2)}) collective-permute-start(f32[8,2,72,128]{3,2,1,0:T(8,128)} %get-tuple-element.29), channel_id=1, source_target_pairs={{0,1},{1,0},{2,3},{3,2},{4,5},{5,4},{6,7},{7,6},{8,9},{9,8},{10,11... | collective-permute-start | bytes 1769480 | tf_op jit(solution)/shard_map/ppermute | solution.py:492
  18.4 6.9 %collective-permute-start.4 = (f32[256,512]{1,0:T(8,128)S(1)}, f32[256,512]{1,0:T(8,128)S(1)}, u32[]{:S(2)}, u32[]{:S(2)}) collective-permute-start(f32[256,512]{1,0:T(8,128)S(1)} %collective-permute-done.far_ref), channel_id=1, source_target_pairs={{0,1},{1,0},{2,3},{3,2},{4,5},{5,4},{6,7},{7,6},{8,9},{9,8},{10,11... | collective-permute-start | bytes 1572872 | tf_op jit(solution)/shard_map/ppermute | solution.py:492
  21.6 14.3 %collective-permute-start.3 = (f32[4,2,72,128]{3,2,1,0:T(8,128)S(1)}, f32[4,2,72,128]{3,2,1,0:T(8,128)S(1)}, u32[]{:S(2)}, u32[]{:S(2)}) collective-permute-start(f32[4,2,72,128]{3,2,1,0:T(8,128)S(1)} %dynamic-slice_add_fusion), channel_id=1, source_target_pairs={{0,2},{1,3},{4,6},{5,7},{8,10},{9,11},{12,14},{13,15},{16,18},{17,... | collective-permute-start | bytes 884744 | tf_op jit(solution)/shard_map/ppermute | solution.py:549
  25.3 12.3 %copy-start.3 = (s32[1,2]{1,0:T(1,128)S(1)}, s32[1,2]{1,0:T(1,128)}, u32[]{:S(2)}) copy-start(s32[1,2]{1,0:T(1,128)} %param.8) | copy-start | bytes 28
  33.9 2.0 %copy-start = (f32[1024,1024]{1,0:T(8,128)}, f32[1024,1024]{1,0:T(8,128)S(1)}, u32[]{:S(2)}) copy-start(f32[1024,1024]{1,0:T(8,128)S(1)} %factor_first.1.in_ref) | copy-start | bytes 12582916
  35.9 1.6 %collective-permute-start.5 = (f32[4,2,72,128]{3,2,1,0:T(8,128)S(1)}, f32[4,2,72,128]{3,2,1,0:T(8,128)S(1)}, u32[]{:S(2)}, u32[]{:S(2)}) collective-permute-start(f32[4,2,72,128]{3,2,1,0:T(8,128)S(1)} %collective-permute-done.3), channel_id=1, source_target_pairs={{0,1},{1,0},{2,3},{3,2},{4,5},{5,4},{6,7},{7,6},{8,9},{9,8},{10,11... | collective-permute-start | bytes 884744 | tf_op jit(solution)/shard_map/ppermute | solution.py:492
  37.6 8.4 %copy-start.1 = (f32[1024,1024]{1,0:T(8,128)S(1)}, f32[1024,1024]{1,0:T(8,128)}, u32[]{:S(2)}) copy-start(f32[1024,1024]{1,0:T(8,128)} %copy-done) | copy-start | bytes 12582916
  43.3 11.1 %collective-permute-start.6 = (f32[2,1024]{1,0:T(2,128)S(1)}, f32[2,1024]{1,0:T(2,128)S(1)}, u32[]{:S(2)}, u32[]{:S(2)}) collective-permute-start(f32[2,1024]{1,0:T(2,128)S(1)} %pool.1), channel_id=1, source_target_pairs={{0,1},{1,0},{2,3},{3,2},{4,5},{5,4},{6,7},{7,6},{8,9},{9,8},{10,11... | collective-permute-start | bytes 24584 | tf_op jit(solution)/shard_map/ppermute | solution.py:492
  44.6 9.9 %collective-permute-start.7 = (f32[2,1024]{1,0:T(2,128)S(1)}, f32[2,1024]{1,0:T(2,128)S(1)}, u32[]{:S(2)}, u32[]{:S(2)}) collective-permute-start(f32[2,1024]{1,0:T(2,128)S(1)} %pool.1), channel_id=1, source_target_pairs={{0,2},{1,3},{2,0},{3,1},{4,6},{5,7},{6,4},{7,5},{8,10},{9,11},{10,... | collective-permute-start | bytes 24584 | tf_op jit(solution)/shard_map/ppermute | solution.py:492
  44.6 9.9 %collective-permute-start.8 = (f32[2,1024]{1,0:T(2,128)S(1)}, f32[2,1024]{1,0:T(2,128)S(1)}, u32[]{:S(2)}, u32[]{:S(2)}) collective-permute-start(f32[2,1024]{1,0:T(2,128)S(1)} %pool.1), channel_id=1, source_target_pairs={{0,3},{1,2},{2,1},{3,0},{4,7},{5,6},{6,5},{7,4},{8,11},{9,10},{10,... | collective-permute-start | bytes 24584 | tf_op jit(solution)/shard_map/ppermute | solution.py:492
  54.5 9.3 %collective-permute-start.9 = (f32[1,2,1024]{2,1,0:T(2,128)S(1)}, f32[1,2,1024]{2,1,0:T(2,128)S(1)}, u32[]{:S(2)}, u32[]{:S(2)}) collective-permute-start(f32[1,2,1024]{2,1,0:T(2,128)S(1)} %add_bitcast_fusion), channel_id=1, source_target_pairs={{0,4},{4,0},{8,12},{12,8},{16,20},{20,16},{24,28},{28,24},{1,5},{5... | collective-permute-start | bytes 24584 | tf_op jit(solution)/shard_map/ppermute | solution.py:492
  63.8 11.3 %collective-permute-start.10 = (f32[2,2,1024]{2,1,0:T(2,128)S(1)}, f32[2,2,1024]{2,1,0:T(2,128)S(1)}, u32[]{:S(2)}, u32[]{:S(2)}) collective-permute-start(f32[2,2,1024]{2,1,0:T(2,128)S(1)} %constant_dynamic-update-slice_fusion.refs_0_), channel_id=1, source_target_pairs={{0,8},{4,12},{8,0},{12,4},{16,24},{20,28},{24,16},{28,20},{1,9},{5... | collective-permute-start | bytes 49160 | tf_op jit(solution)/shard_map/ppermute | solution.py:492
  65.5 9.7 %collective-permute-start.11 = (f32[2,2,1024]{2,1,0:T(2,128)S(1)}, f32[2,2,1024]{2,1,0:T(2,128)S(1)}, u32[]{:S(2)}, u32[]{:S(2)}) collective-permute-start(f32[2,2,1024]{2,1,0:T(2,128)S(1)} %constant_dynamic-update-slice_fusion.refs_0_), channel_id=1, source_target_pairs={{0,16},{4,20},{8,24},{12,28},{16,0},{20,4},{24,8},{28,12},{1,17},{... | collective-permute-start | bytes 49160 | tf_op jit(solution)/shard_map/ppermute | solution.py:492
  68.1 7.1 %collective-permute-start.12 = (f32[2,2,1024]{2,1,0:T(2,128)S(1)}, f32[2,2,1024]{2,1,0:T(2,128)S(1)}, u32[]{:S(2)}, u32[]{:S(2)}) collective-permute-start(f32[2,2,1024]{2,1,0:T(2,128)S(1)} %constant_dynamic-update-slice_fusion.refs_0_), channel_id=1, source_target_pairs={{0,24},{4,28},{8,16},{12,20},{16,8},{20,12},{24,0},{28,4},{1,25},{... | collective-permute-start | bytes 49160 | tf_op jit(solution)/shard_map/ppermute | solution.py:492

commit v4 on v3

--- a/solution.py
+++ b/solution.py
@@ -20,6 +20,10 @@
 
 def hbm(x):
     return pltpu.with_memory_space_constraint(x, pltpu.HBM)
+
+
+def vmem(x):
+    return pltpu.with_memory_space_constraint(x, VMEM)
 
 
 def params(mib):
@@ -116,9 +120,8 @@
     )(hbm(hidden), hbm(w_query), hbm(w_key), hbm(w_value))
 
 
-def pool_kernel(len_ref, start_ref, h_ref, fq_ref, num_ref, den_ref, prior_ref, wo_ref, out_ref):
+def pool_columns(step, steps, len_ref, start_ref, h_ref, fq_ref, num_ref, den_ref, prior_ref, wo_ref, out_ref):
     count, span = fq_ref.shape[0], fq_ref.shape[1]
-    step = pl.program_id(0)
     low = iota((HEAD_DIM, LANES), 1) < HEAD_DIM
     same_head = (iota((LANES, LANES), 0) < HEAD_DIM) == (iota((LANES, LANES), 1) < HEAD_DIM)
     summing = jnp.concatenate([same_head.astype(BF16)] * 2, axis=0)
@@ -165,10 +168,14 @@
     here = pl.ds(pl.multiple_of(step * COLS, COLS), COLS)
     out_ref[:, here] += jnp.concatenate(hsums, axis=0)
 
-    @pl.when(step == pl.num_programs(0) - 1)
+    @pl.when(step == steps - 1)
     def _():
         for module in range(count):
             out_ref[module : module + 1, :] /= len_ref[module].astype(F32)
+
+
+def pool_kernel(*refs):
+    pool_columns(pl.program_id(0), pl.num_programs(0), *refs)
 
 
 def pooled_rows(flat_len, start, hidden, fq, num, den, prior, w_out):
@@ -292,6 +299,8 @@
         ref[low:high, :low] = scaled[:, n - high :]
     if k + 1 == panels:
         return
+    if k % 2 == 0:
+        ref[low:high, high : high + LANES] = jnp.zeros((LANES, LANES), F32)
     rest = n - high
     coefs, beyond = split_six(scaled[:, :rest], 0)
     near = slice(high, high + LANES)
@@ -345,9 +354,78 @@
 
 
 def panels_kernel(panels, in_ref, out_ref):
-    out_ref[...] = in_ref[...]
+    del in_ref
     for k in panels:
         eliminate(out_ref, k)
+
+
+def panels_pool_kernel(panels, in_ref, len_ref, start_ref, core_ref, *refs):
+    del in_ref
+    *sources, matrix_ref, out_ref = refs[:10]
+    *held, prior_ref, beside_ref, sems = refs[10:]
+    half = prior_ref.shape[0] // 2
+    own = pl.ds(core_ref[0] * half, half)
+    other = pl.ds((1 - core_ref[0]) * half, half)
+    targets = held + [prior_ref.at[own], prior_ref.at[other], beside_ref]
+    copies = [
+        pltpu.make_async_copy(source, to, sems.at[i])
+        for i, (source, to) in enumerate(zip(sources, targets))
+    ]
+    for copy in copies:
+        copy.start()
+    for k in panels:
+        eliminate(matrix_ref, k)
+    for copy in copies:
+        copy.wait()
+    h_ref, fq_ref, num_ref, den_ref, wo_ref = held
+
+    @pl.when(core_ref[0] == 1)
+    def _():
+        prior_ref[...] += beside_ref[...]
+
+    steps = wo_ref.shape[0] // COLS
+    pairs = COLS // LANES
+
+    def run(step, carried):
+        cols = pl.ds(pl.multiple_of(step * COLS, COLS), COLS)
+        pool_columns(
+            step,
+            steps,
+            len_ref,
+            start_ref,
+            h_ref.at[:, :, cols],
+            fq_ref.at[:, :, cols],
+            num_ref.at[:, :, cols],
+            den_ref.at[:, :, cols],
+            prior_ref.at[pl.ds(step * pairs, pairs)],
+            wo_ref.at[cols, :],
+            out_ref,
+        )
+        return carried
+
+    lax.fori_loop(0, steps, run, 0)
+
+
+def factor_next_pool(
+    panels, matrix, flat_len, start, core, hidden, fq, num, den, w_out, far_half, other_half, beside
+):
+    n = matrix.shape[1]
+    count, span, width = hidden.shape
+    whole, anywhere = pl.BlockSpec(memory_space=VMEM), pl.BlockSpec(memory_space=pl.ANY)
+    operands = [hbm(x) for x in (hidden, fq, num, den, w_out)]
+    states = [far_half, other_half, beside]
+    return pl.pallas_call(
+        functools.partial(panels_pool_kernel, panels),
+        in_specs=[whole] + [pl.BlockSpec(memory_space=SMEM)] * 3 + [anywhere] * 8,
+        out_specs=[whole, whole],
+        out_shape=[pltpu.VMEM((n, n), F32), jax.ShapeDtypeStruct((count, width), F32)],
+        scratch_shapes=[pltpu.VMEM(x.shape, x.dtype) for x in operands + [beside, beside]]
+        + [pltpu.SemaphoreType.DMA((8,))],
+        input_output_aliases={0: 0},
+        compiler_params=params(24),
+        name="factor_next_pool",
+        cost_estimate=pl.CostEstimate(flops=8_000_000_000, transcendentals=0, bytes_accessed=12 << 20),
+    )(vmem(matrix), flat_len, start, core, *operands, *states)
 
 
 def factor_first(panels, me, own, core, far, far_core):
@@ -357,7 +435,7 @@
         functools.partial(load_kernel, panels),
         in_specs=[pl.BlockSpec(memory_space=SMEM)] + [anywhere] * 4,
         out_specs=pl.BlockSpec(memory_space=VMEM),
-        out_shape=jax.ShapeDtypeStruct((n, n), F32),
+        out_shape=pltpu.VMEM((n, n), F32),
         scratch_shapes=[pltpu.SemaphoreType.DMA((4,))],
         compiler_params=params(14),
         name="factor_first",
@@ -371,18 +449,19 @@
         functools.partial(panels_kernel, panels),
         in_specs=[pl.BlockSpec(memory_space=VMEM)],
         out_specs=pl.BlockSpec(memory_space=VMEM),
-        out_shape=jax.ShapeDtypeStruct((n, n), F32),
+        out_shape=pltpu.VMEM((n, n), F32),
         input_output_aliases={0: 0},
         compiler_params=params(14),
         name="factor_next",
         cost_estimate=pl.CostEstimate(flops=8_000_000_000, transcendentals=0, bytes_accessed=4 << 20),
-    )(matrix)
+    )(vmem(matrix))
 
 
 def whiten_kernel(
     at_ref, *refs
 ):
-    *piece_refs, inv_ref, cov_ref, white_ref, cov_out_ref, loss_ref, rows_ref, centred_ref, held_ref = refs
+    *piece_refs, inv_ref, cov_ref, white_ref, cov_out_ref, loss_ref = refs[:-5]
+    rows_ref, centred_ref, held_ref, new_cov_ref, sem = refs[-5:]
     count, n = white_ref.shape
     total = centred_ref.shape[0]
     chunks = n // LANES
@@ -398,9 +477,24 @@
     centred = embed - jnp.sum(embed, axis=0, keepdims=True) / total
     weight = 0.5 / (total - 1)
     root = 2.0**0.5
-    for k in range(chunks):
-        upto = (k + 1) * LANES
-        rows_ref[:, k, :] = dot_f32(root * centred[:, :upto], inv_ref[k * LANES : upto, :upto], 1, 1)
+    start = pl.multiple_of(at_ref[1] * share, share)
+    centred_ref[...] = centred
+    left, right = split_six(centred_ref[:, pl.ds(start, share)], 0)[0], split_six(centred, 0)[1]
+    new_cov_ref[...] = 0.5 * cov_ref[...] + weight * dot(left, right, 0, 0)
+    written = pltpu.make_async_copy(new_cov_ref, cov_out_ref, sem)
+    written.start()
+    thirds = jnp.concatenate(split(root * centred, 3), axis=0)
+    for k in range(0, chunks, 2):
+        upto = (k + 2) * LANES
+        one, two, three = split(inv_ref[k * LANES : upto, :upto], 3)
+        by_one = dot(thirds[:, :upto], one, 1, 1)
+        by_two = dot(thirds[: 2 * total, :upto], two, 1, 1)
+        product = by_one[:total] + (by_one[total : 2 * total] + by_two[:total])
+        product = product + (
+            by_one[2 * total :] + by_two[total:] + dot(thirds[:total, :upto], three, 1, 1)
+        )
+        rows_ref[:, k, :] = product[:, :LANES]
+        rows_ref[:, k + 1, :] = product[:, LANES:]
     w = [rows_ref[a] for a in range(total)]
     pairs = [(a, b) for a in range(total) for b in range(a, total)]
     products = jnp.concatenate([w[a] * w[b] for a, b in pairs], axis=0)
@@ -453,21 +547,18 @@
         own = rows_ref[at_ref[0] * count + m]
         for k in range(chunks):
             white_ref[m : m + 1, k * LANES : (k + 1) * LANES] = own[k : k + 1, :]
-    start = pl.multiple_of(at_ref[1] * share, share)
-    centred_ref[...] = centred
-    left = centred_ref[:, pl.ds(start, share)]
-    cov_out_ref[...] = 0.5 * cov_ref[...] + weight * dot_f32(left, centred, 0, 0)
+    written.wait()
 
 
 def whiten(at, pieces, inverse, running_cov):
     groups = sum(piece.shape[0] for piece in pieces)
     count, n = pieces[0].shape[1:]
     total = groups * count
-    vmem = pl.BlockSpec(memory_space=VMEM)
+    whole = pl.BlockSpec(memory_space=VMEM)
     return pl.pallas_call(
         whiten_kernel,
-        in_specs=[pl.BlockSpec(memory_space=SMEM)] + [vmem] * (len(pieces) + 2),
-        out_specs=[vmem, vmem, vmem],
+        in_specs=[pl.BlockSpec(memory_space=SMEM)] + [whole] * (len(pieces) + 2),
+        out_specs=[whole, pl.BlockSpec(memory_space=pl.ANY), whole],
         out_shape=[
             jax.ShapeDtypeStruct((count, n), F32),
             jax.ShapeDtypeStruct(running_cov.shape, F32),
@@ -477,6 +568,8 @@
             pltpu.VMEM((total, n // LANES, LANES), F32),
             pltpu.VMEM((total, n), F32),
             pltpu.VMEM((groups, count, n), F32),
+            pltpu.VMEM(running_cov.shape, F32),
+            pltpu.SemaphoreType.DMA,
         ],
         compiler_params=params(12),
         name="whiten",
@@ -534,7 +627,7 @@
     me, group = lax.axis_index("seq"), lax.axis_index("dp")
     width = hidden.shape[2]
     half = width // 2
-    core, far_side = me & 1, me >= 2
+    core = me & 1
     at = jnp.stack([group, me]).astype(jnp.int32)
     chip_columns = lax.dynamic_slice_in_dim(running_cov, (me >> 1) * half, half, 1)
     far_cov = swap(chip_columns, "seq", 2)
@@ -544,30 +637,41 @@
     core_states = swap(states, "seq", 1)
     far_core_cov = swap(far_cov, "seq", 1)
     quarter = states.shape[0] // 2
+    matrix = factor_first((0,), at[1:], running_cov, core_cov, far_cov, far_core_cov)
+    core_states, matrix = lax.optimization_barrier((core_states, matrix))
     mine = lax.dynamic_slice_in_dim(states, core * quarter, quarter, 0)
     mine = mine + lax.dynamic_slice_in_dim(core_states, core * quarter, quarter, 0)
     far_half = lax.ppermute(mine, "seq", [(0, 2), (1, 3)])
-    matrix = factor_first((0, 1), at[1:], running_cov, core_cov, far_cov, far_core_cov)
+    matrix = factor_next((1, 2), matrix)
     far_half, matrix = lax.optimization_barrier((far_half, matrix))
     other_half = swap(far_half, "seq", 1)
-    prior = jnp.where(
-        core == 0,
-        jnp.concatenate([far_half, other_half], axis=0),
-        jnp.concatenate([other_half, far_half], axis=0),
+    matrix = factor_next((3,), matrix)
+    other_half, matrix = lax.optimization_barrier((other_half, matrix))
+    matrix, partial = factor_next_pool(
+        (4,),
+        matrix,
+        flat_len,
+        start,
+        core.astype(jnp.int32).reshape(1),
+        hidden,
+        fq,
+        num,
+        den,
+        w_out,
+        far_half,
+        other_half,
+        core_states,
     )
-    prior = prior + jnp.where(core == 1, core_states, 0.0)
-    partial = pooled_rows(flat_len, start, hidden, fq, num, den, prior, w_out)
-    partial, matrix = lax.optimization_barrier((partial, matrix))
     got = [swap(partial, "seq", by) for by in (1, 2, 3)]
-    matrix = factor_next((2, 3), matrix)
+    matrix = factor_next((5,), matrix)
     partial, got, matrix = lax.optimization_barrier((partial, got, matrix))
     embed = ((partial + got[0]) + (got[1] + got[2]))[None]
     beside = swap(embed, "dp", 1)
-    matrix = factor_next((4, 5), matrix)
+    matrix = factor_next((6,), matrix)
     embed, beside, matrix = lax.optimization_barrier((embed, beside, matrix))
     embed = jnp.concatenate([embed, beside], axis=0)
     pieces = [embed] + [swap(embed, "dp", by) for by in (2, 4, 6)]
-    matrix = factor_next((6, 7), matrix)
+    matrix = factor_next((7,), matrix)
     white, cov, loss = whiten(at, pieces, matrix, running_cov)
     return white, cov, loss.reshape(())
 

time: 81.4 us -> 72.8 us (0.89)
  Pallas kernels: 56.7 us -> 52.7 us
  local copies, waits for them, and re-layouts: 3.05 us -> 1.19 us
  waiting for transfers between devices: 3.37 us -> 2.04 us
  other arithmetic: 1.25 us -> 0.13 us
    pallas_call x1, Pallas kernels: 8.64 us -> 4.71 us  [factor_first(): pl.pallas_call(functools.partial(load_kernel, panels), in_specs=[pl.Block...]
    pallas_call x1, Pallas kernels: 5.69 us -> 7.69 us  [factor_next_pool(): pl.pallas_call(functools.partial(panels_pool_kernel, panels), in_specs=[w...]
    unnamed x9 -> x7, local copies, waits for them, and re-layouts: 1.97 us -> 0.02 us
    pallas_call x1, Pallas kernels: 6.04 us -> 4.29 us  [whiten(): pl.pallas_call(whiten_kernel, in_specs=[pl.BlockSpec(memory_space=SMEM)]...]
    ppermute x12, waiting for transfers between devices: 3.37 us -> 2.04 us  [swap(): return lax.ppermute(x, axis, [(i, i ^ by) for i in range(size)])]
    add x1, other arithmetic: 1.08 us -> 0.04 us  [body_fixed(): mine + lax.dynamic_slice_in_dim(core_states, core * quarter, quarter, 0)]
    pallas_call x3 -> x5, Pallas kernels: 23.1 us -> 22.9 us  [factor_next(): pl.pallas_call(functools.partial(panels_kernel, panels), in_specs=[pl.Blo...]
  transfers between devices with their start and end apart: 13 -> 13, of which waited for: 2 -> 2; matrix products, arithmetic and copies ran while one was open for 3% -> 2% of each run, Pallas kernels for 55% -> 56%
where the time goes in v4:
time: 72.8 us; the launch traced here: 72.6 us
  Pallas kernels  52.7 us (72%)
  starting transfers between devices  15.5 us (21%)
  waiting for transfers between devices  2.04 us (3%)
  local copies, waits for them, and re-layouts  1.19 us (2%)
  between operations  1.01 us (1%)
    pallas_call x5, Pallas kernels, factor_next(): pl.pallas_call(functools.partial(panels_kernel, panels), in_specs=[pl.Blo...  22.9 us
    pallas_call x1, Pallas kernels, encode(): pl.pallas_call(encode_kernel, grid=(steps,), in_specs=[pl.BlockSpec(hidde...  13.2 us
    ppermute x12, starting transfers between devices, swap(): return lax.ppermute(x, axis, [(i, i ^ by) for i in range(size)])  12 us
    pallas_call x1, Pallas kernels, factor_next_pool(): pl.pallas_call(functools.partial(panels_pool_kernel, panels), in_specs=[w...  7.69 us
    pallas_call x1, Pallas kernels, factor_first(): pl.pallas_call(functools.partial(load_kernel, panels), in_specs=[pl.Block...  4.71 us
    pallas_call x1, Pallas kernels, whiten(): pl.pallas_call(whiten_kernel, in_specs=[pl.BlockSpec(memory_space=SMEM)]...  4.29 us
    ppermute x1, starting transfers between devices, body_fixed(): far_half = lax.ppermute(mine, 'seq', [(0, 2), (1, 3)])  3.49 us
    ppermute x12, waiting for transfers between devices, swap(): return lax.ppermute(x, axis, [(i, i ^ by) for i in range(size)])  2.04 us
  transfers between devices with their start and end apart: 13, of which 2 were waited for; matrix products, arithmetic and copies ran while one was open for 2% of the time, Pallas kernels for 56%

profile of v4, /device:TPU:0, one launch (start us, length us, event | category | flops | bytes accessed | tf_op | source)
XLA Modules:
  0.0 72.6 jit_solution(6030078480170343445)
XLA Ops:
  0.6 0.5 collective-permute-start.1
  1.1 0.0 copy-start
  1.1 1.2 %constant_dynamic-slice_fusion = f32[256,512]{1,0:T(8,128)S(1)} fusion(f32[256,1024]{1,0:T(8,128)} %refs_5_.1, s32[]{:T(128)S(6)} %select_n.7), kind=kLoop, calls=%fused_computation.4 | loop fusion | bytes 1048580 | tf_op jit(solution)/shard_map/dynamic_slice | solution.py:632
  2.3 2.6 %collective-permute-start = (f32[256,512]{1,0:T(8,128)S(1)}, f32[256,512]{1,0:T(8,128)S(1)}, u32[]{:S(2)}, u32[]{:S(2)}) collective-permute-start(f32[256,512]{1,0:T(8,128)S(1)} %constant_dynamic-slice_fusion), channel_id=1, source_target_pairs={{0,2},{1,3},{2,0},{3,1},{4,6},{5,7},{6,4},{7,5},{8,10},{9,11},{10,... | collective-permute-start | bytes 1572872 | tf_op jit(solution)/shard_map/ppermute | solution.py:585
  4.9 13.2 %encode.1 = (bf16[2,256,1024]{2,1,0:T(8,128)(2,1)}, f32[2,256,1024]{2,1,0:T(8,128)}, f32[2,256,1024]{2,1,0:T(8,128)}, f32[8,2,72,128]{3,2,1,0:T(8,128)}) custom-call(bf16[2,256,1024]{2,1,0:T(8,128)(2,1)} %bitcast.11, bf16[1024,1024]{1,0:T(8,128)(2,1)} %wq_ref.1, bf16[1024,1024]{1,0:T(8,128)(2,1)} %wk_ref.1, bf16[1024,1024]{1,0:T(8,128)(2,1)} %wv_ref.1), custom_call_target="tpu_custom_call" | custom-call | tf_op jit(solution)/shard_map/encode/pallas_call | solution.py:102
  18.1 0.0 collective-permute-done.far_ref
  18.1 0.0 collective-permute-done.1.core_ref
  18.1 0.3 collective-permute-start.3
  18.4 0.1 pad_add_fusion.at_ref
  18.5 0.0 copy-start.2
  18.5 0.3 collective-permute-start.2
  18.8 1.3 %collective-permute-done.3.far_core_ref = f32[256,512]{1,0:T(8,128)S(1)} collective-permute-done((f32[256,512]{1,0:T(8,128)S(1)}, f32[256,512]{1,0:T(8,128)S(1)}, u32[]{:S(2)}, u32[]{:S(2)}) %collective-permute-start.3) | collective-permute-done | bytes 524320 | tf_op jit(solution)/shard_map/ppermute | solution.py:585
  20.1 0.0 copy-done
  20.1 4.7 %factor_first.1.in_ref = f32[1024,1024]{1,0:T(8,128)S(1)} custom-call(s32[1]{0:T(128)} %bitcast.1.me_ref, f32[256,1024]{1,0:T(8,128)S(1)} %copy-done, f32[256,1024]{1,0:T(8,128)S(1)} %collective-permute-done.1.core_ref, f32[256,512]{1,0:T(8,128)S(1)} %collective-permute-done.far_ref, f32[256,512]{1,0:T(8,128)S(1)} %collective-permute-done.3.far_core_ref), custom_call_target="tpu_custom_call" | custom-call | flops 8000000000 | bytes 4194304 | tf_op jit(solution)/shard_map/factor_first/pallas_call | solution.py:434
  24.8 0.0 collective-permute-done.2.refs_7_
  24.8 0.0 copy-done.2
  24.9 3.5 %collective-permute-start.4 = (f32[4,2,72,128]{3,2,1,0:T(8,128)S(1)}, f32[4,2,72,128]{3,2,1,0:T(8,128)S(1)}, u32[]{:S(2)}, u32[]{:S(2)}) collective-permute-start(f32[4,2,72,128]{3,2,1,0:T(8,128)S(1)} %dynamic-slice_add_fusion), channel_id=1, source_target_pairs={{0,2},{1,3},{4,6},{5,7},{8,10},{9,11},{12,14},{13,15},{16,18},{17,... | collective-permute-start | bytes 884744 | tf_op jit(solution)/shard_map/ppermute | solution.py:644
  28.4 8.3 %factor_next.5.in_ref = f32[1024,1024]{1,0:T(8,128)S(1)} custom-call(f32[1024,1024]{1,0:T(8,128)S(1)} %factor_first.1.in_ref), custom_call_target="tpu_custom_call", output_to_operand_aliasing={{}: (0, {})} | custom-call | flops 8000000000 | bytes 4194304 | tf_op jit(solution)/shard_map/factor_next/pallas_call | solution.py:448
  36.7 0.0 copy-start.1
  36.7 0.0 collective-permute-done.4.refs_5_
  36.7 0.1 collective-permute-start.5
  36.8 4.2 %factor_next.6.in_ref = f32[1024,1024]{1,0:T(8,128)S(1)} custom-call(f32[1024,1024]{1,0:T(8,128)S(1)} %factor_next.5.in_ref), custom_call_target="tpu_custom_call", output_to_operand_aliasing={{}: (0, {})} | custom-call | flops 8000000000 | bytes 4194304 | tf_op jit(solution)/shard_map/factor_next/pallas_call | solution.py:448
  41.0 0.0 collective-permute-done.5.refs_6_
  41.0 0.0 copy-done.1
  41.0 7.7 %factor_next_pool.1 = (f32[1024,1024]{1,0:T(8,128)S(1)}, f32[2,1024]{1,0:T(2,128)S(1)}) custom-call(f32[1024,1024]{1,0:T(8,128)S(1)} %factor_next.6.in_ref, s32[2]{0:T(128)S(1)} %bitcast.10, s32[1]{0:T(128)} %bitcast.4.start_ref, s32[1]{0:T(128)} %bitcast.5.core_ref, bf16[2,256,1024]{2,1,0:T(8,128)(2,1)} %bitcast.12, ...), custom_call_target="tpu_custom_call", output_to_operand_aliasing={{0}: (0, {})} | custom-call | flops 8000000000 | bytes 12582912 | tf_op jit(solution)/shard_map/factor_next_pool/pallas_call | solution.py:417
  48.7 0.7 collective-permute-start.8
  49.4 1.6 %collective-permute-start.7 = (f32[2,1024]{1,0:T(2,128)S(1)}, f32[2,1024]{1,0:T(2,128)S(1)}, u32[]{:S(2)}, u32[]{:S(2)}) collective-permute-start(f32[2,1024]{1,0:T(2,128)S(1)} %get-tuple-element.44), channel_id=1, source_target_pairs={{0,2},{1,3},{2,0},{3,1},{4,6},{5,7},{6,4},{7,5},{8,10},{9,11},{10,... | collective-permute-start | bytes 24584 | tf_op jit(solution)/shard_map/ppermute | solution.py:585
  50.9 0.0 collective-permute-start.6
  50.9 3.8 %factor_next.7.in_ref = f32[1024,1024]{1,0:T(8,128)S(1)} custom-call(f32[1024,1024]{1,0:T(8,128)S(1)} %get-tuple-element.43.in_ref), custom_call_target="tpu_custom_call", output_to_operand_aliasing={{}: (0, {})} | custom-call | flops 8000000000 | bytes 4194304 | tf_op jit(solution)/shard_map/factor_next/pallas_call | solution.py:448
  54.7 0.0 collective-permute-done.8
  54.7 0.0 collective-permute-done.7
  54.8 0.0 collective-permute-done.6
  54.8 1.6 %collective-permute-start.9 = (f32[1,2,1024]{2,1,0:T(2,128)S(1)}, f32[1,2,1024]{2,1,0:T(2,128)S(1)}, u32[]{:S(2)}, u32[]{:S(2)}) collective-permute-start(f32[1,2,1024]{2,1,0:T(2,128)S(1)} %add_bitcast_fusion), channel_id=1, source_target_pairs={{0,4},{4,0},{8,12},{12,8},{16,20},{20,16},{24,28},{28,24},{1,5},{5... | collective-permute-start | bytes 24584 | tf_op jit(solution)/shard_map/ppermute | solution.py:585
  56.3 3.5 %factor_next.8.in_ref = f32[1024,1024]{1,0:T(8,128)S(1)} custom-call(f32[1024,1024]{1,0:T(8,128)S(1)} %factor_next.7.in_ref), custom_call_target="tpu_custom_call", output_to_operand_aliasing={{}: (0, {})} | custom-call | flops 8000000000 | bytes 4194304 | tf_op jit(solution)/shard_map/factor_next/pallas_call | solution.py:448
  59.8 0.0 collective-permute-done.9
  59.9 3.7 %collective-permute-start.12 = (f32[2,2,1024]{2,1,0:T(2,128)S(1)}, f32[2,2,1024]{2,1,0:T(2,128)S(1)}, u32[]{:S(2)}, u32[]{:S(2)}) collective-permute-start(f32[2,2,1024]{2,1,0:T(2,128)S(1)} %constant_dynamic-update-slice_fusion.refs_0_), channel_id=1, source_target_pairs={{0,24},{4,28},{8,16},{12,20},{16,8},{20,12},{24,0},{28,4},{1,25},{... | collective-permute-start | bytes 49160 | tf_op jit(solution)/shard_map/ppermute | solution.py:585
  63.5 0.0 collective-permute-start.11
  63.5 0.8 %collective-permute-start.10 = (f32[2,2,1024]{2,1,0:T(2,128)S(1)}, f32[2,2,1024]{2,1,0:T(2,128)S(1)}, u32[]{:S(2)}, u32[]{:S(2)}) collective-permute-start(f32[2,2,1024]{2,1,0:T(2,128)S(1)} %constant_dynamic-update-slice_fusion.refs_0_), channel_id=1, source_target_pairs={{0,8},{4,12},{8,0},{12,4},{16,24},{20,28},{24,16},{28,20},{1,9},{5... | collective-permute-start | bytes 49160 | tf_op jit(solution)/shard_map/ppermute | solution.py:585
  64.3 3.1 %factor_next.9.refs_4_ = f32[1024,1024]{1,0:T(8,128)S(1)} custom-call(f32[1024,1024]{1,0:T(8,128)S(1)} %factor_next.8.in_ref), custom_call_target="tpu_custom_call", output_to_operand_aliasing={{}: (0, {})} | custom-call | flops 8000000000 | bytes 4194304 | tf_op jit(solution)/shard_map/factor_next/pallas_call | solution.py:448
  67.4 0.0 collective-permute-done.12.refs_3_
  67.5 0.7 collective-permute-done.11.refs_2_
  68.1 0.0 collective-permute-done.10.refs_1_
  68.1 4.3 %whiten.1 = (f32[2,1024]{1,0:T(2,128)}, f32[256,1024]{1,0:T(8,128)}, f32[1,1]{1,0:T(1,128)}) custom-call(s32[2]{0:T(128)S(1)} %pad_add_fusion.at_ref, f32[2,2,1024]{2,1,0:T(2,128)S(1)} %constant_dynamic-update-slice_fusion.refs_0_, f32[2,2,1024]{2,1,0:T(2,128)S(1)} %collective-permute-done.10.refs_1_, f32[2,2,1024]{2,1,0:T(2,128)S(1)} %collective-permute-done.11.refs_2_, ...), custom_call_target="tpu_custom_call" | custom-call | tf_op jit(solution)/shard_map/whiten/pallas_call | solution.py:558
  (4 shorter events, 0.1 us)
Async XLA Ops:
  0.6 17.5 %collective-permute-start.1 = (f32[256,1024]{1,0:T(8,128)}, f32[256,1024]{1,0:T(8,128)S(1)}, u32[]{:S(2)}, u32[]{:S(2)}) collective-permute-start(f32[256,1024]{1,0:T(8,128)} %refs_5_.1), channel_id=1, source_target_pairs={{0,1},{1,0},{2,3},{3,2},{4,5},{5,4},{6,7},{7,6},{8,9},{9,8},{10,11... | collective-permute-start | bytes 3145736 | tf_op jit(solution)/shard_map/ppermute | solution.py:585
  1.1 19.0 %copy-start = (f32[256,1024]{1,0:T(8,128)S(1)}, f32[256,1024]{1,0:T(8,128)}, u32[]{:S(2)}) copy-start(f32[256,1024]{1,0:T(8,128)} %refs_5_.1) | copy-start | bytes 3145732
  2.3 15.8 %collective-permute-start = (f32[256,512]{1,0:T(8,128)S(1)}, f32[256,512]{1,0:T(8,128)S(1)}, u32[]{:S(2)}, u32[]{:S(2)}) collective-permute-start(f32[256,512]{1,0:T(8,128)S(1)} %constant_dynamic-slice_fusion), channel_id=1, source_target_pairs={{0,2},{1,3},{2,0},{3,1},{4,6},{5,7},{6,4},{7,5},{8,10},{9,11},{10,... | collective-permute-start | bytes 1572872 | tf_op jit(solution)/shard_map/ppermute | solution.py:585
  18.1 2.0 %collective-permute-start.3 = (f32[256,512]{1,0:T(8,128)S(1)}, f32[256,512]{1,0:T(8,128)S(1)}, u32[]{:S(2)}, u32[]{:S(2)}) collective-permute-start(f32[256,512]{1,0:T(8,128)S(1)} %collective-permute-done.far_ref), channel_id=1, source_target_pairs={{0,1},{1,0},{2,3},{3,2},{4,5},{5,4},{6,7},{7,6},{8,9},{9,8},{10,11... | collective-permute-start | bytes 1572872 | tf_op jit(solution)/shard_map/ppermute | solution.py:585
  18.5 6.4 %copy-start.2 = (f32[8,2,72,128]{3,2,1,0:T(8,128)S(1)}, f32[8,2,72,128]{3,2,1,0:T(8,128)}, u32[]{:S(2)}) copy-start(f32[8,2,72,128]{3,2,1,0:T(8,128)} %get-tuple-element.30) | copy-start | bytes 1769476
  18.5 6.4 %collective-permute-start.2 = (f32[8,2,72,128]{3,2,1,0:T(8,128)}, f32[8,2,72,128]{3,2,1,0:T(8,128)S(1)}, u32[]{:S(2)}, u32[]{:S(2)}) collective-permute-start(f32[8,2,72,128]{3,2,1,0:T(8,128)} %get-tuple-element.30), channel_id=1, source_target_pairs={{0,1},{1,0},{2,3},{3,2},{4,5},{5,4},{6,7},{7,6},{8,9},{9,8},{10,11... | collective-permute-start | bytes 1769480 | tf_op jit(solution)/shard_map/ppermute | solution.py:585
  24.9 11.8 %collective-permute-start.4 = (f32[4,2,72,128]{3,2,1,0:T(8,128)S(1)}, f32[4,2,72,128]{3,2,1,0:T(8,128)S(1)}, u32[]{:S(2)}, u32[]{:S(2)}) collective-permute-start(f32[4,2,72,128]{3,2,1,0:T(8,128)S(1)} %dynamic-slice_add_fusion), channel_id=1, source_target_pairs={{0,2},{1,3},{4,6},{5,7},{8,10},{9,11},{12,14},{13,15},{16,18},{17,... | collective-permute-start | bytes 884744 | tf_op jit(solution)/shard_map/ppermute | solution.py:644
  36.7 4.3 %copy-start.1 = (s32[1,2]{1,0:T(1,128)S(1)}, s32[1,2]{1,0:T(1,128)}, u32[]{:S(2)}) copy-start(s32[1,2]{1,0:T(1,128)} %param.8) | copy-start | bytes 28
  36.7 4.3 %collective-permute-start.5 = (f32[4,2,72,128]{3,2,1,0:T(8,128)S(1)}, f32[4,2,72,128]{3,2,1,0:T(8,128)S(1)}, u32[]{:S(2)}, u32[]{:S(2)}) collective-permute-start(f32[4,2,72,128]{3,2,1,0:T(8,128)S(1)} %collective-permute-done.4.refs_5_), channel_id=1, source_target_pairs={{0,1},{1,0},{2,3},{3,2},{4,5},{5,4},{6,7},{7,6},{8,9},{9,8},{10,11... | collective-permute-start | bytes 884744 | tf_op jit(solution)/shard_map/ppermute | solution.py:585
  48.7 6.1 %collective-permute-start.8 = (f32[2,1024]{1,0:T(2,128)S(1)}, f32[2,1024]{1,0:T(2,128)S(1)}, u32[]{:S(2)}, u32[]{:S(2)}) collective-permute-start(f32[2,1024]{1,0:T(2,128)S(1)} %get-tuple-element.44), channel_id=1, source_target_pairs={{0,3},{1,2},{2,1},{3,0},{4,7},{5,6},{6,5},{7,4},{8,11},{9,10},{10,... | collective-permute-start | bytes 24584 | tf_op jit(solution)/shard_map/ppermute | solution.py:585
  49.4 5.4 %collective-permute-start.7 = (f32[2,1024]{1,0:T(2,128)S(1)}, f32[2,1024]{1,0:T(2,128)S(1)}, u32[]{:S(2)}, u32[]{:S(2)}) collective-permute-start(f32[2,1024]{1,0:T(2,128)S(1)} %get-tuple-element.44), channel_id=1, source_target_pairs={{0,2},{1,3},{2,0},{3,1},{4,6},{5,7},{6,4},{7,5},{8,10},{9,11},{10,... | collective-permute-start | bytes 24584 | tf_op jit(solution)/shard_map/ppermute | solution.py:585
  50.9 3.8 %collective-permute-start.6 = (f32[2,1024]{1,0:T(2,128)S(1)}, f32[2,1024]{1,0:T(2,128)S(1)}, u32[]{:S(2)}, u32[]{:S(2)}) collective-permute-start(f32[2,1024]{1,0:T(2,128)S(1)} %get-tuple-element.44), channel_id=1, source_target_pairs={{0,1},{1,0},{2,3},{3,2},{4,5},{5,4},{6,7},{7,6},{8,9},{9,8},{10,11... | collective-permute-start | bytes 24584 | tf_op jit(solution)/shard_map/ppermute | solution.py:585
  54.8 5.0 %collective-permute-start.9 = (f32[1,2,1024]{2,1,0:T(2,128)S(1)}, f32[1,2,1024]{2,1,0:T(2,128)S(1)}, u32[]{:S(2)}, u32[]{:S(2)}) collective-permute-start(f32[1,2,1024]{2,1,0:T(2,128)S(1)} %add_bitcast_fusion), channel_id=1, source_target_pairs={{0,4},{4,0},{8,12},{12,8},{16,20},{20,16},{24,28},{28,24},{1,5},{5... | collective-permute-start | bytes 24584 | tf_op jit(solution)/shard_map/ppermute | solution.py:585
  59.9 7.6 %collective-permute-start.12 = (f32[2,2,1024]{2,1,0:T(2,128)S(1)}, f32[2,2,1024]{2,1,0:T(2,128)S(1)}, u32[]{:S(2)}, u32[]{:S(2)}) collective-permute-start(f32[2,2,1024]{2,1,0:T(2,128)S(1)} %constant_dynamic-update-slice_fusion.refs_0_), channel_id=1, source_target_pairs={{0,24},{4,28},{8,16},{12,20},{16,8},{20,12},{24,0},{28,4},{1,25},{... | collective-permute-start | bytes 49160 | tf_op jit(solution)/shard_map/ppermute | solution.py:585
  63.5 4.6 %collective-permute-start.11 = (f32[2,2,1024]{2,1,0:T(2,128)S(1)}, f32[2,2,1024]{2,1,0:T(2,128)S(1)}, u32[]{:S(2)}, u32[]{:S(2)}) collective-permute-start(f32[2,2,1024]{2,1,0:T(2,128)S(1)} %constant_dynamic-update-slice_fusion.refs_0_), channel_id=1, source_target_pairs={{0,16},{4,20},{8,24},{12,28},{16,0},{20,4},{24,8},{28,12},{1,17},{... | collective-permute-start | bytes 49160 | tf_op jit(solution)/shard_map/ppermute | solution.py:585
  63.5 4.6 %collective-permute-start.10 = (f32[2,2,1024]{2,1,0:T(2,128)S(1)}, f32[2,2,1024]{2,1,0:T(2,128)S(1)}, u32[]{:S(2)}, u32[]{:S(2)}) collective-permute-start(f32[2,2,1024]{2,1,0:T(2,128)S(1)} %constant_dynamic-update-slice_fusion.refs_0_), channel_id=1, source_target_pairs={{0,8},{4,12},{8,0},{12,4},{16,24},{20,28},{24,16},{28,20},{1,9},{5... | collective-permute-start | bytes 49160 | tf_op jit(solution)/shard_map/ppermute | solution.py:585

commit v5 on v4

--- a/solution.py
+++ b/solution.py
@@ -212,7 +212,7 @@
 GROUP = 16
 
 
-def leaf_factor(mat):
+def leaf_factor(mat, jobs=()):
     groups, tiles = LANES // GROUP, GROUP // 8
     sub, lane = iota((8, LANES), 0), iota((8, LANES), 1)
     rows = [
@@ -227,6 +227,8 @@
         return jnp.broadcast_to(x[:, c : c + 1], (8, LANES))
 
     for g in range(groups):
+        for job in jobs[g::groups]:
+            job()
         base = GROUP * g
         own = (lane >= base) & (lane < base + GROUP)
         here = [[col_of(rows[g][v], base + c) for v in range(tiles)] for c in range(GROUP)]
@@ -278,48 +280,59 @@
     return jnp.concatenate([x for pair in rows for x in pair], axis=0)
 
 
+def deferred(ref, p):
+    n = ref.shape[0]
+    panels, k = n // LANES, p + 1
+    low, high = p * LANES, k * LANES
+    one, two, three = split(ref[low:high, :], 3)
+    right = jnp.concatenate([one, two, one, two, three, one], axis=0)
+    one, two, three = one[:, high:], two[:, high:], three[:, high:]
+    left = jnp.concatenate([one, one, two, two, one, three], axis=0)
+
+    def job(rows, lanes, fresh=False):
+        def run():
+            product = dot(left[:, : rows.stop - high], right[:, lanes], 0, 0)
+            if fresh:
+                ref[rows, lanes] = -product
+            else:
+                ref[rows, lanes] -= product
+
+        return run
+
+    below = slice(high, n)
+    jobs = [job(below, slice(low, high), fresh=True)]
+    for at in range(0, low, COLS):
+        jobs.append(job(below, slice(at, min(at + COLS, low))))
+    for b in range(k + 1, panels, 2):
+        end = min(b + 2, panels) * LANES
+        jobs.append(job(slice(high, end), slice(b * LANES, end)))
+    return jobs
+
+
 def eliminate(ref, k):
     n = ref.shape[0]
     panels = n // LANES
     low, high = k * LANES, (k + 1) * LANES
     row, col = iota((LANES, LANES), 0), iota((LANES, LANES), 1)
-    inverse = jnp.where(col <= row, leaf_factor(ref[low:high, low:high]), 0.0)
+    jobs = deferred(ref, k - 1) if k > 0 else ()
+    inverse = jnp.where(col <= row, leaf_factor(ref[low:high, low:high], jobs), 0.0)
+    if k % 2 == 1:
+        ref[low - LANES : low, low:high] = jnp.zeros((LANES, LANES), F32)
     one, two, three = split(inverse, 3)
     left = jnp.concatenate([one, one, two, two, one, three], axis=1)
-    parts = []
+    ref[low:high, low:high] = inverse
     if k + 1 < panels:
-        parts.append(ref[low:high, high:])
+        one, two, three = split(ref[low:high, high:], 3)
+        scaled = dot(left, jnp.concatenate([one, two, one, two, three, one], axis=0))
+        ref[low:high, high:] = scaled
+        coefs, beyond = split_six(scaled[:, :LANES], 0)
+        near = slice(high, high + LANES)
+        ref[near, near] -= dot(coefs, beyond, 0, 0)
     if k > 0:
-        parts.append(ref[low:high, :low])
-    if parts:
-        one, two, three = split(jnp.concatenate(parts, axis=1), 3)
-        scaled = dot(left, jnp.concatenate([one, two, one, two, three, one], axis=0))
-    ref[low:high, low:high] = inverse
-    if k > 0:
-        ref[low:high, :low] = scaled[:, n - high :]
-    if k + 1 == panels:
-        return
-    if k % 2 == 0:
-        ref[low:high, high : high + LANES] = jnp.zeros((LANES, LANES), F32)
-    rest = n - high
-    coefs, beyond = split_six(scaled[:, :rest], 0)
-    near = slice(high, high + LANES)
-    ref[near, near] -= dot(coefs[:, :LANES], beyond[:, :LANES], 0, 0)
-    for h in range(k + 1, panels):
-        at = slice(h * LANES, (h + 1) * LANES)
-        first = h + 1 if h == k + 1 else h
-        if first < panels:
-            mine = slice((h - k - 1) * LANES, (h - k) * LANES)
-            ref[at, first * LANES :] -= dot(
-                coefs[:, mine], beyond[:, first * LANES - high :], 0, 0
-            )
-    one, two, three = split(inverse, 3)
-    own = jnp.concatenate([one, two, one, two, three, one], axis=0)
-    ref[high:, low:high] = -dot(coefs, own, 0, 0)
-    if k > 0:
-        one, two, three = split(scaled[:, rest:], 3)
-        before = jnp.concatenate([one, two, one, two, three, one], axis=0)
-        ref[high:, :low] -= dot(coefs, before, 0, 0)
+        one, two, three = split(ref[low:high, :low], 3)
+        ref[low:high, :low] = dot(
+            left, jnp.concatenate([one, two, one, two, three, one], axis=0)
+        )
 
 
 def load_kernel(panels, me_ref, own_ref, core_ref, far_ref, far_core_ref, out_ref, sems):

time: 72.8 us -> 69.5 us (0.955)
  Pallas kernels: 52.7 us -> 49.5 us
    pallas_call x5, Pallas kernels: 22.9 us -> 21.1 us  [factor_next(): pl.pallas_call(functools.partial(panels_kernel, panels), in_specs=[pl.Blo...]
    pallas_call x1, Pallas kernels: 4.71 us -> 3.54 us  [factor_first(): pl.pallas_call(functools.partial(load_kernel, panels), in_specs=[pl.Block...]
  transfers between devices with their start and end apart: 13 -> 13, of which waited for: 2 -> 2; matrix products, arithmetic and copies ran while one was open for 2% -> 2% of each run, Pallas kernels for 56% -> 55%
where the time goes in v5:
time: 69.5 us; the launch traced here: 69.3 us
  Pallas kernels  49.5 us (71%)
  starting transfers between devices  15.5 us (22%)
  waiting for transfers between devices  1.94 us (3%)
  local copies, waits for them, and re-layouts  1.19 us (2%)
  between operations  1.01 us (1%)
    pallas_call x5, Pallas kernels, factor_next(): pl.pallas_call(functools.partial(panels_kernel, panels), in_specs=[pl.Blo...  21.1 us
    pallas_call x1, Pallas kernels, encode(): pl.pallas_call(encode_kernel, grid=(steps,), in_specs=[pl.BlockSpec(hidde...  13.2 us
    ppermute x12, starting transfers between devices, swap(): return lax.ppermute(x, axis, [(i, i ^ by) for i in range(size)])  12.1 us
    pallas_call x1, Pallas kernels, factor_next_pool(): pl.pallas_call(functools.partial(panels_pool_kernel, panels), in_specs=[w...  7.47 us
    pallas_call x1, Pallas kernels, whiten(): pl.pallas_call(whiten_kernel, in_specs=[pl.BlockSpec(memory_space=SMEM)]...  4.29 us
    pallas_call x1, Pallas kernels, factor_first(): pl.pallas_call(functools.partial(load_kernel, panels), in_specs=[pl.Block...  3.54 us
    ppermute x1, starting transfers between devices, body_fixed(): far_half = lax.ppermute(mine, 'seq', [(0, 2), (1, 3)])  3.49 us
    ppermute x12, waiting for transfers between devices, swap(): return lax.ppermute(x, axis, [(i, i ^ by) for i in range(size)])  1.94 us
  transfers between devices with their start and end apart: 13, of which 2 were waited for; matrix products, arithmetic and copies ran while one was open for 2% of the time, Pallas kernels for 55%

profile of v5, /device:TPU:0, one launch (start us, length us, event | category | flops | bytes accessed | tf_op | source)
XLA Modules:
  0.0 69.3 jit_solution(11300098024932989313)
XLA Ops:
  0.6 0.5 collective-permute-start.1
  1.1 0.0 copy-start
  1.1 1.2 %constant_dynamic-slice_fusion = f32[256,512]{1,0:T(8,128)S(1)} fusion(f32[256,1024]{1,0:T(8,128)} %refs_5_.1, s32[]{:T(128)S(6)} %select_n.7), kind=kLoop, calls=%fused_computation.4 | loop fusion | bytes 1048580 | tf_op jit(solution)/shard_map/dynamic_slice | solution.py:645
  2.3 2.6 %collective-permute-start = (f32[256,512]{1,0:T(8,128)S(1)}, f32[256,512]{1,0:T(8,128)S(1)}, u32[]{:S(2)}, u32[]{:S(2)}) collective-permute-start(f32[256,512]{1,0:T(8,128)S(1)} %constant_dynamic-slice_fusion), channel_id=1, source_target_pairs={{0,2},{1,3},{2,0},{3,1},{4,6},{5,7},{6,4},{7,5},{8,10},{9,11},{10,... | collective-permute-start | bytes 1572872 | tf_op jit(solution)/shard_map/ppermute | solution.py:598
  4.9 13.2 %encode.1 = (bf16[2,256,1024]{2,1,0:T(8,128)(2,1)}, f32[2,256,1024]{2,1,0:T(8,128)}, f32[2,256,1024]{2,1,0:T(8,128)}, f32[8,2,72,128]{3,2,1,0:T(8,128)}) custom-call(bf16[2,256,1024]{2,1,0:T(8,128)(2,1)} %bitcast.11, bf16[1024,1024]{1,0:T(8,128)(2,1)} %wq_ref.1, bf16[1024,1024]{1,0:T(8,128)(2,1)} %wk_ref.1, bf16[1024,1024]{1,0:T(8,128)(2,1)} %wv_ref.1), custom_call_target="tpu_custom_call" | custom-call | tf_op jit(solution)/shard_map/encode/pallas_call | solution.py:102
  18.1 0.0 collective-permute-done.far_ref
  18.1 0.0 collective-permute-done.1.core_ref
  18.1 0.3 collective-permute-start.3
  18.4 0.1 pad_add_fusion.at_ref
  18.5 0.0 copy-start.2
  18.5 0.3 collective-permute-start.2
  18.8 1.3 %collective-permute-done.3.far_core_ref = f32[256,512]{1,0:T(8,128)S(1)} collective-permute-done((f32[256,512]{1,0:T(8,128)S(1)}, f32[256,512]{1,0:T(8,128)S(1)}, u32[]{:S(2)}, u32[]{:S(2)}) %collective-permute-start.3) | collective-permute-done | bytes 524320 | tf_op jit(solution)/shard_map/ppermute | solution.py:598
  20.1 0.0 copy-done
  20.1 3.5 %factor_first.1.in_ref = f32[1024,1024]{1,0:T(8,128)S(1)} custom-call(s32[1]{0:T(128)} %bitcast.1.me_ref, f32[256,1024]{1,0:T(8,128)S(1)} %copy-done, f32[256,1024]{1,0:T(8,128)S(1)} %collective-permute-done.1.core_ref, f32[256,512]{1,0:T(8,128)S(1)} %collective-permute-done.far_ref, f32[256,512]{1,0:T(8,128)S(1)} %collective-permute-done.3.far_core_ref), custom_call_target="tpu_custom_call" | custom-call | flops 8000000000 | bytes 4194304 | tf_op jit(solution)/shard_map/factor_first/pallas_call | solution.py:447
  23.6 0.0 collective-permute-done.2.refs_7_
  23.7 0.0 copy-done.2
  23.7 3.5 %collective-permute-start.4 = (f32[4,2,72,128]{3,2,1,0:T(8,128)S(1)}, f32[4,2,72,128]{3,2,1,0:T(8,128)S(1)}, u32[]{:S(2)}, u32[]{:S(2)}) collective-permute-start(f32[4,2,72,128]{3,2,1,0:T(8,128)S(1)} %dynamic-slice_add_fusion), channel_id=1, source_target_pairs={{0,2},{1,3},{4,6},{5,7},{8,10},{9,11},{12,14},{13,15},{16,18},{17,... | collective-permute-start | bytes 884744 | tf_op jit(solution)/shard_map/ppermute | solution.py:657
  27.2 7.2 %factor_next.5.in_ref = f32[1024,1024]{1,0:T(8,128)S(1)} custom-call(f32[1024,1024]{1,0:T(8,128)S(1)} %factor_first.1.in_ref), custom_call_target="tpu_custom_call", output_to_operand_aliasing={{}: (0, {})} | custom-call | flops 8000000000 | bytes 4194304 | tf_op jit(solution)/shard_map/factor_next/pallas_call | solution.py:461
  34.4 0.0 copy-start.1
  34.4 0.0 collective-permute-done.4.refs_5_
  34.4 0.1 collective-permute-start.5
  34.5 3.6 %factor_next.6.in_ref = f32[1024,1024]{1,0:T(8,128)S(1)} custom-call(f32[1024,1024]{1,0:T(8,128)S(1)} %factor_next.5.in_ref), custom_call_target="tpu_custom_call", output_to_operand_aliasing={{}: (0, {})} | custom-call | flops 8000000000 | bytes 4194304 | tf_op jit(solution)/shard_map/factor_next/pallas_call | solution.py:461
  38.1 0.0 collective-permute-done.5.refs_6_
  38.1 0.0 copy-done.1
  38.1 7.5 %factor_next_pool.1 = (f32[1024,1024]{1,0:T(8,128)S(1)}, f32[2,1024]{1,0:T(2,128)S(1)}) custom-call(f32[1024,1024]{1,0:T(8,128)S(1)} %factor_next.6.in_ref, s32[2]{0:T(128)S(1)} %bitcast.10, s32[1]{0:T(128)} %bitcast.4.start_ref, s32[1]{0:T(128)} %bitcast.5.core_ref, bf16[2,256,1024]{2,1,0:T(8,128)(2,1)} %bitcast.12, ...), custom_call_target="tpu_custom_call", output_to_operand_aliasing={{0}: (0, {})} | custom-call | flops 8000000000 | bytes 12582912 | tf_op jit(solution)/shard_map/factor_next_pool/pallas_call | solution.py:430
  45.6 1.8 %collective-permute-start.8 = (f32[2,1024]{1,0:T(2,128)S(1)}, f32[2,1024]{1,0:T(2,128)S(1)}, u32[]{:S(2)}, u32[]{:S(2)}) collective-permute-start(f32[2,1024]{1,0:T(2,128)S(1)} %get-tuple-element.44), channel_id=1, source_target_pairs={{0,3},{1,2},{2,1},{3,0},{4,7},{5,6},{6,5},{7,4},{8,11},{9,10},{10,... | collective-permute-start | bytes 24584 | tf_op jit(solution)/shard_map/ppermute | solution.py:598
  47.4 0.5 collective-permute-start.7
  47.9 0.0 collective-permute-start.6
  47.9 3.5 %factor_next.7.in_ref = f32[1024,1024]{1,0:T(8,128)S(1)} custom-call(f32[1024,1024]{1,0:T(8,128)S(1)} %get-tuple-element.43.in_ref), custom_call_target="tpu_custom_call", output_to_operand_aliasing={{}: (0, {})} | custom-call | flops 8000000000 | bytes 4194304 | tf_op jit(solution)/shard_map/factor_next/pallas_call | solution.py:461
  51.3 0.0 collective-permute-done.8
  51.3 0.0 collective-permute-done.7
  51.4 0.0 collective-permute-done.6
  51.4 1.6 %collective-permute-start.9 = (f32[1,2,1024]{2,1,0:T(2,128)S(1)}, f32[1,2,1024]{2,1,0:T(2,128)S(1)}, u32[]{:S(2)}, u32[]{:S(2)}) collective-permute-start(f32[1,2,1024]{2,1,0:T(2,128)S(1)} %add_bitcast_fusion), channel_id=1, source_target_pairs={{0,4},{4,0},{8,12},{12,8},{16,20},{20,16},{24,28},{28,24},{1,5},{5... | collective-permute-start | bytes 24584 | tf_op jit(solution)/shard_map/ppermute | solution.py:598
  52.9 3.6 %factor_next.8.in_ref = f32[1024,1024]{1,0:T(8,128)S(1)} custom-call(f32[1024,1024]{1,0:T(8,128)S(1)} %factor_next.7.in_ref), custom_call_target="tpu_custom_call", output_to_operand_aliasing={{}: (0, {})} | custom-call | flops 8000000000 | bytes 4194304 | tf_op jit(solution)/shard_map/factor_next/pallas_call | solution.py:461
  56.5 0.0 collective-permute-done.9
  56.6 3.7 %collective-permute-start.12 = (f32[2,2,1024]{2,1,0:T(2,128)S(1)}, f32[2,2,1024]{2,1,0:T(2,128)S(1)}, u32[]{:S(2)}, u32[]{:S(2)}) collective-permute-start(f32[2,2,1024]{2,1,0:T(2,128)S(1)} %constant_dynamic-update-slice_fusion.refs_0_), channel_id=1, source_target_pairs={{0,24},{4,28},{8,16},{12,20},{16,8},{20,12},{24,0},{28,4},{1,25},{... | collective-permute-start | bytes 49160 | tf_op jit(solution)/shard_map/ppermute | solution.py:598
  60.2 0.0 collective-permute-start.11
  60.2 0.8 %collective-permute-start.10 = (f32[2,2,1024]{2,1,0:T(2,128)S(1)}, f32[2,2,1024]{2,1,0:T(2,128)S(1)}, u32[]{:S(2)}, u32[]{:S(2)}) collective-permute-start(f32[2,2,1024]{2,1,0:T(2,128)S(1)} %constant_dynamic-update-slice_fusion.refs_0_), channel_id=1, source_target_pairs={{0,8},{4,12},{8,0},{12,4},{16,24},{20,28},{24,16},{28,20},{1,9},{5... | collective-permute-start | bytes 49160 | tf_op jit(solution)/shard_map/ppermute | solution.py:598
  61.0 3.2 %factor_next.9.refs_4_ = f32[1024,1024]{1,0:T(8,128)S(1)} custom-call(f32[1024,1024]{1,0:T(8,128)S(1)} %factor_next.8.in_ref), custom_call_target="tpu_custom_call", output_to_operand_aliasing={{}: (0, {})} | custom-call | flops 8000000000 | bytes 4194304 | tf_op jit(solution)/shard_map/factor_next/pallas_call | solution.py:461
  64.3 0.0 collective-permute-done.12.refs_3_
  64.3 0.6 collective-permute-done.11.refs_2_
  64.9 0.0 collective-permute-done.10.refs_1_
  64.9 4.3 %whiten.1 = (f32[2,1024]{1,0:T(2,128)}, f32[256,1024]{1,0:T(8,128)}, f32[1,1]{1,0:T(1,128)}) custom-call(s32[2]{0:T(128)S(1)} %pad_add_fusion.at_ref, f32[2,2,1024]{2,1,0:T(2,128)S(1)} %constant_dynamic-update-slice_fusion.refs_0_, f32[2,2,1024]{2,1,0:T(2,128)S(1)} %collective-permute-done.10.refs_1_, f32[2,2,1024]{2,1,0:T(2,128)S(1)} %collective-permute-done.11.refs_2_, ...), custom_call_target="tpu_custom_call" | custom-call | tf_op jit(solution)/shard_map/whiten/pallas_call | solution.py:571
  (4 shorter events, 0.1 us)
Async XLA Ops:
  0.6 17.5 %collective-permute-start.1 = (f32[256,1024]{1,0:T(8,128)}, f32[256,1024]{1,0:T(8,128)S(1)}, u32[]{:S(2)}, u32[]{:S(2)}) collective-permute-start(f32[256,1024]{1,0:T(8,128)} %refs_5_.1), channel_id=1, source_target_pairs={{0,1},{1,0},{2,3},{3,2},{4,5},{5,4},{6,7},{7,6},{8,9},{9,8},{10,11... | collective-permute-start | bytes 3145736 | tf_op jit(solution)/shard_map/ppermute | solution.py:598
  1.1 19.0 %copy-start = (f32[256,1024]{1,0:T(8,128)S(1)}, f32[256,1024]{1,0:T(8,128)}, u32[]{:S(2)}) copy-start(f32[256,1024]{1,0:T(8,128)} %refs_5_.1) | copy-start | bytes 3145732
  2.3 15.8 %collective-permute-start = (f32[256,512]{1,0:T(8,128)S(1)}, f32[256,512]{1,0:T(8,128)S(1)}, u32[]{:S(2)}, u32[]{:S(2)}) collective-permute-start(f32[256,512]{1,0:T(8,128)S(1)} %constant_dynamic-slice_fusion), channel_id=1, source_target_pairs={{0,2},{1,3},{2,0},{3,1},{4,6},{5,7},{6,4},{7,5},{8,10},{9,11},{10,... | collective-permute-start | bytes 1572872 | tf_op jit(solution)/shard_map/ppermute | solution.py:598
  18.1 2.0 %collective-permute-start.3 = (f32[256,512]{1,0:T(8,128)S(1)}, f32[256,512]{1,0:T(8,128)S(1)}, u32[]{:S(2)}, u32[]{:S(2)}) collective-permute-start(f32[256,512]{1,0:T(8,128)S(1)} %collective-permute-done.far_ref), channel_id=1, source_target_pairs={{0,1},{1,0},{2,3},{3,2},{4,5},{5,4},{6,7},{7,6},{8,9},{9,8},{10,11... | collective-permute-start | bytes 1572872 | tf_op jit(solution)/shard_map/ppermute | solution.py:598
  18.5 5.2 %copy-start.2 = (f32[8,2,72,128]{3,2,1,0:T(8,128)S(1)}, f32[8,2,72,128]{3,2,1,0:T(8,128)}, u32[]{:S(2)}) copy-start(f32[8,2,72,128]{3,2,1,0:T(8,128)} %get-tuple-element.30) | copy-start | bytes 1769476
  18.5 5.2 %collective-permute-start.2 = (f32[8,2,72,128]{3,2,1,0:T(8,128)}, f32[8,2,72,128]{3,2,1,0:T(8,128)S(1)}, u32[]{:S(2)}, u32[]{:S(2)}) collective-permute-start(f32[8,2,72,128]{3,2,1,0:T(8,128)} %get-tuple-element.30), channel_id=1, source_target_pairs={{0,1},{1,0},{2,3},{3,2},{4,5},{5,4},{6,7},{7,6},{8,9},{9,8},{10,11... | collective-permute-start | bytes 1769480 | tf_op jit(solution)/shard_map/ppermute | solution.py:598
  23.7 10.7 %collective-permute-start.4 = (f32[4,2,72,128]{3,2,1,0:T(8,128)S(1)}, f32[4,2,72,128]{3,2,1,0:T(8,128)S(1)}, u32[]{:S(2)}, u32[]{:S(2)}) collective-permute-start(f32[4,2,72,128]{3,2,1,0:T(8,128)S(1)} %dynamic-slice_add_fusion), channel_id=1, source_target_pairs={{0,2},{1,3},{4,6},{5,7},{8,10},{9,11},{12,14},{13,15},{16,18},{17,... | collective-permute-start | bytes 884744 | tf_op jit(solution)/shard_map/ppermute | solution.py:657
  34.4 3.7 %copy-start.1 = (s32[1,2]{1,0:T(1,128)S(1)}, s32[1,2]{1,0:T(1,128)}, u32[]{:S(2)}) copy-start(s32[1,2]{1,0:T(1,128)} %param.8) | copy-start | bytes 28
  34.4 3.7 %collective-permute-start.5 = (f32[4,2,72,128]{3,2,1,0:T(8,128)S(1)}, f32[4,2,72,128]{3,2,1,0:T(8,128)S(1)}, u32[]{:S(2)}, u32[]{:S(2)}) collective-permute-start(f32[4,2,72,128]{3,2,1,0:T(8,128)S(1)} %collective-permute-done.4.refs_5_), channel_id=1, source_target_pairs={{0,1},{1,0},{2,3},{3,2},{4,5},{5,4},{6,7},{7,6},{8,9},{9,8},{10,11... | collective-permute-start | bytes 884744 | tf_op jit(solution)/shard_map/ppermute | solution.py:598
  45.6 5.7 %collective-permute-start.8 = (f32[2,1024]{1,0:T(2,128)S(1)}, f32[2,1024]{1,0:T(2,128)S(1)}, u32[]{:S(2)}, u32[]{:S(2)}) collective-permute-start(f32[2,1024]{1,0:T(2,128)S(1)} %get-tuple-element.44), channel_id=1, source_target_pairs={{0,3},{1,2},{2,1},{3,0},{4,7},{5,6},{6,5},{7,4},{8,11},{9,10},{10,... | collective-permute-start | bytes 24584 | tf_op jit(solution)/shard_map/ppermute | solution.py:598
  47.4 4.0 %collective-permute-start.7 = (f32[2,1024]{1,0:T(2,128)S(1)}, f32[2,1024]{1,0:T(2,128)S(1)}, u32[]{:S(2)}, u32[]{:S(2)}) collective-permute-start(f32[2,1024]{1,0:T(2,128)S(1)} %get-tuple-element.44), channel_id=1, source_target_pairs={{0,2},{1,3},{2,0},{3,1},{4,6},{5,7},{6,4},{7,5},{8,10},{9,11},{10,... | collective-permute-start | bytes 24584 | tf_op jit(solution)/shard_map/ppermute | solution.py:598
  47.9 3.5 %collective-permute-start.6 = (f32[2,1024]{1,0:T(2,128)S(1)}, f32[2,1024]{1,0:T(2,128)S(1)}, u32[]{:S(2)}, u32[]{:S(2)}) collective-permute-start(f32[2,1024]{1,0:T(2,128)S(1)} %get-tuple-element.44), channel_id=1, source_target_pairs={{0,1},{1,0},{2,3},{3,2},{4,5},{5,4},{6,7},{7,6},{8,9},{9,8},{10,11... | collective-permute-start | bytes 24584 | tf_op jit(solution)/shard_map/ppermute | solution.py:598
  51.4 5.1 %collective-permute-start.9 = (f32[1,2,1024]{2,1,0:T(2,128)S(1)}, f32[1,2,1024]{2,1,0:T(2,128)S(1)}, u32[]{:S(2)}, u32[]{:S(2)}) collective-permute-start(f32[1,2,1024]{2,1,0:T(2,128)S(1)} %add_bitcast_fusion), channel_id=1, source_target_pairs={{0,4},{4,0},{8,12},{12,8},{16,20},{20,16},{24,28},{28,24},{1,5},{5... | collective-permute-start | bytes 24584 | tf_op jit(solution)/shard_map/ppermute | solution.py:598
  56.6 7.7 %collective-permute-start.12 = (f32[2,2,1024]{2,1,0:T(2,128)S(1)}, f32[2,2,1024]{2,1,0:T(2,128)S(1)}, u32[]{:S(2)}, u32[]{:S(2)}) collective-permute-start(f32[2,2,1024]{2,1,0:T(2,128)S(1)} %constant_dynamic-update-slice_fusion.refs_0_), channel_id=1, source_target_pairs={{0,24},{4,28},{8,16},{12,20},{16,8},{20,12},{24,0},{28,4},{1,25},{... | collective-permute-start | bytes 49160 | tf_op jit(solution)/shard_map/ppermute | solution.py:598
  60.2 4.6 %collective-permute-start.11 = (f32[2,2,1024]{2,1,0:T(2,128)S(1)}, f32[2,2,1024]{2,1,0:T(2,128)S(1)}, u32[]{:S(2)}, u32[]{:S(2)}) collective-permute-start(f32[2,2,1024]{2,1,0:T(2,128)S(1)} %constant_dynamic-update-slice_fusion.refs_0_), channel_id=1, source_target_pairs={{0,16},{4,20},{8,24},{12,28},{16,0},{20,4},{24,8},{28,12},{1,17},{... | collective-permute-start | bytes 49160 | tf_op jit(solution)/shard_map/ppermute | solution.py:598
  60.2 4.6 %collective-permute-start.10 = (f32[2,2,1024]{2,1,0:T(2,128)S(1)}, f32[2,2,1024]{2,1,0:T(2,128)S(1)}, u32[]{:S(2)}, u32[]{:S(2)}) collective-permute-start(f32[2,2,1024]{2,1,0:T(2,128)S(1)} %constant_dynamic-update-slice_fusion.refs_0_), channel_id=1, source_target_pairs={{0,8},{4,12},{8,0},{12,4},{16,24},{20,28},{24,16},{28,20},{1,9},{5... | collective-permute-start | bytes 49160 | tf_op jit(solution)/shard_map/ppermute | solution.py:598

commit v6 on v5

--- a/solution.py
+++ b/solution.py
@@ -57,7 +57,52 @@
     return lax.broadcasted_iota(jnp.int32, shape, dim)
 
 
-def encode_kernel(h_ref, wq_ref, wk_ref, wv_ref, fq_ref, num_ref, den_ref, state_ref):
+def encode_kernel(*refs):
+    (hidden_ref, *weight_refs), results = refs[:4], refs[4:8]
+    (h_ref, w_ref, *held), (in_sems, out_sems) = refs[8:14], refs[14:]
+    steps = w_ref.shape[2] // COLS
+    pairs = COLS // LANES
+
+    def window(j):
+        return pl.ds(pl.multiple_of(j * COLS, COLS), COLS)
+
+    def arriving(i, j):
+        return pltpu.make_async_copy(
+            weight_refs[i].at[:, window(j)], w_ref.at[i, :, window(j)], in_sems.at[i, j]
+        )
+
+    def blocks(refs, j):
+        *arrays, state_ref = refs
+        return [x.at[:, :, window(j)] for x in arrays] + [state_ref.at[pl.ds(j * pairs, pairs)]]
+
+    def leaving(j):
+        return [
+            pltpu.make_async_copy(source, target, out_sems.at[i, j])
+            for i, (source, target) in enumerate(zip(blocks(held, j), blocks(results, j)))
+        ]
+
+    first = pltpu.make_async_copy(hidden_ref, h_ref, in_sems.at[3, 0])
+    first.start()
+    for j in range(steps):
+        for i in range(3):
+            arriving(i, j).start()
+    first.wait()
+
+    def run(j, carried):
+        for i in range(3):
+            arriving(i, j).wait()
+        encode_columns(h_ref, *[w_ref.at[i, :, window(j)] for i in range(3)], *blocks(held, j))
+        for copy in leaving(j):
+            copy.start()
+        return carried
+
+    lax.fori_loop(0, steps, run, 0)
+    for j in range(steps):
+        for copy in leaving(j):
+            copy.wait()
+
+
+def encode_columns(h_ref, wq_ref, wk_ref, wv_ref, fq_ref, num_ref, den_ref, state_ref):
     count, span = h_ref.shape[0], h_ref.shape[1]
     rows = h_ref[...].reshape(count * span, h_ref.shape[2])
     fq = feature(dot(rows, wq_ref[...])).astype(BF16)
@@ -94,28 +139,19 @@
 def encode(hidden, w_query, w_key, w_value):
     count, span, width = hidden.shape
     steps = width // COLS
-    weight = pl.BlockSpec((width, COLS), lambda j: (0, j))
-    block = pl.BlockSpec((count, span, COLS), lambda j: (0, 0, j))
-    pairs = COLS // LANES
     shape = (count, span, width)
     state_shape = (width // LANES, count, HEAD_DIM + 8, LANES)
+    anywhere = pl.BlockSpec(memory_space=pl.ANY)
+    results = [(shape, BF16), (shape, F32), (shape, F32), (state_shape, F32)]
     return pl.pallas_call(
         encode_kernel,
-        grid=(steps,),
-        in_specs=[pl.BlockSpec(hidden.shape, lambda j: (0, 0, 0)), weight, weight, weight],
-        out_specs=[
-            block,
-            block,
-            block,
-            pl.BlockSpec((pairs,) + state_shape[1:], lambda j: (j, 0, 0, 0)),
-        ],
-        out_shape=[
-            pltpu.HBM(shape, BF16),
-            pltpu.HBM(shape, F32),
-            pltpu.HBM(shape, F32),
-            pltpu.HBM(state_shape, F32),
-        ],
-        compiler_params=params(14),
+        in_specs=[anywhere] * 4,
+        out_specs=[anywhere] * 4,
+        out_shape=[pltpu.HBM(*x) for x in results],
+        scratch_shapes=[VMEM(shape, BF16), VMEM((3, width, width), BF16)]
+        + [VMEM(*x) for x in results]
+        + [pltpu.SemaphoreType.DMA((4, steps)), pltpu.SemaphoreType.DMA((4, steps))],
+        compiler_params=params(24),
         name="encode",
     )(hbm(hidden), hbm(w_query), hbm(w_key), hbm(w_value))
 
@@ -399,8 +435,8 @@
     steps = wo_ref.shape[0] // COLS
     pairs = COLS // LANES
 
-    def run(step, carried):
-        cols = pl.ds(pl.multiple_of(step * COLS, COLS), COLS)
+    for step in range(steps):
+        cols = slice(step * COLS, (step + 1) * COLS)
         pool_columns(
             step,
             steps,
@@ -410,13 +446,10 @@
             fq_ref.at[:, :, cols],
             num_ref.at[:, :, cols],
             den_ref.at[:, :, cols],
-            prior_ref.at[pl.ds(step * pairs, pairs)],
+            prior_ref.at[step * pairs : (step + 1) * pairs],
             wo_ref.at[cols, :],
             out_ref,
         )
-        return carried
-
-    lax.fori_loop(0, steps, run, 0)
 
 
 def factor_next_pool(

time: 69.5 us -> 68.7 us (0.988)
    pallas_call x1, Pallas kernels: 7.47 us -> 6.71 us  [factor_next_pool(): pl.pallas_call(functools.partial(panels_pool_kernel, panels), in_specs=[w...]
where the time goes in v6:
time: 68.7 us; the launch traced here: 68.6 us
  Pallas kernels  49 us (71%)
  starting transfers between devices  15.3 us (22%)
  waiting for transfers between devices  1.93 us (3%)
  local copies, waits for them, and re-layouts  1.19 us (2%)
  between operations  1.02 us (1%)
    pallas_call x5, Pallas kernels, factor_next(): pl.pallas_call(functools.partial(panels_kernel, panels), in_specs=[pl.Blo...  21.1 us
    pallas_call x1, Pallas kernels, encode(): pl.pallas_call(encode_kernel, in_specs=[anywhere] * 4, out_specs=[anywher...  13.4 us
    ppermute x12, starting transfers between devices, swap(): return lax.ppermute(x, axis, [(i, i ^ by) for i in range(size)])  12 us
    pallas_call x1, Pallas kernels, factor_next_pool(): pl.pallas_call(functools.partial(panels_pool_kernel, panels), in_specs=[w...  6.71 us
    pallas_call x1, Pallas kernels, whiten(): pl.pallas_call(whiten_kernel, in_specs=[pl.BlockSpec(memory_space=SMEM)]...  4.29 us
    pallas_call x1, Pallas kernels, factor_first(): pl.pallas_call(functools.partial(load_kernel, panels), in_specs=[pl.Block...  3.54 us
    ppermute x1, starting transfers between devices, body_fixed(): far_half = lax.ppermute(mine, 'seq', [(0, 2), (1, 3)])  3.29 us
    ppermute x12, waiting for transfers between devices, swap(): return lax.ppermute(x, axis, [(i, i ^ by) for i in range(size)])  1.93 us
  transfers between devices with their start and end apart: 13, of which 2 were waited for; matrix products, arithmetic and copies ran while one was open for 2% of the time, Pallas kernels for 55%

profile of v6, /device:TPU:0, one launch (start us, length us, event | category | flops | bytes accessed | tf_op | source)
XLA Modules:
  0.0 68.6 jit_solution(12487130105648832648)
XLA Ops:
  0.6 0.5 collective-permute-start.1
  1.1 0.0 copy-start
  1.1 1.2 %constant_dynamic-slice_fusion = f32[256,512]{1,0:T(8,128)S(1)} fusion(f32[256,1024]{1,0:T(8,128)} %refs_5_.1, s32[]{:T(128)S(6)} %select_n.7), kind=kLoop, calls=%fused_computation.4 | loop fusion | bytes 1048580 | tf_op jit(solution)/shard_map/dynamic_slice | solution.py:678
  2.3 2.6 %collective-permute-start = (f32[256,512]{1,0:T(8,128)S(1)}, f32[256,512]{1,0:T(8,128)S(1)}, u32[]{:S(2)}, u32[]{:S(2)}) collective-permute-start(f32[256,512]{1,0:T(8,128)S(1)} %constant_dynamic-slice_fusion), channel_id=1, source_target_pairs={{0,2},{1,3},{2,0},{3,1},{4,6},{5,7},{6,4},{7,5},{8,10},{9,11},{10,... | collective-permute-start | bytes 1572872 | tf_op jit(solution)/shard_map/ppermute | solution.py:631
  4.9 13.4 %encode.1 = (bf16[2,256,1024]{2,1,0:T(8,128)(2,1)}, f32[2,256,1024]{2,1,0:T(8,128)}, f32[2,256,1024]{2,1,0:T(8,128)}, f32[8,2,72,128]{3,2,1,0:T(8,128)}) custom-call(bf16[2,256,1024]{2,1,0:T(8,128)(2,1)} %bitcast.11, bf16[1024,1024]{1,0:T(8,128)(2,1)} %refs_1_.1, bf16[1024,1024]{1,0:T(8,128)(2,1)} %refs_2_.1, bf16[1024,1024]{1,0:T(8,128)(2,1)} %refs_3_.1), custom_call_target="tpu_custom_call" | custom-call | tf_op jit(solution)/shard_map/encode/pallas_call | solution.py:146
  18.3 0.0 collective-permute-done.far_ref
  18.3 0.0 collective-permute-done.1.core_ref
  18.3 0.3 collective-permute-start.3
  18.6 0.1 pad_add_fusion.at_ref
  18.7 0.0 copy-start.2
  18.7 0.3 collective-permute-start.2
  19.0 1.3 %collective-permute-done.3.far_core_ref = f32[256,512]{1,0:T(8,128)S(1)} collective-permute-done((f32[256,512]{1,0:T(8,128)S(1)}, f32[256,512]{1,0:T(8,128)S(1)}, u32[]{:S(2)}, u32[]{:S(2)}) %collective-permute-start.3) | collective-permute-done | bytes 524320 | tf_op jit(solution)/shard_map/ppermute | solution.py:631
  20.3 0.0 copy-done
  20.3 3.5 %factor_first.1.in_ref = f32[1024,1024]{1,0:T(8,128)S(1)} custom-call(s32[1]{0:T(128)} %bitcast.1.me_ref, f32[256,1024]{1,0:T(8,128)S(1)} %copy-done, f32[256,1024]{1,0:T(8,128)S(1)} %collective-permute-done.1.core_ref, f32[256,512]{1,0:T(8,128)S(1)} %collective-permute-done.far_ref, f32[256,512]{1,0:T(8,128)S(1)} %collective-permute-done.3.far_core_ref), custom_call_target="tpu_custom_call" | custom-call | flops 8000000000 | bytes 4194304 | tf_op jit(solution)/shard_map/factor_first/pallas_call | solution.py:480
  23.9 0.0 collective-permute-done.2.refs_7_
  23.9 0.0 copy-done.2
  23.9 3.3 %collective-permute-start.4 = (f32[4,2,72,128]{3,2,1,0:T(8,128)S(1)}, f32[4,2,72,128]{3,2,1,0:T(8,128)S(1)}, u32[]{:S(2)}, u32[]{:S(2)}) collective-permute-start(f32[4,2,72,128]{3,2,1,0:T(8,128)S(1)} %dynamic-slice_add_fusion), channel_id=1, source_target_pairs={{0,2},{1,3},{4,6},{5,7},{8,10},{9,11},{12,14},{13,15},{16,18},{17,... | collective-permute-start | bytes 884744 | tf_op jit(solution)/shard_map/ppermute | solution.py:690
  27.2 7.2 %factor_next.5.in_ref = f32[1024,1024]{1,0:T(8,128)S(1)} custom-call(f32[1024,1024]{1,0:T(8,128)S(1)} %factor_first.1.in_ref), custom_call_target="tpu_custom_call", output_to_operand_aliasing={{}: (0, {})} | custom-call | flops 8000000000 | bytes 4194304 | tf_op jit(solution)/shard_map/factor_next/pallas_call | solution.py:494
  34.4 0.0 copy-start.1
  34.4 0.0 collective-permute-done.4.refs_5_
  34.4 0.1 collective-permute-start.5
  34.5 3.6 %factor_next.6.in_ref = f32[1024,1024]{1,0:T(8,128)S(1)} custom-call(f32[1024,1024]{1,0:T(8,128)S(1)} %factor_next.5.in_ref), custom_call_target="tpu_custom_call", output_to_operand_aliasing={{}: (0, {})} | custom-call | flops 8000000000 | bytes 4194304 | tf_op jit(solution)/shard_map/factor_next/pallas_call | solution.py:494
  38.1 0.0 collective-permute-done.5.refs_6_
  38.1 0.0 copy-done.1
  38.1 6.7 %factor_next_pool.1 = (f32[1024,1024]{1,0:T(8,128)S(1)}, f32[2,1024]{1,0:T(2,128)S(1)}) custom-call(f32[1024,1024]{1,0:T(8,128)S(1)} %factor_next.6.in_ref, s32[2]{0:T(128)S(1)} %bitcast.10, s32[1]{0:T(128)} %bitcast.4.start_ref, s32[1]{0:T(128)} %bitcast.5.core_ref, bf16[2,256,1024]{2,1,0:T(8,128)(2,1)} %bitcast.12, ...), custom_call_target="tpu_custom_call", output_to_operand_aliasing={{0}: (0, {})} | custom-call | flops 8000000000 | bytes 12582912 | tf_op jit(solution)/shard_map/factor_next_pool/pallas_call | solution.py:463
  44.8 1.8 %collective-permute-start.8 = (f32[2,1024]{1,0:T(2,128)S(1)}, f32[2,1024]{1,0:T(2,128)S(1)}, u32[]{:S(2)}, u32[]{:S(2)}) collective-permute-start(f32[2,1024]{1,0:T(2,128)S(1)} %get-tuple-element.44), channel_id=1, source_target_pairs={{0,3},{1,2},{2,1},{3,0},{4,7},{5,6},{6,5},{7,4},{8,11},{9,10},{10,... | collective-permute-start | bytes 24584 | tf_op jit(solution)/shard_map/ppermute | solution.py:631
  46.6 0.5 collective-permute-start.7
  47.1 0.0 collective-permute-start.6
  47.1 3.5 %factor_next.7.in_ref = f32[1024,1024]{1,0:T(8,128)S(1)} custom-call(f32[1024,1024]{1,0:T(8,128)S(1)} %get-tuple-element.43.in_ref), custom_call_target="tpu_custom_call", output_to_operand_aliasing={{}: (0, {})} | custom-call | flops 8000000000 | bytes 4194304 | tf_op jit(solution)/shard_map/factor_next/pallas_call | solution.py:494
  50.6 0.0 collective-permute-done.8
  50.6 0.0 collective-permute-done.7
  50.6 0.0 collective-permute-done.6
  50.6 1.6 %collective-permute-start.9 = (f32[1,2,1024]{2,1,0:T(2,128)S(1)}, f32[1,2,1024]{2,1,0:T(2,128)S(1)}, u32[]{:S(2)}, u32[]{:S(2)}) collective-permute-start(f32[1,2,1024]{2,1,0:T(2,128)S(1)} %add_bitcast_fusion), channel_id=1, source_target_pairs={{0,4},{4,0},{8,12},{12,8},{16,20},{20,16},{24,28},{28,24},{1,5},{5... | collective-permute-start | bytes 24584 | tf_op jit(solution)/shard_map/ppermute | solution.py:631
  52.2 3.6 %factor_next.8.in_ref = f32[1024,1024]{1,0:T(8,128)S(1)} custom-call(f32[1024,1024]{1,0:T(8,128)S(1)} %factor_next.7.in_ref), custom_call_target="tpu_custom_call", output_to_operand_aliasing={{}: (0, {})} | custom-call | flops 8000000000 | bytes 4194304 | tf_op jit(solution)/shard_map/factor_next/pallas_call | solution.py:494
  55.8 0.0 collective-permute-done.9
  55.8 3.7 %collective-permute-start.12 = (f32[2,2,1024]{2,1,0:T(2,128)S(1)}, f32[2,2,1024]{2,1,0:T(2,128)S(1)}, u32[]{:S(2)}, u32[]{:S(2)}) collective-permute-start(f32[2,2,1024]{2,1,0:T(2,128)S(1)} %constant_dynamic-update-slice_fusion.refs_0_), channel_id=1, source_target_pairs={{0,24},{4,28},{8,16},{12,20},{16,8},{20,12},{24,0},{28,4},{1,25},{... | collective-permute-start | bytes 49160 | tf_op jit(solution)/shard_map/ppermute | solution.py:631
  59.5 0.0 collective-permute-start.11
  59.5 0.8 %collective-permute-start.10 = (f32[2,2,1024]{2,1,0:T(2,128)S(1)}, f32[2,2,1024]{2,1,0:T(2,128)S(1)}, u32[]{:S(2)}, u32[]{:S(2)}) collective-permute-start(f32[2,2,1024]{2,1,0:T(2,128)S(1)} %constant_dynamic-update-slice_fusion.refs_0_), channel_id=1, source_target_pairs={{0,8},{4,12},{8,0},{12,4},{16,24},{20,28},{24,16},{28,20},{1,9},{5... | collective-permute-start | bytes 49160 | tf_op jit(solution)/shard_map/ppermute | solution.py:631
  60.2 3.3 %factor_next.9.refs_4_ = f32[1024,1024]{1,0:T(8,128)S(1)} custom-call(f32[1024,1024]{1,0:T(8,128)S(1)} %factor_next.8.in_ref), custom_call_target="tpu_custom_call", output_to_operand_aliasing={{}: (0, {})} | custom-call | flops 8000000000 | bytes 4194304 | tf_op jit(solution)/shard_map/factor_next/pallas_call | solution.py:494
  63.5 0.0 collective-permute-done.12.refs_3_
  63.5 0.6 collective-permute-done.11.refs_2_
  64.1 0.0 collective-permute-done.10.refs_1_
  64.1 4.3 %whiten.1 = (f32[2,1024]{1,0:T(2,128)}, f32[256,1024]{1,0:T(8,128)}, f32[1,1]{1,0:T(1,128)}) custom-call(s32[2]{0:T(128)S(1)} %pad_add_fusion.at_ref, f32[2,2,1024]{2,1,0:T(2,128)S(1)} %constant_dynamic-update-slice_fusion.refs_0_, f32[2,2,1024]{2,1,0:T(2,128)S(1)} %collective-permute-done.10.refs_1_, f32[2,2,1024]{2,1,0:T(2,128)S(1)} %collective-permute-done.11.refs_2_, ...), custom_call_target="tpu_custom_call" | custom-call | tf_op jit(solution)/shard_map/whiten/pallas_call | solution.py:604
  (4 shorter events, 0.1 us)
Async XLA Ops:
  0.6 17.7 %collective-permute-start.1 = (f32[256,1024]{1,0:T(8,128)}, f32[256,1024]{1,0:T(8,128)S(1)}, u32[]{:S(2)}, u32[]{:S(2)}) collective-permute-start(f32[256,1024]{1,0:T(8,128)} %refs_5_.1), channel_id=1, source_target_pairs={{0,1},{1,0},{2,3},{3,2},{4,5},{5,4},{6,7},{7,6},{8,9},{9,8},{10,11... | collective-permute-start | bytes 3145736 | tf_op jit(solution)/shard_map/ppermute | solution.py:631
  1.1 19.2 %copy-start = (f32[256,1024]{1,0:T(8,128)S(1)}, f32[256,1024]{1,0:T(8,128)}, u32[]{:S(2)}) copy-start(f32[256,1024]{1,0:T(8,128)} %refs_5_.1) | copy-start | bytes 3145732
  2.3 16.0 %collective-permute-start = (f32[256,512]{1,0:T(8,128)S(1)}, f32[256,512]{1,0:T(8,128)S(1)}, u32[]{:S(2)}, u32[]{:S(2)}) collective-permute-start(f32[256,512]{1,0:T(8,128)S(1)} %constant_dynamic-slice_fusion), channel_id=1, source_target_pairs={{0,2},{1,3},{2,0},{3,1},{4,6},{5,7},{6,4},{7,5},{8,10},{9,11},{10,... | collective-permute-start | bytes 1572872 | tf_op jit(solution)/shard_map/ppermute | solution.py:631
  18.3 2.0 %collective-permute-start.3 = (f32[256,512]{1,0:T(8,128)S(1)}, f32[256,512]{1,0:T(8,128)S(1)}, u32[]{:S(2)}, u32[]{:S(2)}) collective-permute-start(f32[256,512]{1,0:T(8,128)S(1)} %collective-permute-done.far_ref), channel_id=1, source_target_pairs={{0,1},{1,0},{2,3},{3,2},{4,5},{5,4},{6,7},{7,6},{8,9},{9,8},{10,11... | collective-permute-start | bytes 1572872 | tf_op jit(solution)/shard_map/ppermute | solution.py:631
  18.7 5.2 %copy-start.2 = (f32[8,2,72,128]{3,2,1,0:T(8,128)S(1)}, f32[8,2,72,128]{3,2,1,0:T(8,128)}, u32[]{:S(2)}) copy-start(f32[8,2,72,128]{3,2,1,0:T(8,128)} %get-tuple-element.30) | copy-start | bytes 1769476
  18.7 5.2 %collective-permute-start.2 = (f32[8,2,72,128]{3,2,1,0:T(8,128)}, f32[8,2,72,128]{3,2,1,0:T(8,128)S(1)}, u32[]{:S(2)}, u32[]{:S(2)}) collective-permute-start(f32[8,2,72,128]{3,2,1,0:T(8,128)} %get-tuple-element.30), channel_id=1, source_target_pairs={{0,1},{1,0},{2,3},{3,2},{4,5},{5,4},{6,7},{7,6},{8,9},{9,8},{10,11... | collective-permute-start | bytes 1769480 | tf_op jit(solution)/shard_map/ppermute | solution.py:631
  23.9 10.5 %collective-permute-start.4 = (f32[4,2,72,128]{3,2,1,0:T(8,128)S(1)}, f32[4,2,72,128]{3,2,1,0:T(8,128)S(1)}, u32[]{:S(2)}, u32[]{:S(2)}) collective-permute-start(f32[4,2,72,128]{3,2,1,0:T(8,128)S(1)} %dynamic-slice_add_fusion), channel_id=1, source_target_pairs={{0,2},{1,3},{4,6},{5,7},{8,10},{9,11},{12,14},{13,15},{16,18},{17,... | collective-permute-start | bytes 884744 | tf_op jit(solution)/shard_map/ppermute | solution.py:690
  34.4 3.7 %copy-start.1 = (s32[1,2]{1,0:T(1,128)S(1)}, s32[1,2]{1,0:T(1,128)}, u32[]{:S(2)}) copy-start(s32[1,2]{1,0:T(1,128)} %param.8) | copy-start | bytes 28
  34.4 3.7 %collective-permute-start.5 = (f32[4,2,72,128]{3,2,1,0:T(8,128)S(1)}, f32[4,2,72,128]{3,2,1,0:T(8,128)S(1)}, u32[]{:S(2)}, u32[]{:S(2)}) collective-permute-start(f32[4,2,72,128]{3,2,1,0:T(8,128)S(1)} %collective-permute-done.4.refs_5_), channel_id=1, source_target_pairs={{0,1},{1,0},{2,3},{3,2},{4,5},{5,4},{6,7},{7,6},{8,9},{9,8},{10,11... | collective-permute-start | bytes 884744 | tf_op jit(solution)/shard_map/ppermute | solution.py:631
  44.8 5.7 %collective-permute-start.8 = (f32[2,1024]{1,0:T(2,128)S(1)}, f32[2,1024]{1,0:T(2,128)S(1)}, u32[]{:S(2)}, u32[]{:S(2)}) collective-permute-start(f32[2,1024]{1,0:T(2,128)S(1)} %get-tuple-element.44), channel_id=1, source_target_pairs={{0,3},{1,2},{2,1},{3,0},{4,7},{5,6},{6,5},{7,4},{8,11},{9,10},{10,... | collective-permute-start | bytes 24584 | tf_op jit(solution)/shard_map/ppermute | solution.py:631
  46.6 4.0 %collective-permute-start.7 = (f32[2,1024]{1,0:T(2,128)S(1)}, f32[2,1024]{1,0:T(2,128)S(1)}, u32[]{:S(2)}, u32[]{:S(2)}) collective-permute-start(f32[2,1024]{1,0:T(2,128)S(1)} %get-tuple-element.44), channel_id=1, source_target_pairs={{0,2},{1,3},{2,0},{3,1},{4,6},{5,7},{6,4},{7,5},{8,10},{9,11},{10,... | collective-permute-start | bytes 24584 | tf_op jit(solution)/shard_map/ppermute | solution.py:631
  47.1 3.5 %collective-permute-start.6 = (f32[2,1024]{1,0:T(2,128)S(1)}, f32[2,1024]{1,0:T(2,128)S(1)}, u32[]{:S(2)}, u32[]{:S(2)}) collective-permute-start(f32[2,1024]{1,0:T(2,128)S(1)} %get-tuple-element.44), channel_id=1, source_target_pairs={{0,1},{1,0},{2,3},{3,2},{4,5},{5,4},{6,7},{7,6},{8,9},{9,8},{10,11... | collective-permute-start | bytes 24584 | tf_op jit(solution)/shard_map/ppermute | solution.py:631
  50.6 5.1 %collective-permute-start.9 = (f32[1,2,1024]{2,1,0:T(2,128)S(1)}, f32[1,2,1024]{2,1,0:T(2,128)S(1)}, u32[]{:S(2)}, u32[]{:S(2)}) collective-permute-start(f32[1,2,1024]{2,1,0:T(2,128)S(1)} %add_bitcast_fusion), channel_id=1, source_target_pairs={{0,4},{4,0},{8,12},{12,8},{16,20},{20,16},{24,28},{28,24},{1,5},{5... | collective-permute-start | bytes 24584 | tf_op jit(solution)/shard_map/ppermute | solution.py:631
  55.8 7.7 %collective-permute-start.12 = (f32[2,2,1024]{2,1,0:T(2,128)S(1)}, f32[2,2,1024]{2,1,0:T(2,128)S(1)}, u32[]{:S(2)}, u32[]{:S(2)}) collective-permute-start(f32[2,2,1024]{2,1,0:T(2,128)S(1)} %constant_dynamic-update-slice_fusion.refs_0_), channel_id=1, source_target_pairs={{0,24},{4,28},{8,16},{12,20},{16,8},{20,12},{24,0},{28,4},{1,25},{... | collective-permute-start | bytes 49160 | tf_op jit(solution)/shard_map/ppermute | solution.py:631
  59.5 4.6 %collective-permute-start.11 = (f32[2,2,1024]{2,1,0:T(2,128)S(1)}, f32[2,2,1024]{2,1,0:T(2,128)S(1)}, u32[]{:S(2)}, u32[]{:S(2)}) collective-permute-start(f32[2,2,1024]{2,1,0:T(2,128)S(1)} %constant_dynamic-update-slice_fusion.refs_0_), channel_id=1, source_target_pairs={{0,16},{4,20},{8,24},{12,28},{16,0},{20,4},{24,8},{28,12},{1,17},{... | collective-permute-start | bytes 49160 | tf_op jit(solution)/shard_map/ppermute | solution.py:631
  59.5 4.6 %collective-permute-start.10 = (f32[2,2,1024]{2,1,0:T(2,128)S(1)}, f32[2,2,1024]{2,1,0:T(2,128)S(1)}, u32[]{:S(2)}, u32[]{:S(2)}) collective-permute-start(f32[2,2,1024]{2,1,0:T(2,128)S(1)} %constant_dynamic-update-slice_fusion.refs_0_), channel_id=1, source_target_pairs={{0,8},{4,12},{8,0},{12,4},{16,24},{20,28},{24,16},{28,20},{1,9},{5... | collective-permute-start | bytes 49160 | tf_op jit(solution)/shard_map/ppermute | solution.py:631

commit v7 on v6

--- a/solution.py
+++ b/solution.py
@@ -156,42 +156,49 @@
     )(hbm(hidden), hbm(w_query), hbm(w_key), hbm(w_value))
 
 
-def pool_columns(step, steps, len_ref, start_ref, h_ref, fq_ref, num_ref, den_ref, prior_ref, wo_ref, out_ref):
-    count, span = fq_ref.shape[0], fq_ref.shape[1]
+def pool_unit(module, pair, cols, len_ref, start_ref, h_ref, fq_ref, num_ref, den_ref, prior_ref):
+    span = fq_ref.shape[1]
     low = iota((HEAD_DIM, LANES), 1) < HEAD_DIM
     same_head = (iota((LANES, LANES), 0) < HEAD_DIM) == (iota((LANES, LANES), 1) < HEAD_DIM)
     summing = jnp.concatenate([same_head.astype(BF16)] * 2, axis=0)
-    sums = []
-    hsums = []
-    for module in range(count):
-        valid = iota((span, LANES), 0) + start_ref[0] < len_ref[module]
-        heads = []
-        plain = []
-        for pair in range(COLS // LANES):
-            cols = slice(pair * LANES, (pair + 1) * LANES)
-            q = fq_ref[module, :, cols]
-            prior = prior_ref[pair, module]
-            state = prior[:HEAD_DIM].astype(BF16)
-            empty = jnp.zeros_like(state)
-            state = jnp.concatenate(
-                [jnp.where(low, state, empty), jnp.where(low, empty, state)], axis=0
-            )
-            hi, lo = split(q.astype(F32) * prior[HEAD_DIM : HEAD_DIM + 1], 2)
-            numer = num_ref[module, :, cols] + dot(q, state)
-            denom = den_ref[module, :, cols] + dot(jnp.concatenate([hi, lo], axis=1), summing)
-            attended = (numer / denom).astype(BF16).astype(F32)
-            heads.append(jnp.sum(jnp.where(valid, attended, 0.0), axis=0, keepdims=True))
-            plain.append(
-                jnp.sum(
-                    jnp.where(valid, h_ref[module, :, cols].astype(F32), 0.0), axis=0, keepdims=True
-                )
-            )
-        sums.append(jnp.concatenate(heads, axis=1))
-        hsums.append(jnp.concatenate(plain, axis=1))
-    sums = jnp.concatenate(sums, axis=0)
-    pieces = split(sums, 3)
-    part = dot(jnp.concatenate(pieces, axis=0), wo_ref[...])
-    part = part[:count] + part[count : 2 * count] + part[2 * count :]
+    valid = iota((span, LANES), 0) + start_ref[0] < len_ref[module]
+    q = fq_ref[module, :, cols]
+    prior = prior_ref[pair, module]
+    state = prior[:HEAD_DIM].astype(BF16)
+    empty = jnp.zeros_like(state)
+    state = jnp.concatenate([jnp.where(low, state, empty), jnp.where(low, empty, state)], axis=0)
+    hi, lo = split(q.astype(F32) * prior[HEAD_DIM : HEAD_DIM + 1], 2)
+    numer = num_ref[module, :, cols] + dot(q, state)
+    denom = den_ref[module, :, cols] + dot(jnp.concatenate([hi, lo], axis=1), summing)
+    attended = (numer / denom).astype(BF16).astype(F32)
+    plain = h_ref[module, :, cols].astype(F32)
+    return [
+        jnp.sum(jnp.where(valid, x, 0.0), axis=0, keepdims=True) for x in (attended, plain)
+    ]
+
+
+def project(sums, w_out):
+    count = sums.shape[0]
+    part = dot(jnp.concatenate(split(sums, 3), axis=0), w_out)
+    return part[:count] + part[count : 2 * count] + part[2 * count :]
+
+
+def pool_columns(step, steps, *refs):
+    *sources, wo_ref, out_ref = refs
+    len_ref = refs[0]
+    count = sources[2].shape[0]
+    units = [
+        [
+            pool_unit(module, pair, slice(pair * LANES, (pair + 1) * LANES), *sources)
+            for pair in range(COLS // LANES)
+        ]
+        for module in range(count)
+    ]
+    sums, plain = [
+        jnp.concatenate([jnp.concatenate([u[i] for u in row], axis=1) for row in units], axis=0)
+        for i in range(2)
+    ]
+    part = project(sums, wo_ref[...])
 
     @pl.when(step == 0)
     def _():
@@ -202,7 +209,7 @@
         out_ref[...] += part
 
     here = pl.ds(pl.multiple_of(step * COLS, COLS), COLS)
-    out_ref[:, here] += jnp.concatenate(hsums, axis=0)
+    out_ref[:, here] += plain
 
     @pl.when(step == steps - 1)
     def _():
@@ -246,9 +253,10 @@
 
 
 GROUP = 16
-
-
-def leaf_factor(mat, jobs=()):
+POOL_GAPS = 2
+
+
+def leaf_factor(mat, jobs=(), later={}):
     groups, tiles = LANES // GROUP, GROUP // 8
     sub, lane = iota((8, LANES), 0), iota((8, LANES), 1)
     rows = [
@@ -264,6 +272,8 @@
 
     for g in range(groups):
         for job in jobs[g::groups]:
+            job()
+        for job in later.get(g, ()):
             job()
         base = GROUP * g
         own = (lane >= base) & (lane < base + GROUP)
@@ -345,13 +355,13 @@
     return jobs
 
 
-def eliminate(ref, k):
+def eliminate(ref, k, later={}):
     n = ref.shape[0]
     panels = n // LANES
     low, high = k * LANES, (k + 1) * LANES
     row, col = iota((LANES, LANES), 0), iota((LANES, LANES), 1)
     jobs = deferred(ref, k - 1) if k > 0 else ()
-    inverse = jnp.where(col <= row, leaf_factor(ref[low:high, low:high], jobs), 0.0)
+    inverse = jnp.where(col <= row, leaf_factor(ref[low:high, low:high], jobs, later), 0.0)
     if k % 2 == 1:
         ref[low - LANES : low, low:high] = jnp.zeros((LANES, LANES), F32)
     one, two, three = split(inverse, 3)
@@ -411,7 +421,7 @@
 def panels_pool_kernel(panels, in_ref, len_ref, start_ref, core_ref, *refs):
     del in_ref
     *sources, matrix_ref, out_ref = refs[:10]
-    *held, prior_ref, beside_ref, sems = refs[10:]
+    *held, prior_ref, beside_ref, sums_ref, plain_ref, sems = refs[10:]
     half = prior_ref.shape[0] // 2
     own = pl.ds(core_ref[0] * half, half)
     other = pl.ds((1 - core_ref[0]) * half, half)
@@ -420,36 +430,41 @@
         pltpu.make_async_copy(source, to, sems.at[i])
         for i, (source, to) in enumerate(zip(sources, targets))
     ]
-    for copy in copies:
+    h_ref, fq_ref, num_ref, den_ref, wo_ref = held
+    last = copies.pop(4)
+    for copy in copies + [last]:
         copy.start()
+
+    def arrived():
+        for copy in copies:
+            copy.wait()
+
+        @pl.when(core_ref[0] == 1)
+        def _():
+            prior_ref[...] += beside_ref[...]
+
+    def unit(module, pair):
+        def run():
+            cols = slice(pair * LANES, (pair + 1) * LANES)
+            rows = slice(module, module + 1)
+            sums_ref[rows, cols], plain_ref[rows, cols] = pool_unit(
+                module, pair, cols, len_ref, start_ref, h_ref, fq_ref, num_ref, den_ref, prior_ref
+            )
+
+        return run
+
+    count = h_ref.shape[0]
+    units = [unit(m, pair) for pair in range(prior_ref.shape[0]) for m in range(count)]
+    groups = LANES // GROUP
+    gaps = range(groups - POOL_GAPS, groups)
+    later = {g: units[i::POOL_GAPS] for i, g in enumerate(gaps)}
+    later[gaps[0]] = [arrived] + later[gaps[0]]
     for k in panels:
-        eliminate(matrix_ref, k)
-    for copy in copies:
-        copy.wait()
-    h_ref, fq_ref, num_ref, den_ref, wo_ref = held
-
-    @pl.when(core_ref[0] == 1)
-    def _():
-        prior_ref[...] += beside_ref[...]
-
-    steps = wo_ref.shape[0] // COLS
-    pairs = COLS // LANES
-
-    for step in range(steps):
-        cols = slice(step * COLS, (step + 1) * COLS)
-        pool_columns(
-            step,
-            steps,
-            len_ref,
-            start_ref,
-            h_ref.at[:, :, cols],
-            fq_ref.at[:, :, cols],
-            num_ref.at[:, :, cols],
-            den_ref.at[:, :, cols],
-            prior_ref.at[step * pairs : (step + 1) * pairs],
-            wo_ref.at[cols, :],
-            out_ref,
-        )
+        eliminate(matrix_ref, k, later if k == panels[-1] else {})
+    last.wait()
+    pooled = plain_ref[...] + project(sums_ref[...], wo_ref[...])
+    for module in range(count):
+        out_ref[module : module + 1, :] = pooled[module : module + 1] / len_ref[module].astype(F32)
 
 
 def factor_next_pool(
@@ -466,6 +481,7 @@
         out_specs=[whole, whole],
         out_shape=[pltpu.VMEM((n, n), F32), jax.ShapeDtypeStruct((count, width), F32)],
         scratch_shapes=[pltpu.VMEM(x.shape, x.dtype) for x in operands + [beside, beside]]
+        + [pltpu.VMEM((count, width), F32)] * 2
         + [pltpu.SemaphoreType.DMA((8,))],
         input_output_aliases={0: 0},
         compiler_params=params(24),
@@ -712,11 +728,11 @@
     matrix = factor_next((5,), matrix)
     partial, got, matrix = lax.optimization_barrier((partial, got, matrix))
     embed = ((partial + got[0]) + (got[1] + got[2]))[None]
-    beside = swap(embed, "dp", 1)
+    near = [swap(embed, "dp", by) for by in (1, 2, 3)]
     matrix = factor_next((6,), matrix)
-    embed, beside, matrix = lax.optimization_barrier((embed, beside, matrix))
-    embed = jnp.concatenate([embed, beside], axis=0)
-    pieces = [embed] + [swap(embed, "dp", by) for by in (2, 4, 6)]
+    embed, near, matrix = lax.optimization_barrier((embed, near, matrix))
+    embed = jnp.concatenate([embed] + near, axis=0)
+    pieces = [embed, swap(embed, "dp", 4)]
     matrix = factor_next((7,), matrix)
     white, cov, loss = whiten(at, pieces, matrix, running_cov)
     return white, cov, loss.reshape(())

time: 68.7 us -> 68.2 us (level)
  transfers between devices with their start and end apart: 13 -> 13, of which waited for: 2 -> 1; matrix products, arithmetic and copies ran while one was open for 2% -> 2% of each run, Pallas kernels for 55% -> 56%
where the time goes in v7:
time: 68.2 us; the launch traced here: 68 us
  Pallas kernels  48.8 us (72%)
  starting transfers between devices  15.5 us (23%)
  waiting for transfers between devices  1.35 us (2%)
  local copies, waits for them, and re-layouts  1.21 us (2%)
  between operations  1.04 us (2%)
    pallas_call x5, Pallas kernels, factor_next(): pl.pallas_call(functools.partial(panels_kernel, panels), in_specs=[pl.Blo...  21.1 us
    pallas_call x1, Pallas kernels, encode(): pl.pallas_call(encode_kernel, in_specs=[anywhere] * 4, out_specs=[anywher...  13.4 us
    ppermute x12, starting transfers between devices, swap(): return lax.ppermute(x, axis, [(i, i ^ by) for i in range(size)])  12.2 us
    pallas_call x1, Pallas kernels, factor_next_pool(): pl.pallas_call(functools.partial(panels_pool_kernel, panels), in_specs=[w...  6.52 us
    pallas_call x1, Pallas kernels, whiten(): pl.pallas_call(whiten_kernel, in_specs=[pl.BlockSpec(memory_space=SMEM)]...  4.29 us
    pallas_call x1, Pallas kernels, factor_first(): pl.pallas_call(functools.partial(load_kernel, panels), in_specs=[pl.Block...  3.54 us
    ppermute x1, starting transfers between devices, body_fixed(): far_half = lax.ppermute(mine, 'seq', [(0, 2), (1, 3)])  3.29 us
  transfers between devices with their start and end apart: 13, of which 1 were waited for; matrix products, arithmetic and copies ran while one was open for 2% of the time, Pallas kernels for 56%

profile of v7, /device:TPU:0, one launch (start us, length us, event | category | flops | bytes accessed | tf_op | source)
XLA Modules:
  0.0 68.0 jit_solution(12008065976079591693)
XLA Ops:
  0.6 0.5 collective-permute-start.1
  1.1 0.0 copy-start
  1.1 1.2 %constant_dynamic-slice_fusion = f32[256,512]{1,0:T(8,128)S(1)} fusion(f32[256,1024]{1,0:T(8,128)} %refs_3_.3, s32[]{:T(128)S(6)} %select_n.7), kind=kLoop, calls=%fused_computation.6 | loop fusion | bytes 1048580 | tf_op jit(solution)/shard_map/dynamic_slice | solution.py:694
  2.3 2.6 %collective-permute-start = (f32[256,512]{1,0:T(8,128)S(1)}, f32[256,512]{1,0:T(8,128)S(1)}, u32[]{:S(2)}, u32[]{:S(2)}) collective-permute-start(f32[256,512]{1,0:T(8,128)S(1)} %constant_dynamic-slice_fusion), channel_id=1, source_target_pairs={{0,2},{1,3},{2,0},{3,1},{4,6},{5,7},{6,4},{7,5},{8,10},{9,11},{10,... | collective-permute-start | bytes 1572872 | tf_op jit(solution)/shard_map/ppermute | solution.py:647
  4.9 13.4 %encode.1 = (bf16[2,256,1024]{2,1,0:T(8,128)(2,1)}, f32[2,256,1024]{2,1,0:T(8,128)}, f32[2,256,1024]{2,1,0:T(8,128)}, f32[8,2,72,128]{3,2,1,0:T(8,128)}) custom-call(bf16[2,256,1024]{2,1,0:T(8,128)(2,1)} %bitcast.11, bf16[1024,1024]{1,0:T(8,128)(2,1)} %refs_1_.1, bf16[1024,1024]{1,0:T(8,128)(2,1)} %refs_2_.1, bf16[1024,1024]{1,0:T(8,128)(2,1)} %refs_3_.2), custom_call_target="tpu_custom_call" | custom-call | tf_op jit(solution)/shard_map/encode/pallas_call | solution.py:146
  18.3 0.0 collective-permute-done.far_ref
  18.3 0.0 collective-permute-done.1.core_ref
  18.3 0.3 collective-permute-start.3
  18.6 0.1 pad_add_fusion.at_ref
  18.7 0.0 copy-start.2
  18.7 0.3 collective-permute-start.2
  19.0 1.3 %collective-permute-done.3.far_core_ref = f32[256,512]{1,0:T(8,128)S(1)} collective-permute-done((f32[256,512]{1,0:T(8,128)S(1)}, f32[256,512]{1,0:T(8,128)S(1)}, u32[]{:S(2)}, u32[]{:S(2)}) %collective-permute-start.3) | collective-permute-done | bytes 524320 | tf_op jit(solution)/shard_map/ppermute | solution.py:647
  20.3 0.0 copy-done
  20.3 3.5 %factor_first.1.in_ref = f32[1024,1024]{1,0:T(8,128)S(1)} custom-call(s32[1]{0:T(128)} %bitcast.1.me_ref, f32[256,1024]{1,0:T(8,128)S(1)} %copy-done, f32[256,1024]{1,0:T(8,128)S(1)} %collective-permute-done.1.core_ref, f32[256,512]{1,0:T(8,128)S(1)} %collective-permute-done.far_ref, f32[256,512]{1,0:T(8,128)S(1)} %collective-permute-done.3.far_core_ref), custom_call_target="tpu_custom_call" | custom-call | flops 8000000000 | bytes 4194304 | tf_op jit(solution)/shard_map/factor_first/pallas_call | solution.py:496
  23.9 0.0 collective-permute-done.2.refs_7_
  23.9 0.0 copy-done.2
  23.9 3.3 %collective-permute-start.4 = (f32[4,2,72,128]{3,2,1,0:T(8,128)S(1)}, f32[4,2,72,128]{3,2,1,0:T(8,128)S(1)}, u32[]{:S(2)}, u32[]{:S(2)}) collective-permute-start(f32[4,2,72,128]{3,2,1,0:T(8,128)S(1)} %dynamic-slice_add_fusion), channel_id=1, source_target_pairs={{0,2},{1,3},{4,6},{5,7},{8,10},{9,11},{12,14},{13,15},{16,18},{17,... | collective-permute-start | bytes 884744 | tf_op jit(solution)/shard_map/ppermute | solution.py:706
  27.2 7.2 %factor_next.5.in_ref = f32[1024,1024]{1,0:T(8,128)S(1)} custom-call(f32[1024,1024]{1,0:T(8,128)S(1)} %factor_first.1.in_ref), custom_call_target="tpu_custom_call", output_to_operand_aliasing={{}: (0, {})} | custom-call | flops 8000000000 | bytes 4194304 | tf_op jit(solution)/shard_map/factor_next/pallas_call | solution.py:510
  34.4 0.0 copy-start.1
  34.4 0.0 collective-permute-done.4.refs_5_
  34.4 0.1 collective-permute-start.5
  34.5 3.6 %factor_next.6.in_ref = f32[1024,1024]{1,0:T(8,128)S(1)} custom-call(f32[1024,1024]{1,0:T(8,128)S(1)} %factor_next.5.in_ref), custom_call_target="tpu_custom_call", output_to_operand_aliasing={{}: (0, {})} | custom-call | flops 8000000000 | bytes 4194304 | tf_op jit(solution)/shard_map/factor_next/pallas_call | solution.py:510
  38.1 0.0 collective-permute-done.5.refs_6_
  38.1 0.0 copy-done.1
  38.1 6.5 %factor_next_pool.1 = (f32[1024,1024]{1,0:T(8,128)S(1)}, f32[2,1024]{1,0:T(2,128)S(1)}) custom-call(f32[1024,1024]{1,0:T(8,128)S(1)} %factor_next.6.in_ref, s32[2]{0:T(128)S(1)} %bitcast.10, s32[1]{0:T(128)} %bitcast.4.start_ref, s32[1]{0:T(128)} %bitcast.5.core_ref, bf16[2,256,1024]{2,1,0:T(8,128)(2,1)} %bitcast.12, ...), custom_call_target="tpu_custom_call", output_to_operand_aliasing={{0}: (0, {})} | custom-call | flops 8000000000 | bytes 12582912 | tf_op jit(solution)/shard_map/factor_next_pool/pallas_call | solution.py:478
  44.6 1.8 %collective-permute-start.8 = (f32[2,1024]{1,0:T(2,128)S(1)}, f32[2,1024]{1,0:T(2,128)S(1)}, u32[]{:S(2)}, u32[]{:S(2)}) collective-permute-start(f32[2,1024]{1,0:T(2,128)S(1)} %get-tuple-element.46), channel_id=1, source_target_pairs={{0,3},{1,2},{2,1},{3,0},{4,7},{5,6},{6,5},{7,4},{8,11},{9,10},{10,... | collective-permute-start | bytes 24584 | tf_op jit(solution)/shard_map/ppermute | solution.py:647
  46.4 0.5 collective-permute-start.7
  46.9 0.0 collective-permute-start.6
  46.9 3.5 %factor_next.7.in_ref = f32[1024,1024]{1,0:T(8,128)S(1)} custom-call(f32[1024,1024]{1,0:T(8,128)S(1)} %get-tuple-element.45.in_ref), custom_call_target="tpu_custom_call", output_to_operand_aliasing={{}: (0, {})} | custom-call | flops 8000000000 | bytes 4194304 | tf_op jit(solution)/shard_map/factor_next/pallas_call | solution.py:510
  50.4 0.0 collective-permute-done.8
  50.4 0.0 collective-permute-done.7
  50.4 0.0 collective-permute-done.6
  50.4 2.6 %collective-permute-start.11 = (f32[1,2,1024]{2,1,0:T(2,128)S(1)}, f32[1,2,1024]{2,1,0:T(2,128)S(1)}, u32[]{:S(2)}, u32[]{:S(2)}) collective-permute-start(f32[1,2,1024]{2,1,0:T(2,128)S(1)} %add_bitcast_fusion), channel_id=1, source_target_pairs={{0,12},{4,8},{8,4},{12,0},{16,28},{20,24},{24,20},{28,16},{1,13},{... | collective-permute-start | bytes 24584 | tf_op jit(solution)/shard_map/ppermute | solution.py:647
  53.0 0.4 collective-permute-start.10
  53.4 0.5 collective-permute-start.9
  54.0 3.6 %factor_next.8.in_ref = f32[1024,1024]{1,0:T(8,128)S(1)} custom-call(f32[1024,1024]{1,0:T(8,128)S(1)} %factor_next.7.in_ref), custom_call_target="tpu_custom_call", output_to_operand_aliasing={{}: (0, {})} | custom-call | flops 8000000000 | bytes 4194304 | tf_op jit(solution)/shard_map/factor_next/pallas_call | solution.py:510
  57.6 0.0 collective-permute-done.11
  57.6 0.0 collective-permute-done.10
  57.6 0.0 collective-permute-done.9
  57.6 2.6 %collective-permute-start.12 = (f32[4,2,1024]{2,1,0:T(2,128)S(1)}, f32[4,2,1024]{2,1,0:T(2,128)S(1)}, u32[]{:S(2)}, u32[]{:S(2)}) collective-permute-start(f32[4,2,1024]{2,1,0:T(2,128)S(1)} %constant_dynamic-update-slice_fusion.refs_0_), channel_id=1, source_target_pairs={{0,16},{4,20},{8,24},{12,28},{16,0},{20,4},{24,8},{28,12},{1,17},{... | collective-permute-start | bytes 98312 | tf_op jit(solution)/shard_map/ppermute | solution.py:647
  60.3 3.3 %factor_next.9.refs_2_ = f32[1024,1024]{1,0:T(8,128)S(1)} custom-call(f32[1024,1024]{1,0:T(8,128)S(1)} %factor_next.8.in_ref), custom_call_target="tpu_custom_call", output_to_operand_aliasing={{}: (0, {})} | custom-call | flops 8000000000 | bytes 4194304 | tf_op jit(solution)/shard_map/factor_next/pallas_call | solution.py:510
  63.5 0.0 collective-permute-done.12.refs_1_
  63.6 4.3 %whiten.1 = (f32[2,1024]{1,0:T(2,128)}, f32[256,1024]{1,0:T(8,128)}, f32[1,1]{1,0:T(1,128)}) custom-call(s32[2]{0:T(128)S(1)} %pad_add_fusion.at_ref, f32[4,2,1024]{2,1,0:T(2,128)S(1)} %constant_dynamic-update-slice_fusion.refs_0_, f32[4,2,1024]{2,1,0:T(2,128)S(1)} %collective-permute-done.12.refs_1_, f32[1024,1024]{1,0:T(8,128)S(1)} %factor_next.9.refs_2_, ...), custom_call_target="tpu_custom_call" | custom-call | tf_op jit(solution)/shard_map/whiten/pallas_call | solution.py:620
  (6 shorter events, 0.1 us)
Async XLA Ops:
  0.6 17.7 %collective-permute-start.1 = (f32[256,1024]{1,0:T(8,128)}, f32[256,1024]{1,0:T(8,128)S(1)}, u32[]{:S(2)}, u32[]{:S(2)}) collective-permute-start(f32[256,1024]{1,0:T(8,128)} %refs_3_.3), channel_id=1, source_target_pairs={{0,1},{1,0},{2,3},{3,2},{4,5},{5,4},{6,7},{7,6},{8,9},{9,8},{10,11... | collective-permute-start | bytes 3145736 | tf_op jit(solution)/shard_map/ppermute | solution.py:647
  1.1 19.2 %copy-start = (f32[256,1024]{1,0:T(8,128)S(1)}, f32[256,1024]{1,0:T(8,128)}, u32[]{:S(2)}) copy-start(f32[256,1024]{1,0:T(8,128)} %refs_3_.3) | copy-start | bytes 3145732
  2.3 16.0 %collective-permute-start = (f32[256,512]{1,0:T(8,128)S(1)}, f32[256,512]{1,0:T(8,128)S(1)}, u32[]{:S(2)}, u32[]{:S(2)}) collective-permute-start(f32[256,512]{1,0:T(8,128)S(1)} %constant_dynamic-slice_fusion), channel_id=1, source_target_pairs={{0,2},{1,3},{2,0},{3,1},{4,6},{5,7},{6,4},{7,5},{8,10},{9,11},{10,... | collective-permute-start | bytes 1572872 | tf_op jit(solution)/shard_map/ppermute | solution.py:647
  18.3 2.0 %collective-permute-start.3 = (f32[256,512]{1,0:T(8,128)S(1)}, f32[256,512]{1,0:T(8,128)S(1)}, u32[]{:S(2)}, u32[]{:S(2)}) collective-permute-start(f32[256,512]{1,0:T(8,128)S(1)} %collective-permute-done.far_ref), channel_id=1, source_target_pairs={{0,1},{1,0},{2,3},{3,2},{4,5},{5,4},{6,7},{7,6},{8,9},{9,8},{10,11... | collective-permute-start | bytes 1572872 | tf_op jit(solution)/shard_map/ppermute | solution.py:647
  18.7 5.2 %copy-start.2 = (f32[8,2,72,128]{3,2,1,0:T(8,128)S(1)}, f32[8,2,72,128]{3,2,1,0:T(8,128)}, u32[]{:S(2)}) copy-start(f32[8,2,72,128]{3,2,1,0:T(8,128)} %get-tuple-element.32) | copy-start | bytes 1769476
  18.7 5.2 %collective-permute-start.2 = (f32[8,2,72,128]{3,2,1,0:T(8,128)}, f32[8,2,72,128]{3,2,1,0:T(8,128)S(1)}, u32[]{:S(2)}, u32[]{:S(2)}) collective-permute-start(f32[8,2,72,128]{3,2,1,0:T(8,128)} %get-tuple-element.32), channel_id=1, source_target_pairs={{0,1},{1,0},{2,3},{3,2},{4,5},{5,4},{6,7},{7,6},{8,9},{9,8},{10,11... | collective-permute-start | bytes 1769480 | tf_op jit(solution)/shard_map/ppermute | solution.py:647
  23.9 10.5 %collective-permute-start.4 = (f32[4,2,72,128]{3,2,1,0:T(8,128)S(1)}, f32[4,2,72,128]{3,2,1,0:T(8,128)S(1)}, u32[]{:S(2)}, u32[]{:S(2)}) collective-permute-start(f32[4,2,72,128]{3,2,1,0:T(8,128)S(1)} %dynamic-slice_add_fusion), channel_id=1, source_target_pairs={{0,2},{1,3},{4,6},{5,7},{8,10},{9,11},{12,14},{13,15},{16,18},{17,... | collective-permute-start | bytes 884744 | tf_op jit(solution)/shard_map/ppermute | solution.py:706
  34.4 3.7 %copy-start.1 = (s32[1,2]{1,0:T(1,128)S(1)}, s32[1,2]{1,0:T(1,128)}, u32[]{:S(2)}) copy-start(s32[1,2]{1,0:T(1,128)} %param.8) | copy-start | bytes 28
  34.4 3.7 %collective-permute-start.5 = (f32[4,2,72,128]{3,2,1,0:T(8,128)S(1)}, f32[4,2,72,128]{3,2,1,0:T(8,128)S(1)}, u32[]{:S(2)}, u32[]{:S(2)}) collective-permute-start(f32[4,2,72,128]{3,2,1,0:T(8,128)S(1)} %collective-permute-done.4.refs_5_), channel_id=1, source_target_pairs={{0,1},{1,0},{2,3},{3,2},{4,5},{5,4},{6,7},{7,6},{8,9},{9,8},{10,11... | collective-permute-start | bytes 884744 | tf_op jit(solution)/shard_map/ppermute | solution.py:647
  44.6 5.7 %collective-permute-start.8 = (f32[2,1024]{1,0:T(2,128)S(1)}, f32[2,1024]{1,0:T(2,128)S(1)}, u32[]{:S(2)}, u32[]{:S(2)}) collective-permute-start(f32[2,1024]{1,0:T(2,128)S(1)} %get-tuple-element.46), channel_id=1, source_target_pairs={{0,3},{1,2},{2,1},{3,0},{4,7},{5,6},{6,5},{7,4},{8,11},{9,10},{10,... | collective-permute-start | bytes 24584 | tf_op jit(solution)/shard_map/ppermute | solution.py:647
  46.4 4.0 %collective-permute-start.7 = (f32[2,1024]{1,0:T(2,128)S(1)}, f32[2,1024]{1,0:T(2,128)S(1)}, u32[]{:S(2)}, u32[]{:S(2)}) collective-permute-start(f32[2,1024]{1,0:T(2,128)S(1)} %get-tuple-element.46), channel_id=1, source_target_pairs={{0,2},{1,3},{2,0},{3,1},{4,6},{5,7},{6,4},{7,5},{8,10},{9,11},{10,... | collective-permute-start | bytes 24584 | tf_op jit(solution)/shard_map/ppermute | solution.py:647
  46.9 3.5 %collective-permute-start.6 = (f32[2,1024]{1,0:T(2,128)S(1)}, f32[2,1024]{1,0:T(2,128)S(1)}, u32[]{:S(2)}, u32[]{:S(2)}) collective-permute-start(f32[2,1024]{1,0:T(2,128)S(1)} %get-tuple-element.46), channel_id=1, source_target_pairs={{0,1},{1,0},{2,3},{3,2},{4,5},{5,4},{6,7},{7,6},{8,9},{9,8},{10,11... | collective-permute-start | bytes 24584 | tf_op jit(solution)/shard_map/ppermute | solution.py:647
  50.4 7.1 %collective-permute-start.11 = (f32[1,2,1024]{2,1,0:T(2,128)S(1)}, f32[1,2,1024]{2,1,0:T(2,128)S(1)}, u32[]{:S(2)}, u32[]{:S(2)}) collective-permute-start(f32[1,2,1024]{2,1,0:T(2,128)S(1)} %add_bitcast_fusion), channel_id=1, source_target_pairs={{0,12},{4,8},{8,4},{12,0},{16,28},{20,24},{24,20},{28,16},{1,13},{... | collective-permute-start | bytes 24584 | tf_op jit(solution)/shard_map/ppermute | solution.py:647
  53.0 4.6 %collective-permute-start.10 = (f32[1,2,1024]{2,1,0:T(2,128)S(1)}, f32[1,2,1024]{2,1,0:T(2,128)S(1)}, u32[]{:S(2)}, u32[]{:S(2)}) collective-permute-start(f32[1,2,1024]{2,1,0:T(2,128)S(1)} %add_bitcast_fusion), channel_id=1, source_target_pairs={{0,8},{4,12},{8,0},{12,4},{16,24},{20,28},{24,16},{28,20},{1,9},{5... | collective-permute-start | bytes 24584 | tf_op jit(solution)/shard_map/ppermute | solution.py:647
  53.4 4.1 %collective-permute-start.9 = (f32[1,2,1024]{2,1,0:T(2,128)S(1)}, f32[1,2,1024]{2,1,0:T(2,128)S(1)}, u32[]{:S(2)}, u32[]{:S(2)}) collective-permute-start(f32[1,2,1024]{2,1,0:T(2,128)S(1)} %add_bitcast_fusion), channel_id=1, source_target_pairs={{0,4},{4,0},{8,12},{12,8},{16,20},{20,16},{24,28},{28,24},{1,5},{5... | collective-permute-start | bytes 24584 | tf_op jit(solution)/shard_map/ppermute | solution.py:647
  57.6 5.9 %collective-permute-start.12 = (f32[4,2,1024]{2,1,0:T(2,128)S(1)}, f32[4,2,1024]{2,1,0:T(2,128)S(1)}, u32[]{:S(2)}, u32[]{:S(2)}) collective-permute-start(f32[4,2,1024]{2,1,0:T(2,128)S(1)} %constant_dynamic-update-slice_fusion.refs_0_), channel_id=1, source_target_pairs={{0,16},{4,20},{8,24},{12,28},{16,0},{20,4},{24,8},{28,12},{1,17},{... | collective-permute-start | bytes 98312 | tf_op jit(solution)/shard_map/ppermute | solution.py:647

commit v8 on v7

--- a/solution.py
+++ b/solution.py
@@ -11,6 +11,7 @@
 HEAD_DIM = 64
 LANES = 128
 COLS = 256
+WIDE = 512
 F32 = jnp.float32
 BF16 = jnp.bfloat16
 HIGHEST = lax.Precision.HIGHEST
@@ -60,11 +61,11 @@
 def encode_kernel(*refs):
     (hidden_ref, *weight_refs), results = refs[:4], refs[4:8]
     (h_ref, w_ref, *held), (in_sems, out_sems) = refs[8:14], refs[14:]
-    steps = w_ref.shape[2] // COLS
-    pairs = COLS // LANES
+    steps = w_ref.shape[2] // WIDE
+    pairs = WIDE // LANES
 
     def window(j):
-        return pl.ds(pl.multiple_of(j * COLS, COLS), COLS)
+        return pl.ds(pl.multiple_of(j * WIDE, WIDE), WIDE)
 
     def arriving(i, j):
         return pltpu.make_async_copy(
@@ -117,7 +118,7 @@
     for module in range(count):
         at = slice(module * span, (module + 1) * span)
         running = dot(ones_below, fk[at])
-        for pair in range(COLS // LANES):
+        for pair in range(WIDE // LANES):
             cols = slice(pair * LANES, (pair + 1) * LANES)
             q, k, v = fq[at, cols], fk[at, cols], values[at, cols]
             state = dot(k, v, 0, 0)
@@ -138,7 +139,7 @@
 
 def encode(hidden, w_query, w_key, w_value):
     count, span, width = hidden.shape
-    steps = width // COLS
+    steps = width // WIDE
     shape = (count, span, width)
     state_shape = (width // LANES, count, HEAD_DIM + 8, LANES)
     anywhere = pl.BlockSpec(memory_space=pl.ANY)
@@ -151,7 +152,7 @@
         scratch_shapes=[VMEM(shape, BF16), VMEM((3, width, width), BF16)]
         + [VMEM(*x) for x in results]
         + [pltpu.SemaphoreType.DMA((4, steps)), pltpu.SemaphoreType.DMA((4, steps))],
-        compiler_params=params(24),
+        compiler_params=params(28),
         name="encode",
     )(hbm(hidden), hbm(w_query), hbm(w_key), hbm(w_value))
 

time: 68.2 us -> 68.2 us (level)
  Pallas kernels: 48.8 us -> 47.6 us
  starting transfers between devices: 15.5 us -> 16.4 us
    pallas_call x1, Pallas kernels: 13.4 us -> 12.2 us  [encode(): pl.pallas_call(encode_kernel, in_specs=[anywhere] * 4, out_specs=[anywher...]
    ppermute x1, starting transfers between devices: 3.29 us -> 4.18 us  [body_fixed(): far_half = lax.ppermute(mine, 'seq', [(0, 2), (1, 3)])]
  transfers between devices with their start and end apart: 13 -> 13, of which waited for: 1 -> 2; matrix products, arithmetic and copies ran while one was open for 2% -> 2% of each run, Pallas kernels for 56% -> 54%
where the time goes in v8:
time: 68.2 us; the launch traced here: 68 us
  Pallas kernels  47.6 us (70%)
  starting transfers between devices  16.4 us (24%)
  waiting for transfers between devices  1.75 us (3%)
  local copies, waits for them, and re-layouts  1.21 us (2%)
  between operations  1.03 us (2%)
    pallas_call x5, Pallas kernels, factor_next(): pl.pallas_call(functools.partial(panels_kernel, panels), in_specs=[pl.Blo...  21.1 us
    ppermute x12, starting transfers between devices, swap(): return lax.ppermute(x, axis, [(i, i ^ by) for i in range(size)])  12.2 us
    pallas_call x1, Pallas kernels, encode(): pl.pallas_call(encode_kernel, in_specs=[anywhere] * 4, out_specs=[anywher...  12.2 us
    pallas_call x1, Pallas kernels, factor_next_pool(): pl.pallas_call(functools.partial(panels_pool_kernel, panels), in_specs=[w...  6.52 us
    pallas_call x1, Pallas kernels, whiten(): pl.pallas_call(whiten_kernel, in_specs=[pl.BlockSpec(memory_space=SMEM)]...  4.29 us
    ppermute x1, starting transfers between devices, body_fixed(): far_half = lax.ppermute(mine, 'seq', [(0, 2), (1, 3)])  4.18 us
    pallas_call x1, Pallas kernels, factor_first(): pl.pallas_call(functools.partial(load_kernel, panels), in_specs=[pl.Block...  3.54 us
    ppermute x12, waiting for transfers between devices, swap(): return lax.ppermute(x, axis, [(i, i ^ by) for i in range(size)])  1.75 us
  transfers between devices with their start and end apart: 13, of which 2 were waited for; matrix products, arithmetic and copies ran while one was open for 2% of the time, Pallas kernels for 54%

profile of v8, /device:TPU:0, one launch (start us, length us, event | category | flops | bytes accessed | tf_op | source)
XLA Modules:
  0.0 68.0 jit_solution(15727706207908044722)
XLA Ops:
  0.6 0.5 collective-permute-start.1
  1.1 0.0 copy-start
  1.1 1.2 %constant_dynamic-slice_fusion = f32[256,512]{1,0:T(8,128)S(1)} fusion(f32[256,1024]{1,0:T(8,128)} %refs_3_.3, s32[]{:T(128)S(6)} %select_n.7), kind=kLoop, calls=%fused_computation.6 | loop fusion | bytes 1048580 | tf_op jit(solution)/shard_map/dynamic_slice | solution.py:695
  2.3 2.6 %collective-permute-start = (f32[256,512]{1,0:T(8,128)S(1)}, f32[256,512]{1,0:T(8,128)S(1)}, u32[]{:S(2)}, u32[]{:S(2)}) collective-permute-start(f32[256,512]{1,0:T(8,128)S(1)} %constant_dynamic-slice_fusion), channel_id=1, source_target_pairs={{0,2},{1,3},{2,0},{3,1},{4,6},{5,7},{6,4},{7,5},{8,10},{9,11},{10,... | collective-permute-start | bytes 1572872 | tf_op jit(solution)/shard_map/ppermute | solution.py:648
  4.9 12.2 %encode.1 = (bf16[2,256,1024]{2,1,0:T(8,128)(2,1)}, f32[2,256,1024]{2,1,0:T(8,128)}, f32[2,256,1024]{2,1,0:T(8,128)}, f32[8,2,72,128]{3,2,1,0:T(8,128)}) custom-call(bf16[2,256,1024]{2,1,0:T(8,128)(2,1)} %bitcast.11, bf16[1024,1024]{1,0:T(8,128)(2,1)} %refs_1_.1, bf16[1024,1024]{1,0:T(8,128)(2,1)} %refs_2_.1, bf16[1024,1024]{1,0:T(8,128)(2,1)} %refs_3_.2), custom_call_target="tpu_custom_call" | custom-call | tf_op jit(solution)/shard_map/encode/pallas_call | solution.py:147
  17.1 0.4 collective-permute-done.far_ref
  17.5 0.0 collective-permute-done.1.core_ref
  17.5 0.0 collective-permute-start.3
  17.5 0.1 pad_add_fusion.at_ref
  17.6 0.0 copy-start.2
  17.6 0.5 collective-permute-start.2
  18.1 1.3 %collective-permute-done.3.far_core_ref = f32[256,512]{1,0:T(8,128)S(1)} collective-permute-done((f32[256,512]{1,0:T(8,128)S(1)}, f32[256,512]{1,0:T(8,128)S(1)}, u32[]{:S(2)}, u32[]{:S(2)}) %collective-permute-start.3) | collective-permute-done | bytes 524320 | tf_op jit(solution)/shard_map/ppermute | solution.py:648
  19.4 0.0 copy-done
  19.4 3.5 %factor_first.1.in_ref = f32[1024,1024]{1,0:T(8,128)S(1)} custom-call(s32[1]{0:T(128)} %bitcast.1.me_ref, f32[256,1024]{1,0:T(8,128)S(1)} %copy-done, f32[256,1024]{1,0:T(8,128)S(1)} %collective-permute-done.1.core_ref, f32[256,512]{1,0:T(8,128)S(1)} %collective-permute-done.far_ref, f32[256,512]{1,0:T(8,128)S(1)} %collective-permute-done.3.far_core_ref), custom_call_target="tpu_custom_call" | custom-call | flops 8000000000 | bytes 4194304 | tf_op jit(solution)/shard_map/factor_first/pallas_call | solution.py:497
  23.0 0.0 collective-permute-done.2.refs_7_
  23.0 0.0 copy-done.2
  23.0 4.2 %collective-permute-start.4 = (f32[4,2,72,128]{3,2,1,0:T(8,128)S(1)}, f32[4,2,72,128]{3,2,1,0:T(8,128)S(1)}, u32[]{:S(2)}, u32[]{:S(2)}) collective-permute-start(f32[4,2,72,128]{3,2,1,0:T(8,128)S(1)} %dynamic-slice_add_fusion), channel_id=1, source_target_pairs={{0,2},{1,3},{4,6},{5,7},{8,10},{9,11},{12,14},{13,15},{16,18},{17,... | collective-permute-start | bytes 884744 | tf_op jit(solution)/shard_map/ppermute | solution.py:707
  27.2 7.2 %factor_next.5.in_ref = f32[1024,1024]{1,0:T(8,128)S(1)} custom-call(f32[1024,1024]{1,0:T(8,128)S(1)} %factor_first.1.in_ref), custom_call_target="tpu_custom_call", output_to_operand_aliasing={{}: (0, {})} | custom-call | flops 8000000000 | bytes 4194304 | tf_op jit(solution)/shard_map/factor_next/pallas_call | solution.py:511
  34.4 0.0 copy-start.1
  34.4 0.0 collective-permute-done.4.refs_5_
  34.4 0.1 collective-permute-start.5
  34.5 3.6 %factor_next.6.in_ref = f32[1024,1024]{1,0:T(8,128)S(1)} custom-call(f32[1024,1024]{1,0:T(8,128)S(1)} %factor_next.5.in_ref), custom_call_target="tpu_custom_call", output_to_operand_aliasing={{}: (0, {})} | custom-call | flops 8000000000 | bytes 4194304 | tf_op jit(solution)/shard_map/factor_next/pallas_call | solution.py:511
  38.1 0.0 collective-permute-done.5.refs_6_
  38.1 0.0 copy-done.1
  38.1 6.5 %factor_next_pool.1 = (f32[1024,1024]{1,0:T(8,128)S(1)}, f32[2,1024]{1,0:T(2,128)S(1)}) custom-call(f32[1024,1024]{1,0:T(8,128)S(1)} %factor_next.6.in_ref, s32[2]{0:T(128)S(1)} %bitcast.10, s32[1]{0:T(128)} %bitcast.4.start_ref, s32[1]{0:T(128)} %bitcast.5.core_ref, bf16[2,256,1024]{2,1,0:T(8,128)(2,1)} %bitcast.12, ...), custom_call_target="tpu_custom_call", output_to_operand_aliasing={{0}: (0, {})} | custom-call | flops 8000000000 | bytes 12582912 | tf_op jit(solution)/shard_map/factor_next_pool/pallas_call | solution.py:479
  44.6 1.8 %collective-permute-start.8 = (f32[2,1024]{1,0:T(2,128)S(1)}, f32[2,1024]{1,0:T(2,128)S(1)}, u32[]{:S(2)}, u32[]{:S(2)}) collective-permute-start(f32[2,1024]{1,0:T(2,128)S(1)} %get-tuple-element.46), channel_id=1, source_target_pairs={{0,3},{1,2},{2,1},{3,0},{4,7},{5,6},{6,5},{7,4},{8,11},{9,10},{10,... | collective-permute-start | bytes 24584 | tf_op jit(solution)/shard_map/ppermute | solution.py:648
  46.4 0.5 collective-permute-start.7
  46.9 0.0 collective-permute-start.6
  46.9 3.5 %factor_next.7.in_ref = f32[1024,1024]{1,0:T(8,128)S(1)} custom-call(f32[1024,1024]{1,0:T(8,128)S(1)} %get-tuple-element.45.in_ref), custom_call_target="tpu_custom_call", output_to_operand_aliasing={{}: (0, {})} | custom-call | flops 8000000000 | bytes 4194304 | tf_op jit(solution)/shard_map/factor_next/pallas_call | solution.py:511
  50.4 0.0 collective-permute-done.8
  50.4 0.0 collective-permute-done.7
  50.4 0.0 collective-permute-done.6
  50.4 2.6 %collective-permute-start.11 = (f32[1,2,1024]{2,1,0:T(2,128)S(1)}, f32[1,2,1024]{2,1,0:T(2,128)S(1)}, u32[]{:S(2)}, u32[]{:S(2)}) collective-permute-start(f32[1,2,1024]{2,1,0:T(2,128)S(1)} %add_bitcast_fusion), channel_id=1, source_target_pairs={{0,12},{4,8},{8,4},{12,0},{16,28},{20,24},{24,20},{28,16},{1,13},{... | collective-permute-start | bytes 24584 | tf_op jit(solution)/shard_map/ppermute | solution.py:648
  53.0 0.4 collective-permute-start.10
  53.4 0.5 collective-permute-start.9
  54.0 3.6 %factor_next.8.in_ref = f32[1024,1024]{1,0:T(8,128)S(1)} custom-call(f32[1024,1024]{1,0:T(8,128)S(1)} %factor_next.7.in_ref), custom_call_target="tpu_custom_call", output_to_operand_aliasing={{}: (0, {})} | custom-call | flops 8000000000 | bytes 4194304 | tf_op jit(solution)/shard_map/factor_next/pallas_call | solution.py:511
  57.6 0.0 collective-permute-done.11
  57.6 0.0 collective-permute-done.10
  57.6 0.0 collective-permute-done.9
  57.6 2.6 %collective-permute-start.12 = (f32[4,2,1024]{2,1,0:T(2,128)S(1)}, f32[4,2,1024]{2,1,0:T(2,128)S(1)}, u32[]{:S(2)}, u32[]{:S(2)}) collective-permute-start(f32[4,2,1024]{2,1,0:T(2,128)S(1)} %constant_dynamic-update-slice_fusion.refs_0_), channel_id=1, source_target_pairs={{0,16},{4,20},{8,24},{12,28},{16,0},{20,4},{24,8},{28,12},{1,17},{... | collective-permute-start | bytes 98312 | tf_op jit(solution)/shard_map/ppermute | solution.py:648
  60.3 3.3 %factor_next.9.refs_2_ = f32[1024,1024]{1,0:T(8,128)S(1)} custom-call(f32[1024,1024]{1,0:T(8,128)S(1)} %factor_next.8.in_ref), custom_call_target="tpu_custom_call", output_to_operand_aliasing={{}: (0, {})} | custom-call | flops 8000000000 | bytes 4194304 | tf_op jit(solution)/shard_map/factor_next/pallas_call | solution.py:511
  63.5 0.0 collective-permute-done.12.refs_1_
  63.6 4.3 %whiten.1 = (f32[2,1024]{1,0:T(2,128)}, f32[256,1024]{1,0:T(8,128)}, f32[1,1]{1,0:T(1,128)}) custom-call(s32[2]{0:T(128)S(1)} %pad_add_fusion.at_ref, f32[4,2,1024]{2,1,0:T(2,128)S(1)} %constant_dynamic-update-slice_fusion.refs_0_, f32[4,2,1024]{2,1,0:T(2,128)S(1)} %collective-permute-done.12.refs_1_, f32[1024,1024]{1,0:T(8,128)S(1)} %factor_next.9.refs_2_, ...), custom_call_target="tpu_custom_call" | custom-call | tf_op jit(solution)/shard_map/whiten/pallas_call | solution.py:621
  (6 shorter events, 0.1 us)
Async XLA Ops:
  0.6 16.9 %collective-permute-start.1 = (f32[256,1024]{1,0:T(8,128)}, f32[256,1024]{1,0:T(8,128)S(1)}, u32[]{:S(2)}, u32[]{:S(2)}) collective-permute-start(f32[256,1024]{1,0:T(8,128)} %refs_3_.3), channel_id=1, source_target_pairs={{0,1},{1,0},{2,3},{3,2},{4,5},{5,4},{6,7},{7,6},{8,9},{9,8},{10,11... | collective-permute-start | bytes 3145736 | tf_op jit(solution)/shard_map/ppermute | solution.py:648
  1.1 18.3 %copy-start = (f32[256,1024]{1,0:T(8,128)S(1)}, f32[256,1024]{1,0:T(8,128)}, u32[]{:S(2)}) copy-start(f32[256,1024]{1,0:T(8,128)} %refs_3_.3) | copy-start | bytes 3145732
  2.3 15.2 %collective-permute-start = (f32[256,512]{1,0:T(8,128)S(1)}, f32[256,512]{1,0:T(8,128)S(1)}, u32[]{:S(2)}, u32[]{:S(2)}) collective-permute-start(f32[256,512]{1,0:T(8,128)S(1)} %constant_dynamic-slice_fusion), channel_id=1, source_target_pairs={{0,2},{1,3},{2,0},{3,1},{4,6},{5,7},{6,4},{7,5},{8,10},{9,11},{10,... | collective-permute-start | bytes 1572872 | tf_op jit(solution)/shard_map/ppermute | solution.py:648
  17.5 1.9 %collective-permute-start.3 = (f32[256,512]{1,0:T(8,128)S(1)}, f32[256,512]{1,0:T(8,128)S(1)}, u32[]{:S(2)}, u32[]{:S(2)}) collective-permute-start(f32[256,512]{1,0:T(8,128)S(1)} %collective-permute-done.far_ref), channel_id=1, source_target_pairs={{0,1},{1,0},{2,3},{3,2},{4,5},{5,4},{6,7},{7,6},{8,9},{9,8},{10,11... | collective-permute-start | bytes 1572872 | tf_op jit(solution)/shard_map/ppermute | solution.py:648
  17.6 5.4 %copy-start.2 = (f32[8,2,72,128]{3,2,1,0:T(8,128)S(1)}, f32[8,2,72,128]{3,2,1,0:T(8,128)}, u32[]{:S(2)}) copy-start(f32[8,2,72,128]{3,2,1,0:T(8,128)} %get-tuple-element.32) | copy-start | bytes 1769476
  17.6 5.4 %collective-permute-start.2 = (f32[8,2,72,128]{3,2,1,0:T(8,128)}, f32[8,2,72,128]{3,2,1,0:T(8,128)S(1)}, u32[]{:S(2)}, u32[]{:S(2)}) collective-permute-start(f32[8,2,72,128]{3,2,1,0:T(8,128)} %get-tuple-element.32), channel_id=1, source_target_pairs={{0,1},{1,0},{2,3},{3,2},{4,5},{5,4},{6,7},{7,6},{8,9},{9,8},{10,11... | collective-permute-start | bytes 1769480 | tf_op jit(solution)/shard_map/ppermute | solution.py:648
  23.0 11.4 %collective-permute-start.4 = (f32[4,2,72,128]{3,2,1,0:T(8,128)S(1)}, f32[4,2,72,128]{3,2,1,0:T(8,128)S(1)}, u32[]{:S(2)}, u32[]{:S(2)}) collective-permute-start(f32[4,2,72,128]{3,2,1,0:T(8,128)S(1)} %dynamic-slice_add_fusion), channel_id=1, source_target_pairs={{0,2},{1,3},{4,6},{5,7},{8,10},{9,11},{12,14},{13,15},{16,18},{17,... | collective-permute-start | bytes 884744 | tf_op jit(solution)/shard_map/ppermute | solution.py:707
  34.4 3.7 %copy-start.1 = (s32[1,2]{1,0:T(1,128)S(1)}, s32[1,2]{1,0:T(1,128)}, u32[]{:S(2)}) copy-start(s32[1,2]{1,0:T(1,128)} %param.8) | copy-start | bytes 28
  34.4 3.7 %collective-permute-start.5 = (f32[4,2,72,128]{3,2,1,0:T(8,128)S(1)}, f32[4,2,72,128]{3,2,1,0:T(8,128)S(1)}, u32[]{:S(2)}, u32[]{:S(2)}) collective-permute-start(f32[4,2,72,128]{3,2,1,0:T(8,128)S(1)} %collective-permute-done.4.refs_5_), channel_id=1, source_target_pairs={{0,1},{1,0},{2,3},{3,2},{4,5},{5,4},{6,7},{7,6},{8,9},{9,8},{10,11... | collective-permute-start | bytes 884744 | tf_op jit(solution)/shard_map/ppermute | solution.py:648
  44.6 5.7 %collective-permute-start.8 = (f32[2,1024]{1,0:T(2,128)S(1)}, f32[2,1024]{1,0:T(2,128)S(1)}, u32[]{:S(2)}, u32[]{:S(2)}) collective-permute-start(f32[2,1024]{1,0:T(2,128)S(1)} %get-tuple-element.46), channel_id=1, source_target_pairs={{0,3},{1,2},{2,1},{3,0},{4,7},{5,6},{6,5},{7,4},{8,11},{9,10},{10,... | collective-permute-start | bytes 24584 | tf_op jit(solution)/shard_map/ppermute | solution.py:648
  46.4 4.0 %collective-permute-start.7 = (f32[2,1024]{1,0:T(2,128)S(1)}, f32[2,1024]{1,0:T(2,128)S(1)}, u32[]{:S(2)}, u32[]{:S(2)}) collective-permute-start(f32[2,1024]{1,0:T(2,128)S(1)} %get-tuple-element.46), channel_id=1, source_target_pairs={{0,2},{1,3},{2,0},{3,1},{4,6},{5,7},{6,4},{7,5},{8,10},{9,11},{10,... | collective-permute-start | bytes 24584 | tf_op jit(solution)/shard_map/ppermute | solution.py:648
  46.9 3.5 %collective-permute-start.6 = (f32[2,1024]{1,0:T(2,128)S(1)}, f32[2,1024]{1,0:T(2,128)S(1)}, u32[]{:S(2)}, u32[]{:S(2)}) collective-permute-start(f32[2,1024]{1,0:T(2,128)S(1)} %get-tuple-element.46), channel_id=1, source_target_pairs={{0,1},{1,0},{2,3},{3,2},{4,5},{5,4},{6,7},{7,6},{8,9},{9,8},{10,11... | collective-permute-start | bytes 24584 | tf_op jit(solution)/shard_map/ppermute | solution.py:648
  50.4 7.1 %collective-permute-start.11 = (f32[1,2,1024]{2,1,0:T(2,128)S(1)}, f32[1,2,1024]{2,1,0:T(2,128)S(1)}, u32[]{:S(2)}, u32[]{:S(2)}) collective-permute-start(f32[1,2,1024]{2,1,0:T(2,128)S(1)} %add_bitcast_fusion), channel_id=1, source_target_pairs={{0,12},{4,8},{8,4},{12,0},{16,28},{20,24},{24,20},{28,16},{1,13},{... | collective-permute-start | bytes 24584 | tf_op jit(solution)/shard_map/ppermute | solution.py:648
  53.0 4.6 %collective-permute-start.10 = (f32[1,2,1024]{2,1,0:T(2,128)S(1)}, f32[1,2,1024]{2,1,0:T(2,128)S(1)}, u32[]{:S(2)}, u32[]{:S(2)}) collective-permute-start(f32[1,2,1024]{2,1,0:T(2,128)S(1)} %add_bitcast_fusion), channel_id=1, source_target_pairs={{0,8},{4,12},{8,0},{12,4},{16,24},{20,28},{24,16},{28,20},{1,9},{5... | collective-permute-start | bytes 24584 | tf_op jit(solution)/shard_map/ppermute | solution.py:648
  53.4 4.1 %collective-permute-start.9 = (f32[1,2,1024]{2,1,0:T(2,128)S(1)}, f32[1,2,1024]{2,1,0:T(2,128)S(1)}, u32[]{:S(2)}, u32[]{:S(2)}) collective-permute-start(f32[1,2,1024]{2,1,0:T(2,128)S(1)} %add_bitcast_fusion), channel_id=1, source_target_pairs={{0,4},{4,0},{8,12},{12,8},{16,20},{20,16},{24,28},{28,24},{1,5},{5... | collective-permute-start | bytes 24584 | tf_op jit(solution)/shard_map/ppermute | solution.py:648
  57.6 5.9 %collective-permute-start.12 = (f32[4,2,1024]{2,1,0:T(2,128)S(1)}, f32[4,2,1024]{2,1,0:T(2,128)S(1)}, u32[]{:S(2)}, u32[]{:S(2)}) collective-permute-start(f32[4,2,1024]{2,1,0:T(2,128)S(1)} %constant_dynamic-update-slice_fusion.refs_0_), channel_id=1, source_target_pairs={{0,16},{4,20},{8,24},{12,28},{16,0},{20,4},{24,8},{28,12},{1,17},{... | collective-permute-start | bytes 98312 | tf_op jit(solution)/shard_map/ppermute | solution.py:648
